TPU v7x, 32 devices: a whole 2x2x4 slice. The times are simulated.
32 devices in a mesh: groups: 2 (over x), blk: 16 (over z, y, core).
Axes of the slice: x: 2, y: 2, z: 4, core: 2. Of those that a mesh axis runs over, the one named last changes fastest.
Arguments:
- traces: bfloat16 [8192, 12000], P(('groups', 'blk')), parts along dimension 0
- record_id: int32 [8192], P(('groups', 'blk')), parts along dimension 0, may hold values from 0 to 4095, as said below
Outputs:
- correlations: bfloat16 [1024, 4, 32, 801], P(('groups', 'blk')), parts along dimension 0
There are 2 independent parts, one for each index of `groups`. A program takes and returns all parts, laid end to end along the dimension named above; each array names one. Nothing has to cross between parts.
Inputs may be any that keep to these rules, and one draw needn't show every extreme that they name: `record_id`: every value appears exactly once among one part's records; value v is channel v // 8 in window v mod 8. The records of one index of blk hold at most 32 of one owner's records (owner = v // 256), some index holds exactly 32 records for some owner in every draw, and every owner's 256 records come from the devices together.
All inputs are finite; a program needn't handle non-finite values.
Results may differ from a plain program's by a relative error of at most 0.0075.
Values may be sent and summed in bfloat16 or wider, within the bound.
No kernel may reach another device: no remote copies, remote signals or barrier semaphores. Data moves between devices by JAX's collectives and lax.ppermute only.
A program may use at most 192 MiB of HBM per device.

v0:
```python
import functools
import math

import jax
import jax.numpy as jnp
import numpy as np
from jax import lax
from jax.experimental import pallas as pl
from jax.experimental.pallas import tpu as pltpu
from jax.sharding import PartitionSpec as P

NWIN = 8
WS = 12000
F = 512
LOWBIN = 60
LAG = 400
HOPS = 3
NLAG = 2 * LAG + 1
HALF = WS // 2
CHUNK = 240
STEPS = HALF // CHUNK
KPAD = 256
BINS = LOWBIN + np.concatenate([np.arange(0, F, 2), np.arange(1, F, 2)])
VMEM_LIMIT = 56 * 1024 * 1024


def shifted(block, axis, distance):
    devices = range(lax.axis_size(axis))
    route = [((i - distance) % len(devices), i) for i in devices]
    return lax.ppermute(block, axis, route)


def inverse_table():
    bin_index = jnp.asarray(BINS, jnp.int32)[:, None]
    lag_index = jnp.arange(NLAG, dtype=jnp.int32)[None, :] - LAG + WS
    residue = (bin_index * lag_index % WS).astype(jnp.float32)
    angles = 2.0 * math.pi / WS * residue
    table = jnp.concatenate([jnp.cos(angles), -jnp.sin(angles)], axis=0)
    return table.astype(jnp.bfloat16)


def forward_start():
    angles = 2.0 * np.pi / WS * (BINS[:, None] * np.arange(CHUNK)[None, :] % WS)
    start = np.zeros((2, F, KPAD), np.float32)
    start[0, :, :CHUNK] = np.cos(angles)
    start[1, :, :CHUNK] = -np.sin(angles)
    step = 2.0 * np.pi / WS * (BINS * CHUNK % WS)
    turn = np.stack([np.cos(step), -np.sin(step)]).astype(np.float32)
    return start, np.ascontiguousarray(np.broadcast_to(turn[:, :, None], (2, F, 128)))


def label_kernel(capacity, rec_count, id_ref, target_ref, label_ref):
    ids = id_ref[...]
    slots = label_ref.shape[1]
    owner = ids // rec_count
    row = jnp.broadcast_to(owner, (rec_count, rec_count))
    col = row.T
    before = lax.broadcasted_iota(jnp.int32, row.shape, 0) < lax.broadcasted_iota(
        jnp.int32, row.shape, 1
    )
    same = jnp.where((row == col) & before, 1, 0)
    rank = jnp.sum(same, axis=0, keepdims=True)
    target = owner * capacity + rank
    target_ref[...] = target
    packed = jnp.broadcast_to(target, (128, rec_count)).T
    id_col = jnp.broadcast_to(ids, (128, rec_count)).T
    for part in range(slots // 128):
        lane = lax.broadcasted_iota(jnp.int32, packed.shape, 1) + part * 128
        hit = jnp.where(packed == lane, id_col + 1, 0)
        label_ref[:, part * 128 : (part + 1) * 128] = jnp.sum(hit, axis=0, keepdims=True) - 1


def make_labels(record_id, peer_count, capacity):
    rec_count = record_id.shape[0]
    slots = peer_count * capacity
    return pl.pallas_call(
        functools.partial(label_kernel, capacity, rec_count),
        out_shape=(
            jax.ShapeDtypeStruct((1, rec_count), jnp.int32),
            jax.ShapeDtypeStruct((1, slots), jnp.int32),
        ),
        name="labels",
    )(record_id.reshape(1, rec_count))


def spectrum_kernel(target_ref, x0_ref, x1_ref, start_ref, turn_ref, out_ref, state, table, sums, acc):
    step = pl.program_id(0)

    @pl.when(step == 0)
    def _():
        state[...] = start_ref[...]
        sums[...] = jnp.zeros_like(sums)
        acc[...] = jnp.zeros_like(acc)

    half = F // 2
    block = 64
    for row in range(0, F, block):
        rows = slice(row, row + block)
        real = state[0, rows, :]
        imag = state[1, rows, :]
        base = row if row < half else row + half
        table[base : base + block, :] = real.astype(jnp.bfloat16)
        table[base + half : base + half + block, :] = imag.astype(jnp.bfloat16)
        turn_real = jnp.concatenate([turn_ref[0, rows, :]] * 2, axis=1)
        turn_imag = jnp.concatenate([turn_ref[1, rows, :]] * 2, axis=1)
        state[0, rows, :] = real * turn_real - imag * turn_imag
        state[1, rows, :] = real * turn_imag + imag * turn_real
    sums[0, :CHUNK, :] = x0_ref[...] + x1_ref[...]
    sums[1, :CHUNK, :] = x0_ref[...] - x1_ref[...]
    acc[:F, :] += jnp.dot(table[:F, :], sums[0], preferred_element_type=jnp.float32)
    acc[F:, :] += jnp.dot(table[F:, :], sums[1], preferred_element_type=jnp.float32)

    @pl.when(step == STEPS - 1)
    def _():
        power = jnp.sum(acc[...] * acc[...], axis=0, keepdims=True) / F
        scale = lax.rsqrt(power + 1e-06)
        slot = lax.broadcasted_iota(jnp.int32, (out_ref.shape[0], target_ref.shape[1]), 0)
        pick = jnp.where(slot == target_ref[...], 1.0, 0.0).astype(jnp.bfloat16)
        for place, row in enumerate((0, F, half, F + half)):
            white = (acc[row : row + half, :] * scale).astype(jnp.bfloat16)
            out_ref[:, place * half : (place + 1) * half] = lax.dot_general(
                pick, white, (((1,), (1,)), ((), ())), preferred_element_type=jnp.float32
            ).astype(jnp.bfloat16)


def spectra(traces, target, slots):
    rec_count = traces.shape[0]
    start, turn = forward_start()
    lanes = traces.T
    return pl.pallas_call(
        spectrum_kernel,
        grid=(STEPS,),
        in_specs=[
            pl.BlockSpec((1, rec_count), lambda i: (0, 0)),
            pl.BlockSpec((CHUNK, rec_count), lambda i: (i, 0)),
            pl.BlockSpec((CHUNK, rec_count), lambda i: (i + STEPS, 0)),
            pl.BlockSpec((2, F, KPAD), lambda i: (0, 0, 0)),
            pl.BlockSpec((2, F, 128), lambda i: (0, 0, 0)),
        ],
        out_specs=pl.BlockSpec((slots, 2 * F), lambda i: (0, 0)),
        out_shape=jax.ShapeDtypeStruct((slots, 2 * F), jnp.bfloat16),
        scratch_shapes=[
            pltpu.VMEM((2, F, KPAD), jnp.float32),
            pltpu.VMEM((2 * F, KPAD), jnp.bfloat16),
            pltpu.VMEM((2, KPAD, rec_count), jnp.bfloat16),
            pltpu.VMEM((2 * F, rec_count), jnp.float32),
        ],
        compiler_params=pltpu.CompilerParams(vmem_limit_bytes=VMEM_LIMIT),
        cost_estimate=pl.CostEstimate(
            flops=2 * rec_count * WS * F, bytes_accessed=2 * rec_count * WS, transcendentals=0
        ),
        name="spectra",
    )(target, lanes, lanes, jnp.asarray(start), jnp.asarray(turn))


def place_kernel(rec_count, label_ref, arrived_ref, out_ref):
    label = label_ref[...]
    local = label % rec_count
    row = jnp.where(label >= 0, local % NWIN * (rec_count // NWIN) + local // NWIN, -1)
    want = lax.broadcasted_iota(jnp.int32, (rec_count, label.shape[1]), 0)
    pick = jnp.where(want == row, 1.0, 0.0).astype(jnp.bfloat16)
    out_ref[...] = jnp.dot(pick, arrived_ref[...], preferred_element_type=jnp.float32).astype(
        jnp.bfloat16
    )


def place(labels, arrived, rec_count):
    return pl.pallas_call(
        functools.partial(place_kernel, rec_count),
        out_shape=jax.ShapeDtypeStruct((rec_count, 2 * F), jnp.bfloat16),
        compiler_params=pltpu.CompilerParams(vmem_limit_bytes=VMEM_LIMIT),
        name="place",
    )(labels, arrived)


def correlate_kernel(hop_index, group, *refs):
    own_ref, other_ref, inverse_ref = refs[:3]
    out_ref, mine, theirs, cross = refs[-4:]
    width = own_ref.shape[0] // NWIN
    step = pl.program_id(0)

    @pl.when(step == 0)
    def _():
        for w in range(NWIN):
            rows = slice(w * width, (w + 1) * width)
            real = own_ref[rows, :F].astype(jnp.float32)
            imag = own_ref[rows, F:].astype(jnp.float32)
            mine[0, rows, :] = real + imag
            mine[1, rows, :] = real
            mine[2, rows, :] = imag
            real = other_ref[rows, :F].astype(jnp.float32)
            imag = other_ref[rows, F:].astype(jnp.float32)
            theirs[0, rows, :] = real
            theirs[1, rows, :] = real + imag
            theirs[2, rows, :] = real - imag

    blocks = [
        pl.ds(pl.multiple_of(w * width + step * group, group), group) for w in range(NWIN)
    ]
    for tile in range(F // 128):
        lanes = slice(tile * 128, (tile + 1) * 128)
        for first in range(0, group, 2):
            total = [[None] * 3 for _ in range(2)]
            for w in range(NWIN):
                for j in range(3):
                    factor = theirs[j, w * width : (w + 1) * width, lanes]
                    rows = mine.at[j, blocks[w], lanes]
                    for c in range(2):
                        term = factor * rows[first + c : first + c + 1, :]
                        total[c][j] = term if w == 0 else total[c][j] + term
            for c in range(2):
                rows = slice((first + c) * width, (first + c + 1) * width)
                cross[rows, tile * 128 : (tile + 1) * 128] = (total[c][0] - total[c][2]).astype(
                    jnp.bfloat16
                )
                cross[rows, F + tile * 128 : F + (tile + 1) * 128] = (
                    total[c][0] - total[c][1]
                ).astype(jnp.bfloat16)
    lagged = jnp.dot(cross[...], inverse_ref[...], preferred_element_type=jnp.float32)
    lagged = (lagged * (1.0 / math.sqrt(F * NWIN))).reshape(group, width, NLAG)
    if hop_index == 0:
        shape = (group, width, NLAG)
        channel = lax.broadcasted_iota(jnp.int32, shape, 0) + step * group
        lagged = jnp.where(channel == lax.broadcasted_iota(jnp.int32, shape, 1), 0.0, lagged)
    out_ref[...] = lagged.astype(jnp.bfloat16)[:, None]


def correlate(own, other, inverse, hop_index, result):
    rec_count = own.shape[0]
    width = rec_count // NWIN
    group = 8
    whole = lambda shape: pl.BlockSpec(shape, lambda i: (0,) * len(shape))
    in_specs = [whole(own.shape), whole(other.shape), whole(inverse.shape)]
    operands = [own, other, inverse]
    aliases = {}
    if result is not None:
        in_specs.append(pl.BlockSpec(memory_space=pl.ANY))
        operands.append(result)
        aliases = {3: 0}
    pairs = width * width
    return pl.pallas_call(
        functools.partial(correlate_kernel, hop_index, group),
        grid=(width // group,),
        in_specs=in_specs,
        out_specs=pl.BlockSpec((group, 1, width, NLAG), lambda i: (i, hop_index, 0, 0)),
        out_shape=jax.ShapeDtypeStruct((width, HOPS + 1, width, NLAG), jnp.bfloat16),
        scratch_shapes=[
            pltpu.VMEM((3, rec_count, F), jnp.float32),
            pltpu.VMEM((3, rec_count, F), jnp.float32),
            pltpu.VMEM((group * width, 2 * F), jnp.bfloat16),
        ],
        input_output_aliases=aliases,
        compiler_params=pltpu.CompilerParams(vmem_limit_bytes=VMEM_LIMIT),
        cost_estimate=pl.CostEstimate(
            flops=pairs * 2 * F * NLAG * 4, bytes_accessed=pairs * NLAG * 2, transcendentals=0
        ),
        name="correlate",
    )(*operands)


def on_device(traces, record_id):
    rec_count = traces.shape[0]
    peer_count = lax.axis_size("blk")
    capacity = 2 * rec_count // peer_count
    slots = peer_count * capacity
    target, labels = make_labels(record_id, peer_count, capacity)
    labels = lax.all_to_all(
        labels.reshape(peer_count, 1, capacity), "blk", split_axis=0, concat_axis=0, tiled=True
    ).reshape(1, slots)
    outgoing = spectra(traces, target, slots).reshape(peer_count, capacity, 2 * F)
    arrived = lax.all_to_all(outgoing, "blk", split_axis=0, concat_axis=0, tiled=True)
    own = place(labels, arrived.reshape(slots, 2 * F), rec_count)
    inverse = inverse_table()
    result = None
    visiting = own
    for hop_index in range(HOPS + 1):
        if hop_index > 0:
            visiting = shifted(visiting, "blk", -1)
        result = correlate(own, visiting, inverse, hop_index, result)
    return result


def solution(mesh):
    return jax.shard_map(
        on_device,
        mesh=mesh,
        in_specs=(P(("groups", "blk"), None), P(("groups", "blk"))),
        out_specs=P(("groups", "blk"), None, None, None),
        check_vma=False,
    )
```

profile of v0, /device:TPU:0, one launch (start us, length us, event | category | flops | bytes accessed | tf_op | source)
XLA Modules:
  0.0 132.8 jit_solution(39011168326659153)
XLA Ops:
  0.0 1.5 %labels.1 = (s32[1,256]{1,0:T(1,128)}, s32[1,512]{1,0:T(1,128)}) custom-call(s32[1,256]{1,0:T(1,128)} %bitcast.9), custom_call_target="tpu_custom_call" | custom-call | tf_op jit(solution)/shard_map/labels/pallas_call | solution.py:76
  1.5 0.5 broadcast.18
  2.1 1.3 %reduce.6 = s32[512]{0:T(512)S(1)} reduce(s32[1,512]{1,0:T(1,128)} %get-tuple-element.7, s32[]{:T(128)} %broadcast.18), dimensions={0}, to_apply=%get-tuple-element.7.reduce_sub_computation.3 | reduce | bytes 4100 | tf_op jit(solution)/shard_map/labels/pallas_call | solution.py:76
  3.4 0.7 reshape.23
  4.1 7.4 %all-to-all-start = ((s32[16,1,32]{2,1,0:T(1,128)}), s32[16,1,32]{2,1,0:T(1,128)S(1)}, u32[]{:S(2)}, u32[]{:S(2)}) async-start(s32[16,1,32]{2,1,0:T(1,128)} %bitcast.1), calls=%async_computation | async-start | bytes 16384 | tf_op jit(solution)/shard_map/all_to_all | solution.py:267
  11.5 20.1 %spectra.1 = bf16[512,1024]{1,0:T(8,128)(2,1)} custom-call(s32[1,256]{1,0:T(1,128)} %get-tuple-element.8.target_ref, bf16[12000,256]{1,0:T(8,128)(2,1)} %bitcast.5, bf16[12000,256]{1,0:T(8,128)(2,1)} %bitcast.6, f32[2,512,256]{2,1,0:T(8,128)} %constant.25.clone.start_ref, f32[2,512,128]{2,1,0:T(8,128)} %constant.26.clone.turn_ref), custom_call_target="tpu_custom_call" | custom-call | flops 3145728000 | bytes 6144000 | tf_op jit(solution)/shard_map/spectra/pallas_call | solution.py:130
  31.5 0.0 all-to-all-done
  31.6 6.0 %all-to-all-start.1 = ((bf16[16,32,1024]{2,1,0:T(8,128)(2,1)}), bf16[16,32,1024]{2,1,0:T(8,128)(2,1)S(1)}, u32[]{:S(2)}, u32[]{:S(2)}) async-start(bf16[16,32,1024]{2,1,0:T(8,128)(2,1)} %bitcast.7), calls=%async_computation.1 | async-start | bytes 2097152 | tf_op jit(solution)/shard_map/all_to_all | solution.py:271
  37.6 0.7 reduce.7
  38.2 0.7 reshape.24.label_ref
  38.9 21.6 %all-to-all-done.1 = bf16[16,32,1024]{2,1,0:T(8,128)(2,1)S(1)} async-done(((bf16[16,32,1024]{2,1,0:T(8,128)(2,1)}), bf16[16,32,1024]{2,1,0:T(8,128)(2,1)S(1)}, u32[]{:S(2)}, u32[]{:S(2)}) %all-to-all-start.1) | async-done | bytes 1048608 | tf_op jit(solution)/shard_map/all_to_all | solution.py:271
  60.5 1.0 copy-done
  61.5 2.5 %place.1.refs_0_.refs_1_ = bf16[256,1024]{1,0:T(8,128)(2,1)} custom-call(s32[1,512]{1,0:T(1,128)} %reshape.24.label_ref, bf16[512,1024]{1,0:T(8,128)(2,1)} %bitcast.8), custom_call_target="tpu_custom_call" | custom-call | tf_op jit(solution)/shard_map/place/pallas_call | solution.py:168
  64.0 5.4 %collective-permute-start = (bf16[256,1024]{1,0:T(8,128)(2,1)}, bf16[256,1024]{1,0:T(8,128)(2,1)S(1)}, u32[]{:S(2)}, u32[]{:S(2)}) collective-permute-start(bf16[256,1024]{1,0:T(8,128)(2,1)} %place.1.refs_0_.refs_1_), channel_id=1, source_target_pairs={{1,0},{2,1},{3,2},{4,3},{5,4},{6,5},{7,6},{8,7},{9,8},{10,9},{11,1... | collective-permute-start | bytes 1572872 | tf_op jit(solution)/shard_map/ppermute | solution.py:30
  69.3 7.0 %collective-permute-done.refs_1_ = bf16[256,1024]{1,0:T(8,128)(2,1)S(1)} collective-permute-done((bf16[256,1024]{1,0:T(8,128)(2,1)}, bf16[256,1024]{1,0:T(8,128)(2,1)S(1)}, u32[]{:S(2)}, u32[]{:S(2)}) %collective-permute-start) | collective-permute-done | bytes 524320 | tf_op jit(solution)/shard_map/ppermute | solution.py:30
  76.4 4.5 %collective-permute-start.1 = (bf16[256,1024]{1,0:T(8,128)(2,1)S(1)}, bf16[256,1024]{1,0:T(8,128)(2,1)S(1)}, u32[]{:S(2)}, u32[]{:S(2)}) collective-permute-start(bf16[256,1024]{1,0:T(8,128)(2,1)S(1)} %collective-permute-done.refs_1_), channel_id=1, source_target_pairs={{1,0},{2,1},{3,2},{4,3},{5,4},{6,5},{7,6},{8,7},{9,8},{10,9},{11,1... | collective-permute-start | bytes 1572872 | tf_op jit(solution)/shard_map/ppermute | solution.py:30
  80.9 8.3 %cosine_convert_fusion = (bf16[512,801]{1,0:T(8,128)(2,1)S(1)}, bf16[512,801]{1,0:T(8,128)(2,1)S(1)}) fusion(s32[801]{0:T(1024)S(1)} %iota_add_fusion, s32[512]{0:T(512)S(1)} %copy-done.4), kind=kLoop, calls=%fused_computation.5 | loop fusion | flops 4921344 | bytes 1645700 | tf_op jit(solution)/shard_map/convert
  89.2 1.4 %pad_maximum_fusion.refs_2_ = bf16[1024,801]{1,0:T(8,128)(2,1)} fusion(bf16[512,801]{1,0:T(8,128)(2,1)S(1)} %get-tuple-element.10, bf16[512,801]{1,0:T(8,128)(2,1)S(1)} %get-tuple-element.9), kind=kLoop, calls=%fused_computation.3 | loop fusion | flops 3280896 | bytes 3280896 | tf_op jit(solution)/shard_map/concatenate | solution.py:38
  90.6 10.3 %correlate.4.refs_3_ = bf16[32,4,32,801]{3,2,1,0:T(8,128)(2,1)} custom-call(bf16[256,1024]{1,0:T(8,128)(2,1)} %place.1.refs_0_.refs_1_, bf16[256,1024]{1,0:T(8,128)(2,1)} %place.1.refs_0_.refs_1_, bf16[1024,801]{1,0:T(8,128)(2,1)} %pad_maximum_fusion.refs_2_), custom_call_target="tpu_custom_call" | custom-call | flops 3359637504 | bytes 1640448 | tf_op jit(solution)/shard_map/correlate/pallas_call | solution.py:241
  100.9 0.0 collective-permute-start.2
  100.9 10.5 %correlate.5.refs_3_ = bf16[32,4,32,801]{3,2,1,0:T(8,128)(2,1)} custom-call(bf16[256,1024]{1,0:T(8,128)(2,1)} %place.1.refs_0_.refs_1_, bf16[256,1024]{1,0:T(8,128)(2,1)} %copy-done.1, bf16[1024,801]{1,0:T(8,128)(2,1)} %pad_maximum_fusion.refs_2_, bf16[32,4,32,801]{3,2,1,0:T(8,128)(2,1)} %correlate.4.refs_3_), custom_call_target="tpu_custom_call", output_to_operand_aliasing={{}: (3, {})} | custom-call | flops 3359637504 | bytes 1640448 | tf_op jit(solution)/shard_map/correlate/pallas_call | solution.py:241
  111.4 10.3 %correlate.6.refs_3_ = bf16[32,4,32,801]{3,2,1,0:T(8,128)(2,1)} custom-call(bf16[256,1024]{1,0:T(8,128)(2,1)} %place.1.refs_0_.refs_1_, bf16[256,1024]{1,0:T(8,128)(2,1)} %copy-done.2, bf16[1024,801]{1,0:T(8,128)(2,1)} %pad_maximum_fusion.refs_2_, bf16[32,4,32,801]{3,2,1,0:T(8,128)(2,1)} %correlate.5.refs_3_), custom_call_target="tpu_custom_call", output_to_operand_aliasing={{}: (3, {})} | custom-call | flops 3359637504 | bytes 1640448 | tf_op jit(solution)/shard_map/correlate/pallas_call | solution.py:241
  121.7 0.8 copy-done.3
  122.5 10.3 %correlate.7 = bf16[32,4,32,801]{3,2,1,0:T(8,128)(2,1)} custom-call(bf16[256,1024]{1,0:T(8,128)(2,1)} %place.1.refs_0_.refs_1_, bf16[256,1024]{1,0:T(8,128)(2,1)} %copy-done.3, bf16[1024,801]{1,0:T(8,128)(2,1)} %pad_maximum_fusion.refs_2_, bf16[32,4,32,801]{3,2,1,0:T(8,128)(2,1)} %correlate.6.refs_3_), custom_call_target="tpu_custom_call", output_to_operand_aliasing={{}: (3, {})} | custom-call | flops 3359637504 | bytes 1640448 | tf_op jit(solution)/shard_map/correlate/pallas_call | solution.py:241
  (11 shorter events, 0.0 us)
Async XLA Ops:
  4.1 27.5 %all-to-all-start = ((s32[16,1,32]{2,1,0:T(1,128)}), s32[16,1,32]{2,1,0:T(1,128)S(1)}, u32[]{:S(2)}, u32[]{:S(2)}) async-start(s32[16,1,32]{2,1,0:T(1,128)} %bitcast.1), calls=%async_computation | async-start | bytes 16384 | tf_op jit(solution)/shard_map/all_to_all | solution.py:267
  31.5 49.3 %copy-start.4 = (s32[512]{0:T(512)S(1)}, s32[512]{0:T(512)}, u32[]{:S(2)}) copy-start(s32[512]{0:T(512)} %constant.27.clone) | copy-start | bytes 6148
  31.6 29.0 %all-to-all-start.1 = ((bf16[16,32,1024]{2,1,0:T(8,128)(2,1)}), bf16[16,32,1024]{2,1,0:T(8,128)(2,1)S(1)}, u32[]{:S(2)}, u32[]{:S(2)}) async-start(bf16[16,32,1024]{2,1,0:T(8,128)(2,1)} %bitcast.7), calls=%async_computation.1 | async-start | bytes 2097152 | tf_op jit(solution)/shard_map/all_to_all | solution.py:271
  60.5 1.0 copy-start
  64.0 12.4 %collective-permute-start = (bf16[256,1024]{1,0:T(8,128)(2,1)}, bf16[256,1024]{1,0:T(8,128)(2,1)S(1)}, u32[]{:S(2)}, u32[]{:S(2)}) collective-permute-start(bf16[256,1024]{1,0:T(8,128)(2,1)} %place.1.refs_0_.refs_1_), channel_id=1, source_target_pairs={{1,0},{2,1},{3,2},{4,3},{5,4},{6,5},{7,6},{8,7},{9,8},{10,9},{11,1... | collective-permute-start | bytes 1572872 | tf_op jit(solution)/shard_map/ppermute | solution.py:30
  76.4 14.2 %copy-start.1 = (bf16[256,1024]{1,0:T(8,128)(2,1)}, bf16[256,1024]{1,0:T(8,128)(2,1)S(1)}, u32[]{:S(2)}) copy-start(bf16[256,1024]{1,0:T(8,128)(2,1)S(1)} %collective-permute-done.refs_1_) | copy-start | bytes 1572868
  76.4 24.5 %collective-permute-start.1 = (bf16[256,1024]{1,0:T(8,128)(2,1)S(1)}, bf16[256,1024]{1,0:T(8,128)(2,1)S(1)}, u32[]{:S(2)}, u32[]{:S(2)}) collective-permute-start(bf16[256,1024]{1,0:T(8,128)(2,1)S(1)} %collective-permute-done.refs_1_), channel_id=1, source_target_pairs={{1,0},{2,1},{3,2},{4,3},{5,4},{6,5},{7,6},{8,7},{9,8},{10,9},{11,1... | collective-permute-start | bytes 1572872 | tf_op jit(solution)/shard_map/ppermute | solution.py:30
  100.9 10.5 %copy-start.2 = (bf16[256,1024]{1,0:T(8,128)(2,1)}, bf16[256,1024]{1,0:T(8,128)(2,1)S(1)}, u32[]{:S(2)}) copy-start(bf16[256,1024]{1,0:T(8,128)(2,1)S(1)} %collective-permute-done.1.refs_1_) | copy-start | bytes 1572868
  100.9 20.8 %collective-permute-start.2 = (bf16[256,1024]{1,0:T(8,128)(2,1)S(1)}, bf16[256,1024]{1,0:T(8,128)(2,1)S(1)}, u32[]{:S(2)}, u32[]{:S(2)}) collective-permute-start(bf16[256,1024]{1,0:T(8,128)(2,1)S(1)} %collective-permute-done.1.refs_1_), channel_id=1, source_target_pairs={{1,0},{2,1},{3,2},{4,3},{5,4},{6,5},{7,6},{8,7},{9,8},{10,9},{11,1... | collective-permute-start | bytes 1572872 | tf_op jit(solution)/shard_map/ppermute | solution.py:30
  121.7 0.8 copy-start.3
where the time goes:
time: 134 us; the launch traced here: 133 us
  Pallas kernels  65.5 us (49%)
  waiting for transfers between devices  28.6 us (21%)
  starting transfers between devices  23.3 us (17%)
  other arithmetic  11.7 us (9%)
  local copies, waits for them, and re-layouts  3.66 us (3%)
    pallas_call x4, Pallas kernels, correlate(): pl.pallas_call(functools.partial(correlate_kernel, hop_index, group), gri...  41.4 us
    all_to_all x1, waiting for transfers between devices, on_device(): lax.all_to_all(outgoing, 'blk', split_axis=0, concat_axis=0, tiled=True)  21.6 us
    pallas_call x1, Pallas kernels, spectra(): pl.pallas_call(spectrum_kernel, grid=(STEPS,), in_specs=[pl.BlockSpec((1,...  20.1 us
    ppermute x3, starting transfers between devices, shifted(): return lax.ppermute(block, axis, route)  9.9 us
    another operation x1, other arithmetic  8.29 us
    all_to_all x1, starting transfers between devices, on_device(): lax.all_to_all(labels.reshape(peer_count, 1, capacity), 'blk', split_axis...  7.39 us
    ppermute x3, waiting for transfers between devices, shifted(): return lax.ppermute(block, axis, route)  7.02 us
    all_to_all x1, starting transfers between devices, on_device(): lax.all_to_all(outgoing, 'blk', split_axis=0, concat_axis=0, tiled=True)  6.01 us
  transfers between devices with their start and end apart: 5, of which 2 were waited for; matrix products, arithmetic and copies ran while one was open for 8% of the time, Pallas kernels for 39%

commit v1 on v0

v1 whole, which is shorter than its diff:
```python
import functools
import math

import jax
import jax.numpy as jnp
import numpy as np
from jax import lax
from jax.experimental import pallas as pl
from jax.experimental.pallas import tpu as pltpu
from jax.sharding import PartitionSpec as P

NWIN = 8
WS = 12000
F = 512
LOWBIN = 60
LAG = 400
HOPS = 3
NLAG = 2 * LAG + 1
HALF = WS // 2
CHUNK = 1200
STEPS = HALF // CHUNK
BINS = LOWBIN + np.concatenate([np.arange(0, F, 2), np.arange(1, F, 2)])
VMEM_LIMIT = 56 * 1024 * 1024


def moved(block, source_of):
    count = lax.axis_size("blk")
    return lax.ppermute(block, "blk", [(source_of(i) % count, i) for i in range(count)])


def inverse_table():
    bin_index = jnp.asarray(BINS, jnp.int32)[:, None]
    lag_index = jnp.arange(NLAG, dtype=jnp.int32)[None, :] - LAG + WS
    residue = (bin_index * lag_index % WS).astype(jnp.float32)
    angles = 2.0 * math.pi / WS * residue
    table = jnp.concatenate([jnp.cos(angles), -jnp.sin(angles)], axis=0)
    return table.astype(jnp.bfloat16)


def forward_table():
    angles = 2.0 * np.pi / WS * (BINS[:, None] * np.arange(HALF)[None, :] % WS)
    even, odd = angles[: F // 2], angles[F // 2 :]
    table = np.concatenate([np.cos(even), -np.sin(even), np.cos(odd), -np.sin(odd)])
    table = table.reshape(2 * F, STEPS, CHUNK).transpose(1, 0, 2)
    return np.ascontiguousarray(table).astype(np.float32).astype(jnp.bfloat16)


def spectrum_kernel(capacity, id_ref, x0_ref, x1_ref, table_ref, out_ref, first, second):
    step = pl.program_id(0)

    @pl.when(step == 0)
    def _():
        first[...] = jnp.dot(table_ref[...], x0_ref[...], preferred_element_type=jnp.float32)
        second[...] = jnp.dot(table_ref[...], x1_ref[...], preferred_element_type=jnp.float32)

    @pl.when(step > 0)
    def _():
        first[...] += jnp.dot(table_ref[...], x0_ref[...], preferred_element_type=jnp.float32)
        second[...] += jnp.dot(table_ref[...], x1_ref[...], preferred_element_type=jnp.float32)

    @pl.when(step == STEPS - 1)
    def _():
        rec_count = id_ref.shape[1]
        owner = id_ref[...] // rec_count
        row = jnp.broadcast_to(owner, (rec_count, rec_count))
        before = lax.broadcasted_iota(jnp.int32, row.shape, 0) < lax.broadcasted_iota(
            jnp.int32, row.shape, 1
        )
        rank = jnp.sum(jnp.where((row == row.T) & before, 1, 0), axis=0, keepdims=True)
        target = owner * capacity + rank
        slot = lax.broadcasted_iota(jnp.int32, (out_ref.shape[0], rec_count), 0)
        pick = jnp.where(slot == target, 1.0, 0.0).astype(jnp.bfloat16)
        first[:F, :] += second[:F, :]
        first[F:, :] -= second[F:, :]
        power = jnp.sum(first[...] * first[...], axis=0, keepdims=True) / F
        scale = lax.rsqrt(power + 1e-06)
        half = F // 2
        for place, base in enumerate((0, F, half, F + half)):
            white = (first[base : base + half, :] * scale).astype(jnp.bfloat16)
            out_ref[:, place * half : (place + 1) * half] = lax.dot_general(
                pick, white, (((1,), (1,)), ((), ())), preferred_element_type=jnp.float32
            ).astype(jnp.bfloat16)


def spectra(traces, record_id, capacity, slots):
    rec_count = traces.shape[0]
    lanes = traces.T
    return pl.pallas_call(
        functools.partial(spectrum_kernel, capacity),
        grid=(STEPS,),
        in_specs=[
            pl.BlockSpec((1, rec_count), lambda i: (0, 0)),
            pl.BlockSpec((CHUNK, rec_count), lambda i: (i, 0)),
            pl.BlockSpec((CHUNK, rec_count), lambda i: (i + STEPS, 0)),
            pl.BlockSpec((None, 2 * F, CHUNK), lambda i: (i, 0, 0)),
        ],
        out_specs=pl.BlockSpec((slots, 2 * F), lambda i: (0, 0)),
        out_shape=jax.ShapeDtypeStruct((slots, 2 * F), jnp.bfloat16),
        scratch_shapes=[
            pltpu.VMEM((2 * F, rec_count), jnp.float32),
            pltpu.VMEM((2 * F, rec_count), jnp.float32),
        ],
        compiler_params=pltpu.CompilerParams(vmem_limit_bytes=VMEM_LIMIT),
        cost_estimate=pl.CostEstimate(
            flops=4 * rec_count * WS * F, bytes_accessed=2 * WS * (rec_count + F), transcendentals=0
        ),
        name="spectra",
    )(record_id.reshape(1, rec_count), lanes, lanes, jnp.asarray(forward_table()))


def rows_kernel(capacity, me_ref, id_ref, row_ref):
    ids = id_ref[...]
    peers, rec_count = ids.shape
    hit = ids // rec_count == me_ref[0]
    before = lax.broadcasted_iota(jnp.int32, (rec_count, rec_count), 0) < lax.broadcasted_iota(
        jnp.int32, (rec_count, rec_count), 1
    )
    rank = jnp.dot(
        jnp.where(hit, 1.0, 0.0).astype(jnp.bfloat16),
        jnp.where(before, 1.0, 0.0).astype(jnp.bfloat16),
        preferred_element_type=jnp.float32,
    ).astype(jnp.int32)
    local = (ids % rec_count + 1).astype(jnp.float32)
    slots = row_ref.shape[1]
    slot = lax.broadcasted_iota(jnp.int32, (1, slots), 1)
    peer = lax.broadcasted_iota(jnp.int32, (peers, slots), 0)
    label = jnp.zeros((peers, slots), jnp.float32)
    for j in range(capacity):
        value = jnp.sum(jnp.where(hit & (rank == j), local, 0.0), axis=1, keepdims=True)
        label = jnp.where(slot == peer * capacity + j, value, label)
    label = jnp.sum(label, axis=0, keepdims=True).astype(jnp.int32) - 1
    row = label % NWIN * (rec_count // NWIN) + label // NWIN
    row_ref[...] = jnp.where(label >= 0, row, -1)


def arrival_rows(all_ids, capacity):
    peers = all_ids.shape[0]
    me = lax.axis_index("blk").astype(jnp.int32).reshape(1)
    return pl.pallas_call(
        functools.partial(rows_kernel, capacity),
        in_specs=[pl.BlockSpec(memory_space=pltpu.SMEM), pl.BlockSpec(memory_space=pltpu.VMEM)],
        out_shape=jax.ShapeDtypeStruct((1, peers * capacity), jnp.int32),
        name="rows",
    )(me, all_ids)


def place_kernel(row_ref, arrived_ref, out_ref):
    want = lax.broadcasted_iota(jnp.int32, (out_ref.shape[0], row_ref.shape[1]), 0)
    pick = jnp.where(want == row_ref[...], 1.0, 0.0).astype(jnp.bfloat16)
    out_ref[...] = jnp.dot(pick, arrived_ref[...], preferred_element_type=jnp.float32).astype(
        jnp.bfloat16
    )


def place(rows, arrived, rec_count):
    return pl.pallas_call(
        place_kernel,
        out_shape=jax.ShapeDtypeStruct((rec_count, 2 * F), jnp.bfloat16),
        compiler_params=pltpu.CompilerParams(vmem_limit_bytes=VMEM_LIMIT),
        name="place",
    )(rows, arrived)


def correlate_kernel(hop_index, group, *refs):
    own_ref, other_ref, inverse_ref = refs[1:4]
    out_ref, mine, theirs, cross = refs[-4:]
    width = own_ref.shape[0] // NWIN
    step = pl.program_id(0)

    @pl.when(step == 0)
    def _():
        for w in range(NWIN):
            rows = slice(w * width, (w + 1) * width)
            real = own_ref[rows, :F].astype(jnp.float32)
            imag = own_ref[rows, F:].astype(jnp.float32)
            mine[0, rows, :] = real + imag
            mine[1, rows, :] = real
            mine[2, rows, :] = imag
            real = other_ref[rows, :F].astype(jnp.float32)
            imag = other_ref[rows, F:].astype(jnp.float32)
            theirs[0, rows, :] = real
            theirs[1, rows, :] = real + imag
            theirs[2, rows, :] = real - imag

    blocks = [
        pl.ds(pl.multiple_of(w * width + step * group, group), group) for w in range(NWIN)
    ]
    for tile in range(F // 128):
        lanes = slice(tile * 128, (tile + 1) * 128)
        for first in range(0, group, 2):
            total = [[None] * 3 for _ in range(2)]
            for w in range(NWIN):
                for j in range(3):
                    factor = theirs[j, w * width : (w + 1) * width, lanes]
                    rows = mine.at[j, blocks[w], lanes]
                    for c in range(2):
                        term = factor * rows[first + c : first + c + 1, :]
                        total[c][j] = term if w == 0 else total[c][j] + term
            for c in range(2):
                rows = slice((first + c) * width, (first + c + 1) * width)
                cross[rows, tile * 128 : (tile + 1) * 128] = (total[c][0] - total[c][2]).astype(
                    jnp.bfloat16
                )
                cross[rows, F + tile * 128 : F + (tile + 1) * 128] = (
                    total[c][0] - total[c][1]
                ).astype(jnp.bfloat16)
    lagged = jnp.dot(cross[...], inverse_ref[...], preferred_element_type=jnp.float32)
    lagged = (lagged * (1.0 / math.sqrt(F * NWIN))).reshape(group, width, NLAG)
    if hop_index == 0:
        shape = (group, width, NLAG)
        channel = lax.broadcasted_iota(jnp.int32, shape, 0) + step * group
        lagged = jnp.where(channel == lax.broadcasted_iota(jnp.int32, shape, 1), 0.0, lagged)
    out_ref[...] = lagged.astype(jnp.bfloat16)[:, None]


def correlate(own, other, inverse, hop, result):
    rec_count = own.shape[0]
    width = rec_count // NWIN
    group = 8
    whole = lambda shape: pl.BlockSpec(shape, lambda i, h: (0,) * len(shape))
    in_specs = [whole(own.shape), whole(other.shape), whole(inverse.shape)]
    operands = [jnp.asarray(hop, jnp.int32).reshape(1), own, other, inverse]
    aliases = {}
    if result is not None:
        in_specs.append(pl.BlockSpec(memory_space=pl.ANY))
        operands.append(result)
        aliases = {4: 0}
    pairs = width * width
    return pl.pallas_call(
        functools.partial(correlate_kernel, hop if isinstance(hop, int) else None, group),
        grid_spec=pltpu.PrefetchScalarGridSpec(
            num_scalar_prefetch=1,
            grid=(width // group,),
            in_specs=in_specs,
            out_specs=pl.BlockSpec((group, 1, width, NLAG), lambda i, h: (i, h[0], 0, 0)),
            scratch_shapes=[
                pltpu.VMEM((3, rec_count, F), jnp.float32),
                pltpu.VMEM((3, rec_count, F), jnp.float32),
                pltpu.VMEM((group * width, 2 * F), jnp.bfloat16),
            ],
        ),
        out_shape=jax.ShapeDtypeStruct((width, HOPS + 1, width, NLAG), jnp.bfloat16),
        input_output_aliases=aliases,
        compiler_params=pltpu.CompilerParams(vmem_limit_bytes=VMEM_LIMIT),
        cost_estimate=pl.CostEstimate(
            flops=pairs * 2 * F * NLAG * 4, bytes_accessed=pairs * NLAG * 2, transcendentals=0
        ),
        name="correlate",
    )(*operands)


def on_device(traces, record_id):
    rec_count = traces.shape[0]
    peers = lax.axis_size("blk")
    capacity = 2 * rec_count // peers
    slots = peers * capacity
    all_ids = lax.all_to_all(
        jnp.broadcast_to(record_id[None, None], (peers, 1, rec_count)),
        "blk",
        split_axis=0,
        concat_axis=0,
        tiled=True,
    ).reshape(peers, rec_count)
    outgoing = spectra(traces, record_id, capacity, slots).reshape(peers, capacity, 2 * F)
    arrived = lax.all_to_all(outgoing, "blk", split_axis=0, concat_axis=0, tiled=True)
    arrived, rows, inverse = lax.optimization_barrier(
        (arrived, arrival_rows(all_ids, capacity), inverse_table())
    )
    own = place(rows, arrived.reshape(slots, 2 * F), rec_count)

    odd = lax.axis_index("blk") % 2
    near_hop, far_hop = 1 + 2 * odd, 3 - 2 * odd
    ahead = moved(own, lambda i: i + 2)
    near = moved(own, lambda i: i + 3 if i % 2 else i + 1)
    result = correlate(own, own, inverse, 0, None)
    ahead, result = lax.optimization_barrier((ahead, result))
    far = moved(ahead, lambda i: i ^ 1)
    result = correlate(own, ahead, inverse, 2, result)
    near, result = lax.optimization_barrier((near, result))
    result = correlate(own, near, inverse, near_hop, result)
    far, result = lax.optimization_barrier((far, result))
    return correlate(own, far, inverse, far_hop, result)


def solution(mesh):
    return jax.shard_map(
        on_device,
        mesh=mesh,
        in_specs=(P(("groups", "blk"), None), P(("groups", "blk"))),
        out_specs=P(("groups", "blk"), None, None, None),
        check_vma=False,
    )
```

time: 134 us -> 105 us (0.78)
  waiting for transfers between devices: 28.6 us -> 12.5 us
  Pallas kernels: 65.5 us -> 58.2 us
  starting transfers between devices: 23.3 us -> 19 us
  other arithmetic: 11.7 us -> 9.72 us
  local copies, waits for them, and re-layouts: 3.66 us -> 5.28 us
    all_to_all x1, waiting for transfers between devices: 21.6 us -> 10.9 us  [on_device(): lax.all_to_all(outgoing, 'blk', split_axis=0, concat_axis=0, tiled=True)]
    pallas_call x7, Pallas kernels: 65.5 us -> 58.2 us  [the longest x4 41.2 us: correlate(): pl.pallas_call(functools.partial(correlate_kernel, hop if isinstance(hop,...]
    ppermute x3, waiting for transfers between devices: 7.02 us -> 1.64 us  [moved(): lax.ppermute(block, 'blk', [(source_of(i) % count, i) for i in range(coun...]
    ppermute x3, starting transfers between devices: 9.9 us -> 5.49 us  [moved(): lax.ppermute(block, 'blk', [(source_of(i) % count, i) for i in range(coun...]
    unnamed x10 -> x11, local copies, waits for them, and re-layouts: 1.78 us -> 3.99 us
    reshape x2 -> x0, local copies, waits for them, and re-layouts: 1.35 us -> none  [the longest x1 0.67 us: on_device(): labels.reshape(peer_count, 1, capacity)]
  transfers between devices with their start and end apart: 5 -> 5, of which waited for: 2 -> 2; matrix products, arithmetic and copies ran while one was open for 8% -> 10% of each run, Pallas kernels for 39% -> 43%
where the time goes in v1:
time: 105 us
  Pallas kernels  58.2 us (55%)
  starting transfers between devices  19 us (18%)
  waiting for transfers between devices  12.5 us (12%)
  other arithmetic  9.72 us (9%)
  local copies, waits for them, and re-layouts  5.28 us (5%)
    pallas_call x4, Pallas kernels, correlate(): pl.pallas_call(functools.partial(correlate_kernel, hop if isinstance(hop,...  41.2 us
    pallas_call x1, Pallas kernels, spectra(): pl.pallas_call(functools.partial(spectrum_kernel, capacity), grid=(STEPS,...  12.8 us
    all_to_all x1, waiting for transfers between devices, on_device(): lax.all_to_all(outgoing, 'blk', split_axis=0, concat_axis=0, tiled=True)  10.9 us
    another operation x1, other arithmetic  8.31 us
    all_to_all x1, starting transfers between devices, on_device(): lax.all_to_all(jnp.broadcast_to(record_id[None, None], (peers, 1, rec_cou...  7.39 us
    all_to_all x1, starting transfers between devices, on_device(): lax.all_to_all(outgoing, 'blk', split_axis=0, concat_axis=0, tiled=True)  6.14 us
    ppermute x3, starting transfers between devices, moved(): lax.ppermute(block, 'blk', [(source_of(i) % count, i) for i in range(coun...  5.49 us
    unnamed x11, local copies, waits for them, and re-layouts  3.99 us
  transfers between devices with their start and end apart: 5, of which 2 were waited for; matrix products, arithmetic and copies ran while one was open for 10% of the time, Pallas kernels for 43%

profile of v1, /device:TPU:0, one launch (start us, length us, event | category | flops | bytes accessed | tf_op | source)
XLA Modules:
  0.0 104.7 jit_solution(8042262571163162964)
XLA Ops:
  0.0 1.3 %broadcast_in_dim.2 = s32[16,1,256]{2,1,0:T(1,128)} broadcast(s32[256]{0:T(256)} %param.5), dimensions={2} | broadcast | bytes 17408 | tf_op jit(solution)/shard_map/broadcast_in_dim | solution.py:258
  1.3 7.4 %all-to-all-start.1 = ((s32[16,1,256]{2,1,0:T(1,128)}), s32[16,1,256]{2,1,0:T(1,128)S(1)}, u32[]{:S(2)}, u32[]{:S(2)}) async-start(s32[16,1,256]{2,1,0:T(1,128)} %broadcast_in_dim.2), calls=%async_computation.1 | async-start | bytes 32768 | tf_op jit(solution)/shard_map/all_to_all | solution.py:257
  8.7 12.8 %spectra.1 = bf16[512,1024]{1,0:T(8,128)(2,1)} custom-call(s32[1,256]{1,0:T(1,128)} %bitcast.15, bf16[12000,256]{1,0:T(8,128)(2,1)} %bitcast.10, bf16[12000,256]{1,0:T(8,128)(2,1)} %bitcast.11, bf16[5,1024,1200]{2,1,0:T(8,128)(2,1)} %constant.46.clone.table_ref), custom_call_target="tpu_custom_call" | custom-call | flops 6291456000 | bytes 18432000 | tf_op jit(solution)/shard_map/spectra/pallas_call | solution.py:88
  21.4 0.0 all-to-all-done.1
  21.4 6.1 %all-to-all-start = ((bf16[16,32,1024]{2,1,0:T(8,128)(2,1)}), bf16[16,32,1024]{2,1,0:T(8,128)(2,1)S(1)}, u32[]{:S(2)}, u32[]{:S(2)}) async-start(bf16[16,32,1024]{2,1,0:T(8,128)(2,1)} %bitcast.12), calls=%async_computation | async-start | bytes 2097152 | tf_op jit(solution)/shard_map/all_to_all | solution.py:265
  27.6 8.3 %cosine_convert_fusion = (bf16[512,801]{1,0:T(8,128)(2,1)S(1)}, bf16[512,801]{1,0:T(8,128)(2,1)S(1)}) fusion(s32[801]{0:T(1024)S(1)} %iota_add_fusion, s32[512]{0:T(512)S(1)} %copy-done.4), kind=kLoop, calls=%fused_computation.5 | loop fusion | flops 4921344 | bytes 1645700 | tf_op jit(solution)/shard_map/convert
  35.9 1.4 %pad_maximum_fusion.refs_3_ = bf16[1024,801]{1,0:T(8,128)(2,1)} fusion(bf16[512,801]{1,0:T(8,128)(2,1)S(1)} %get-tuple-element.24, bf16[512,801]{1,0:T(8,128)(2,1)S(1)} %get-tuple-element.23), kind=kLoop, calls=%fused_computation.3 | loop fusion | flops 3280896 | bytes 3280896 | tf_op jit(solution)/shard_map/concatenate | solution.py:36
  37.3 0.6 copy.10
  37.9 1.7 %rows.1.row_ref = s32[1,512]{1,0:T(1,128)} custom-call(s32[1]{0:T(128)} %bitcast.4.me_ref, s32[16,256]{1,0:T(8,128)} %bitcast.14), custom_call_target="tpu_custom_call" | custom-call | tf_op jit(solution)/shard_map/rows/pallas_call | solution.py:139
  39.7 10.9 %all-to-all-done = bf16[16,32,1024]{2,1,0:T(8,128)(2,1)S(1)} async-done(((bf16[16,32,1024]{2,1,0:T(8,128)(2,1)}), bf16[16,32,1024]{2,1,0:T(8,128)(2,1)S(1)}, u32[]{:S(2)}, u32[]{:S(2)}) %all-to-all-start) | async-done | bytes 1048608 | tf_op jit(solution)/shard_map/all_to_all | solution.py:265
  50.5 1.0 copy-done
  51.5 2.5 %place.1.refs_1_.refs_2_ = bf16[256,1024]{1,0:T(8,128)(2,1)} custom-call(s32[1,512]{1,0:T(1,128)} %rows.1.row_ref, bf16[512,1024]{1,0:T(8,128)(2,1)} %bitcast.13), custom_call_target="tpu_custom_call" | custom-call | tf_op jit(solution)/shard_map/place/pallas_call | solution.py:156
  54.0 5.5 %collective-permute-start = (bf16[256,1024]{1,0:T(8,128)(2,1)}, bf16[256,1024]{1,0:T(8,128)(2,1)S(1)}, u32[]{:S(2)}, u32[]{:S(2)}) collective-permute-start(bf16[256,1024]{1,0:T(8,128)(2,1)} %place.1.refs_1_.refs_2_), channel_id=1, source_target_pairs={{2,0},{3,1},{4,2},{5,3},{6,4},{7,5},{8,6},{9,7},{10,8},{11,9},{12,... | collective-permute-start | bytes 1572872 | tf_op jit(solution)/shard_map/ppermute | solution.py:28
  59.4 0.0 collective-permute-start.2
  59.4 10.3 %correlate.4.refs_4_ = bf16[32,4,32,801]{3,2,1,0:T(8,128)(2,1)} custom-call(s32[1]{0:T(128)} %constant.44.clone.1.refs_0_, bf16[256,1024]{1,0:T(8,128)(2,1)} %place.1.refs_1_.refs_2_, bf16[256,1024]{1,0:T(8,128)(2,1)} %place.1.refs_1_.refs_2_, bf16[1024,801]{1,0:T(8,128)(2,1)} %pad_maximum_fusion.refs_3_), custom_call_target="tpu_custom_call" | custom-call | flops 3359637504 | bytes 1640448 | tf_op jit(solution)/shard_map/correlate/pallas_call | solution.py:229
  69.8 1.6 %collective-permute-done.refs_2_ = bf16[256,1024]{1,0:T(8,128)(2,1)S(1)} collective-permute-done((bf16[256,1024]{1,0:T(8,128)(2,1)}, bf16[256,1024]{1,0:T(8,128)(2,1)S(1)}, u32[]{:S(2)}, u32[]{:S(2)}) %collective-permute-start) | collective-permute-done | bytes 524320 | tf_op jit(solution)/shard_map/ppermute | solution.py:28
  71.4 0.0 collective-permute-start.1
  71.4 0.8 copy-done.1
  72.2 10.3 %correlate.5.refs_4_ = bf16[32,4,32,801]{3,2,1,0:T(8,128)(2,1)} custom-call(s32[1]{0:T(128)} %constant.45.clone.1.refs_0_, bf16[256,1024]{1,0:T(8,128)(2,1)} %place.1.refs_1_.refs_2_, bf16[256,1024]{1,0:T(8,128)(2,1)} %copy-done.1, bf16[1024,801]{1,0:T(8,128)(2,1)} %pad_maximum_fusion.refs_3_, ...), custom_call_target="tpu_custom_call", output_to_operand_aliasing={{}: (4, {})} | custom-call | flops 3359637504 | bytes 1640448 | tf_op jit(solution)/shard_map/correlate/pallas_call | solution.py:229
  82.5 0.0 collective-permute-done.2.refs_2_
  82.5 0.8 copy-done.3
  83.3 10.3 %correlate.6.refs_4_ = bf16[32,4,32,801]{3,2,1,0:T(8,128)(2,1)} custom-call(s32[1]{0:T(128)} %bitcast.6.refs_0_, bf16[256,1024]{1,0:T(8,128)(2,1)} %place.1.refs_1_.refs_2_, bf16[256,1024]{1,0:T(8,128)(2,1)} %copy-done.3, bf16[1024,801]{1,0:T(8,128)(2,1)} %pad_maximum_fusion.refs_3_, ...), custom_call_target="tpu_custom_call", output_to_operand_aliasing={{}: (4, {})} | custom-call | flops 3359637504 | bytes 1640448 | tf_op jit(solution)/shard_map/correlate/pallas_call | solution.py:229
  93.6 0.8 copy-done.2
  94.4 10.3 %correlate.7 = bf16[32,4,32,801]{3,2,1,0:T(8,128)(2,1)} custom-call(s32[1]{0:T(128)} %bitcast.refs_0_, bf16[256,1024]{1,0:T(8,128)(2,1)} %place.1.refs_1_.refs_2_, bf16[256,1024]{1,0:T(8,128)(2,1)} %copy-done.2, bf16[1024,801]{1,0:T(8,128)(2,1)} %pad_maximum_fusion.refs_3_, bf16[32,4,32,801]{3,2,1,0:T(8,128)(2,1)} %correlate.6.refs_4_), custom_call_target="tpu_custom_call", output_to_operand_aliasing={{}: (4, {})} | custom-call | flops 3359637504 | bytes 1640448 | tf_op jit(solution)/shard_map/correlate/pallas_call | solution.py:229
  (8 shorter events, 0.0 us)
Async XLA Ops:
  1.3 20.2 %all-to-all-start.1 = ((s32[16,1,256]{2,1,0:T(1,128)}), s32[16,1,256]{2,1,0:T(1,128)S(1)}, u32[]{:S(2)}, u32[]{:S(2)}) async-start(s32[16,1,256]{2,1,0:T(1,128)} %broadcast_in_dim.2), calls=%async_computation.1 | async-start | bytes 32768 | tf_op jit(solution)/shard_map/all_to_all | solution.py:257
  21.4 6.2 %copy-start.4 = (s32[512]{0:T(512)S(1)}, s32[512]{0:T(512)}, u32[]{:S(2)}) copy-start(s32[512]{0:T(512)} %constant.47.clone) | copy-start | bytes 6148
  21.4 29.1 %all-to-all-start = ((bf16[16,32,1024]{2,1,0:T(8,128)(2,1)}), bf16[16,32,1024]{2,1,0:T(8,128)(2,1)S(1)}, u32[]{:S(2)}, u32[]{:S(2)}) async-start(bf16[16,32,1024]{2,1,0:T(8,128)(2,1)} %bitcast.12), calls=%async_computation | async-start | bytes 2097152 | tf_op jit(solution)/shard_map/all_to_all | solution.py:265
  50.5 1.0 copy-start
  54.0 17.4 %collective-permute-start = (bf16[256,1024]{1,0:T(8,128)(2,1)}, bf16[256,1024]{1,0:T(8,128)(2,1)S(1)}, u32[]{:S(2)}, u32[]{:S(2)}) collective-permute-start(bf16[256,1024]{1,0:T(8,128)(2,1)} %place.1.refs_1_.refs_2_), channel_id=1, source_target_pairs={{2,0},{3,1},{4,2},{5,3},{6,4},{7,5},{8,6},{9,7},{10,8},{11,9},{12,... | collective-permute-start | bytes 1572872 | tf_op jit(solution)/shard_map/ppermute | solution.py:28
  59.4 23.1 %collective-permute-start.2 = (bf16[256,1024]{1,0:T(8,128)(2,1)}, bf16[256,1024]{1,0:T(8,128)(2,1)S(1)}, u32[]{:S(2)}, u32[]{:S(2)}) collective-permute-start(bf16[256,1024]{1,0:T(8,128)(2,1)} %place.1.refs_1_.refs_2_), channel_id=1, source_target_pairs={{1,0},{4,1},{3,2},{6,3},{5,4},{8,5},{7,6},{10,7},{9,8},{12,9},{11,... | collective-permute-start | bytes 1572872 | tf_op jit(solution)/shard_map/ppermute | solution.py:28
  71.4 0.8 copy-start.1
  71.4 22.2 %collective-permute-start.1 = (bf16[256,1024]{1,0:T(8,128)(2,1)S(1)}, bf16[256,1024]{1,0:T(8,128)(2,1)S(1)}, u32[]{:S(2)}, u32[]{:S(2)}) collective-permute-start(bf16[256,1024]{1,0:T(8,128)(2,1)S(1)} %collective-permute-done.refs_2_), channel_id=1, source_target_pairs={{1,0},{0,1},{3,2},{2,3},{5,4},{4,5},{7,6},{6,7},{9,8},{8,9},{11,10... | collective-permute-start | bytes 1572872 | tf_op jit(solution)/shard_map/ppermute | solution.py:28
  82.5 0.8 copy-start.3
  93.6 0.8 copy-start.2

commit v2 on v1

--- a/solution.py
+++ b/solution.py
@@ -19,8 +19,10 @@
 HALF = WS // 2
 CHUNK = 1200
 STEPS = HALF // CHUNK
+PLUS = 384
+LANES = 512
 BINS = LOWBIN + np.concatenate([np.arange(0, F, 2), np.arange(1, F, 2)])
-VMEM_LIMIT = 56 * 1024 * 1024
+MIB = 1024 * 1024
 
 
 def moved(block, source_of):
@@ -30,11 +32,10 @@
 
 def inverse_table():
     bin_index = jnp.asarray(BINS, jnp.int32)[:, None]
-    lag_index = jnp.arange(NLAG, dtype=jnp.int32)[None, :] - LAG + WS
+    lag_index = jnp.arange(LANES, dtype=jnp.int32)[None, :] - (LAG - PLUS) + WS
     residue = (bin_index * lag_index % WS).astype(jnp.float32)
     angles = 2.0 * math.pi / WS * residue
-    table = jnp.concatenate([jnp.cos(angles), -jnp.sin(angles)], axis=0)
-    return table.astype(jnp.bfloat16)
+    return jnp.cos(angles).astype(jnp.bfloat16), (-jnp.sin(angles)).astype(jnp.bfloat16)
 
 
 def forward_table():
@@ -100,7 +101,7 @@
             pltpu.VMEM((2 * F, rec_count), jnp.float32),
             pltpu.VMEM((2 * F, rec_count), jnp.float32),
         ],
-        compiler_params=pltpu.CompilerParams(vmem_limit_bytes=VMEM_LIMIT),
+        compiler_params=pltpu.CompilerParams(vmem_limit_bytes=56 * MIB),
         cost_estimate=pl.CostEstimate(
             flops=4 * rec_count * WS * F, bytes_accessed=2 * WS * (rec_count + F), transcendentals=0
         ),
@@ -156,13 +157,13 @@
     return pl.pallas_call(
         place_kernel,
         out_shape=jax.ShapeDtypeStruct((rec_count, 2 * F), jnp.bfloat16),
-        compiler_params=pltpu.CompilerParams(vmem_limit_bytes=VMEM_LIMIT),
+        compiler_params=pltpu.CompilerParams(vmem_limit_bytes=8 * MIB),
         name="place",
     )(rows, arrived)
 
 
 def correlate_kernel(hop_index, group, *refs):
-    own_ref, other_ref, inverse_ref = refs[1:4]
+    own_ref, other_ref, cos_ref, sin_ref = refs[1:5]
     out_ref, mine, theirs, cross = refs[-4:]
     width = own_ref.shape[0] // NWIN
     step = pl.program_id(0)
@@ -204,8 +205,22 @@
                 cross[rows, F + tile * 128 : F + (tile + 1) * 128] = (
                     total[c][0] - total[c][1]
                 ).astype(jnp.bfloat16)
-    lagged = jnp.dot(cross[...], inverse_ref[...], preferred_element_type=jnp.float32)
-    lagged = (lagged * (1.0 / math.sqrt(F * NWIN))).reshape(group, width, NLAG)
+    unit = 1.0 / math.sqrt(F * NWIN)
+    even = jnp.dot(cross[:, :F], cos_ref[...], preferred_element_type=jnp.float32)
+    uneven = jnp.dot(cross[:, F:], sin_ref[...], preferred_element_type=jnp.float32)
+    later = (even + uneven) * unit
+    earlier = (even - uneven) * unit
+    rows = group * width
+    lane = lax.broadcasted_iota(jnp.int32, (rows, 128), 1)
+    last = (2 * LAG - PLUS) % 128
+    mirror = (last - lane) & 127
+    turned = [
+        jnp.take_along_axis(earlier[:, q * 128 : (q + 1) * 128], mirror, axis=1)
+        for q in range(LANES // 128)
+    ]
+    top = (2 * LAG - PLUS) // 128
+    pieces = [jnp.where(lane <= last, turned[top - t], turned[top - 1 - t]) for t in range(PLUS // 128)]
+    lagged = jnp.concatenate(pieces + [later[:, : NLAG - PLUS]], axis=1).reshape(group, width, NLAG)
     if hop_index == 0:
         shape = (group, width, NLAG)
         channel = lax.broadcasted_iota(jnp.int32, shape, 0) + step * group
@@ -218,13 +233,13 @@
     width = rec_count // NWIN
     group = 8
     whole = lambda shape: pl.BlockSpec(shape, lambda i, h: (0,) * len(shape))
-    in_specs = [whole(own.shape), whole(other.shape), whole(inverse.shape)]
-    operands = [jnp.asarray(hop, jnp.int32).reshape(1), own, other, inverse]
+    in_specs = [whole(own.shape), whole(other.shape), whole((F, LANES)), whole((F, LANES))]
+    operands = [jnp.asarray(hop, jnp.int32).reshape(1), own, other, *inverse]
     aliases = {}
     if result is not None:
         in_specs.append(pl.BlockSpec(memory_space=pl.ANY))
         operands.append(result)
-        aliases = {4: 0}
+        aliases = {5: 0}
     pairs = width * width
     return pl.pallas_call(
         functools.partial(correlate_kernel, hop if isinstance(hop, int) else None, group),
@@ -241,7 +256,7 @@
         ),
         out_shape=jax.ShapeDtypeStruct((width, HOPS + 1, width, NLAG), jnp.bfloat16),
         input_output_aliases=aliases,
-        compiler_params=pltpu.CompilerParams(vmem_limit_bytes=VMEM_LIMIT),
+        compiler_params=pltpu.CompilerParams(vmem_limit_bytes=14 * MIB),
         cost_estimate=pl.CostEstimate(
             flops=pairs * 2 * F * NLAG * 4, bytes_accessed=pairs * NLAG * 2, transcendentals=0
         ),
@@ -254,15 +269,16 @@
     peers = lax.axis_size("blk")
     capacity = 2 * rec_count // peers
     slots = peers * capacity
+    outgoing = spectra(traces, record_id, capacity, slots).reshape(peers, capacity, 2 * F)
+    outgoing, ids = lax.optimization_barrier((outgoing, record_id))
+    arrived = lax.all_to_all(outgoing, "blk", split_axis=0, concat_axis=0, tiled=True)
     all_ids = lax.all_to_all(
-        jnp.broadcast_to(record_id[None, None], (peers, 1, rec_count)),
+        jnp.broadcast_to(ids[None, None], (peers, 1, rec_count)),
         "blk",
         split_axis=0,
         concat_axis=0,
         tiled=True,
     ).reshape(peers, rec_count)
-    outgoing = spectra(traces, record_id, capacity, slots).reshape(peers, capacity, 2 * F)
-    arrived = lax.all_to_all(outgoing, "blk", split_axis=0, concat_axis=0, tiled=True)
     arrived, rows, inverse = lax.optimization_barrier(
         (arrived, arrival_rows(all_ids, capacity), inverse_table())
     )

time: 105 us -> 94.6 us (0.901)
  blocking collectives: 0 us -> 13.7 us
  Pallas kernels: 58.2 us -> 45.3 us
  starting transfers between devices: 19 us -> 9.15 us
  waiting for transfers between devices: 12.5 us -> 20 us
  other arithmetic: 9.72 us -> 4.72 us
  local copies, waits for them, and re-layouts: 5.28 us -> 1.27 us
    all_to_all x0 -> x1, blocking collectives: none -> 13.7 us  [on_device(): lax.all_to_all(jnp.broadcast_to(ids[None, None], (peers, 1, rec_count)),...]
    pallas_call x4, Pallas kernels: 41.2 us -> 29.6 us  [correlate(): pl.pallas_call(functools.partial(correlate_kernel, hop if isinstance(hop,...]
    another operation x1 -> x0, other arithmetic: 8.31 us -> none
    all_to_all x1 -> x0, starting transfers between devices: 7.39 us -> none  [on_device(): lax.all_to_all(jnp.broadcast_to(record_id[None, None], (peers, 1, rec_cou...]
    all_to_all x1, waiting for transfers between devices: 10.9 us -> 15.8 us  [on_device(): lax.all_to_all(outgoing, 'blk', split_axis=0, concat_axis=0, tiled=True)]
    convert_element_type x0 -> x1, other arithmetic: none -> 4.72 us  [inverse_table(): (-jnp.sin(angles)).astype(jnp.bfloat16)]
    unnamed x11 -> x7, local copies, waits for them, and re-layouts: 3.99 us -> 1.26 us
    ppermute x3, waiting for transfers between devices: 1.64 us -> 4.21 us  [moved(): lax.ppermute(block, 'blk', [(source_of(i) % count, i) for i in range(coun...]
  transfers between devices with their start and end apart: 5 -> 4, of which waited for: 2 -> 2; matrix products, arithmetic and copies ran while one was open for 10% -> 6% of each run, Pallas kernels for 43% -> 25%
where the time goes in v2:
time: 94.6 us; the launch traced here: 94.2 us
  Pallas kernels  45.3 us (48%)
  waiting for transfers between devices  20 us (21%)
  blocking collectives  13.7 us (14%)
  starting transfers between devices  9.15 us (10%)
  other arithmetic  4.72 us (5%)
  local copies, waits for them, and re-layouts  1.27 us (1%)
    pallas_call x4, Pallas kernels, correlate(): pl.pallas_call(functools.partial(correlate_kernel, hop if isinstance(hop,...  29.6 us
    all_to_all x1, waiting for transfers between devices, on_device(): lax.all_to_all(outgoing, 'blk', split_axis=0, concat_axis=0, tiled=True)  15.8 us
    all_to_all x1, blocking collectives, on_device(): lax.all_to_all(jnp.broadcast_to(ids[None, None], (peers, 1, rec_count)),...  13.7 us
    pallas_call x1, Pallas kernels, spectra(): pl.pallas_call(functools.partial(spectrum_kernel, capacity), grid=(STEPS,...  13.5 us
    ppermute x3, starting transfers between devices, moved(): lax.ppermute(block, 'blk', [(source_of(i) % count, i) for i in range(coun...  5.49 us
    convert_element_type x1, other arithmetic, inverse_table(): (-jnp.sin(angles)).astype(jnp.bfloat16)  4.72 us
    ppermute x3, waiting for transfers between devices, moved(): lax.ppermute(block, 'blk', [(source_of(i) % count, i) for i in range(coun...  4.21 us
    all_to_all x1, starting transfers between devices, on_device(): lax.all_to_all(outgoing, 'blk', split_axis=0, concat_axis=0, tiled=True)  3.66 us
  transfers between devices with their start and end apart: 4, of which 2 were waited for; matrix products, arithmetic and copies ran while one was open for 6% of the time, Pallas kernels for 25%

profile of v2, /device:TPU:0, one launch (start us, length us, event | category | flops | bytes accessed | tf_op | source)
XLA Modules:
  0.0 94.2 jit_solution(2268503477804795597)
XLA Ops:
  0.0 0.0 copy-start.1
  0.0 0.0 copy-start.2
  0.0 13.5 %spectra.1 = bf16[512,1024]{1,0:T(8,128)(2,1)} custom-call(s32[1,256]{1,0:T(1,128)} %bitcast.15, bf16[12000,256]{1,0:T(8,128)(2,1)} %bitcast.11, bf16[12000,256]{1,0:T(8,128)(2,1)} %bitcast.12, bf16[5,1024,1200]{2,1,0:T(8,128)(2,1)} %constant.46.clone.table_ref), custom_call_target="tpu_custom_call" | custom-call | flops 6291456000 | bytes 18432000 | tf_op jit(solution)/shard_map/spectra/pallas_call | solution.py:89
  13.5 0.0 copy-done.1
  13.5 13.7 %all_to_all.10 = s32[16,1,256]{2,1,0:T(1,128)S(1)} all-to-all(s32[16,1,256]{2,1,0:T(1,128)S(1)} %broadcast_in_dim.2), channel_id=1, replica_groups=mesh['groups'=2,'blk'=16] {'blk'}, dimensions={0} | all-to-all | bytes 32768 | tf_op jit(solution)/shard_map/all_to_all | solution.py:275
  27.2 3.7 %all-to-all-start = ((bf16[16,32,1024]{2,1,0:T(8,128)(2,1)}), bf16[16,32,1024]{2,1,0:T(8,128)(2,1)S(1)}, u32[]{:S(2)}, u32[]{:S(2)}) async-start(bf16[16,32,1024]{2,1,0:T(8,128)(2,1)} %bitcast.13), calls=%async_computation | async-start | bytes 2097152 | tf_op jit(solution)/shard_map/all_to_all | solution.py:274
  30.9 0.0 copy-done.2
  30.9 4.7 %negate_convert_fusion = (bf16[512,512]{1,0:T(8,128)(2,1)S(1)}, bf16[512,512]{1,0:T(8,128)(2,1)S(1)}) fusion(s32[512]{0:T(512)S(1)} %iota_add_fusion, s32[512]{0:T(512)S(1)} %copy-done.2), kind=kLoop, calls=%fused_computation.3 | loop fusion | flops 3145728 | bytes 1052672 | tf_op jit(solution)/shard_map/convert_element_type | solution.py:38
  35.6 0.6 copy.10
  36.2 1.7 %rows.1.row_ref = s32[1,512]{1,0:T(1,128)} custom-call(s32[1]{0:T(128)} %bitcast.4.me_ref, s32[16,256]{1,0:T(8,128)} %bitcast.14), custom_call_target="tpu_custom_call" | custom-call | tf_op jit(solution)/shard_map/rows/pallas_call | solution.py:140
  37.9 15.8 %all-to-all-done = bf16[16,32,1024]{2,1,0:T(8,128)(2,1)S(1)} async-done(((bf16[16,32,1024]{2,1,0:T(8,128)(2,1)}), bf16[16,32,1024]{2,1,0:T(8,128)(2,1)S(1)}, u32[]{:S(2)}, u32[]{:S(2)}) %all-to-all-start) | async-done | bytes 1048608 | tf_op jit(solution)/shard_map/all_to_all | solution.py:274
  53.8 0.0 copy-start
  53.8 0.7 copy-done
  54.4 0.4 place.1.refs_1_.refs_2_
  54.9 5.5 %collective-permute-start = (bf16[256,1024]{1,0:T(8,128)(2,1)S(1)}, bf16[256,1024]{1,0:T(8,128)(2,1)S(1)}, u32[]{:S(2)}, u32[]{:S(2)}) collective-permute-start(bf16[256,1024]{1,0:T(8,128)(2,1)S(1)} %place.1.refs_1_.refs_2_), channel_id=1, source_target_pairs={{2,0},{3,1},{4,2},{5,3},{6,4},{7,5},{8,6},{9,7},{10,8},{11,9},{12,... | collective-permute-start | bytes 1572872 | tf_op jit(solution)/shard_map/ppermute | solution.py:30
  60.4 0.0 collective-permute-start.2
  60.4 7.4 %correlate.4.refs_5_ = bf16[32,4,32,801]{3,2,1,0:T(8,128)(2,1)} custom-call(s32[1]{0:T(128)} %constant.44.clone.1.refs_0_, bf16[256,1024]{1,0:T(8,128)(2,1)S(1)} %place.1.refs_1_.refs_2_, bf16[256,1024]{1,0:T(8,128)(2,1)S(1)} %place.1.refs_1_.refs_2_, bf16[512,512]{1,0:T(8,128)(2,1)S(1)} %get-tuple-element.21.refs_3_, ...), custom_call_target="tpu_custom_call" | custom-call | flops 3359637504 | bytes 1640448 | tf_op jit(solution)/shard_map/correlate/pallas_call | solution.py:244
  67.8 4.2 %collective-permute-done.refs_2_ = bf16[256,1024]{1,0:T(8,128)(2,1)S(1)} collective-permute-done((bf16[256,1024]{1,0:T(8,128)(2,1)S(1)}, bf16[256,1024]{1,0:T(8,128)(2,1)S(1)}, u32[]{:S(2)}, u32[]{:S(2)}) %collective-permute-start) | collective-permute-done | bytes 524320 | tf_op jit(solution)/shard_map/ppermute | solution.py:30
  72.0 0.0 collective-permute-start.1
  72.0 7.4 %correlate.5.refs_5_ = bf16[32,4,32,801]{3,2,1,0:T(8,128)(2,1)} custom-call(s32[1]{0:T(128)} %constant.45.clone.1.refs_0_, bf16[256,1024]{1,0:T(8,128)(2,1)S(1)} %place.1.refs_1_.refs_2_, bf16[256,1024]{1,0:T(8,128)(2,1)S(1)} %collective-permute-done.refs_2_, bf16[512,512]{1,0:T(8,128)(2,1)S(1)} %get-tuple-element.21.refs_3_, ...), custom_call_target="tpu_custom_call", output_to_operand_aliasing={{}: (5, {})} | custom-call | flops 3359637504 | bytes 1640448 | tf_op jit(solution)/shard_map/correlate/pallas_call | solution.py:244
  79.4 0.0 collective-permute-done.2.refs_2_
  79.4 7.4 %correlate.6.refs_5_ = bf16[32,4,32,801]{3,2,1,0:T(8,128)(2,1)} custom-call(s32[1]{0:T(128)} %bitcast.6.refs_0_, bf16[256,1024]{1,0:T(8,128)(2,1)S(1)} %place.1.refs_1_.refs_2_, bf16[256,1024]{1,0:T(8,128)(2,1)S(1)} %collective-permute-done.2.refs_2_, bf16[512,512]{1,0:T(8,128)(2,1)S(1)} %get-tuple-element.21.refs_3_, ...), custom_call_target="tpu_custom_call", output_to_operand_aliasing={{}: (5, {})} | custom-call | flops 3359637504 | bytes 1640448 | tf_op jit(solution)/shard_map/correlate/pallas_call | solution.py:244
  86.8 0.0 collective-permute-done.1.refs_2_
  86.8 7.4 %correlate.7 = bf16[32,4,32,801]{3,2,1,0:T(8,128)(2,1)} custom-call(s32[1]{0:T(128)} %bitcast.refs_0_, bf16[256,1024]{1,0:T(8,128)(2,1)S(1)} %place.1.refs_1_.refs_2_, bf16[256,1024]{1,0:T(8,128)(2,1)S(1)} %collective-permute-done.1.refs_2_, bf16[512,512]{1,0:T(8,128)(2,1)S(1)} %get-tuple-element.21.refs_3_, ...), custom_call_target="tpu_custom_call", output_to_operand_aliasing={{}: (5, {})} | custom-call | flops 3359637504 | bytes 1640448 | tf_op jit(solution)/shard_map/correlate/pallas_call | solution.py:244
  (2 shorter events, 0.0 us)
Async XLA Ops:
  0.0 13.5 %copy-start.1 = (s32[256]{0:T(256)S(1)}, s32[256]{0:T(256)}, u32[]{:S(2)}) copy-start(s32[256]{0:T(256)} %param.5) | copy-start | bytes 3076
  0.0 30.9 %copy-start.2 = (s32[512]{0:T(512)S(1)}, s32[512]{0:T(512)}, u32[]{:S(2)}) copy-start(s32[512]{0:T(512)} %constant.47.clone) | copy-start | bytes 6148
  27.2 26.6 %all-to-all-start = ((bf16[16,32,1024]{2,1,0:T(8,128)(2,1)}), bf16[16,32,1024]{2,1,0:T(8,128)(2,1)S(1)}, u32[]{:S(2)}, u32[]{:S(2)}) async-start(bf16[16,32,1024]{2,1,0:T(8,128)(2,1)} %bitcast.13), calls=%async_computation | async-start | bytes 2097152 | tf_op jit(solution)/shard_map/all_to_all | solution.py:274
  53.8 0.7 copy-start
  54.9 17.1 %collective-permute-start = (bf16[256,1024]{1,0:T(8,128)(2,1)S(1)}, bf16[256,1024]{1,0:T(8,128)(2,1)S(1)}, u32[]{:S(2)}, u32[]{:S(2)}) collective-permute-start(bf16[256,1024]{1,0:T(8,128)(2,1)S(1)} %place.1.refs_1_.refs_2_), channel_id=1, source_target_pairs={{2,0},{3,1},{4,2},{5,3},{6,4},{7,5},{8,6},{9,7},{10,8},{11,9},{12,... | collective-permute-start | bytes 1572872 | tf_op jit(solution)/shard_map/ppermute | solution.py:30
  60.4 19.1 %collective-permute-start.2 = (bf16[256,1024]{1,0:T(8,128)(2,1)S(1)}, bf16[256,1024]{1,0:T(8,128)(2,1)S(1)}, u32[]{:S(2)}, u32[]{:S(2)}) collective-permute-start(bf16[256,1024]{1,0:T(8,128)(2,1)S(1)} %place.1.refs_1_.refs_2_), channel_id=1, source_target_pairs={{1,0},{4,1},{3,2},{6,3},{5,4},{8,5},{7,6},{10,7},{9,8},{12,9},{11,... | collective-permute-start | bytes 1572872 | tf_op jit(solution)/shard_map/ppermute | solution.py:30
  72.0 14.8 %collective-permute-start.1 = (bf16[256,1024]{1,0:T(8,128)(2,1)S(1)}, bf16[256,1024]{1,0:T(8,128)(2,1)S(1)}, u32[]{:S(2)}, u32[]{:S(2)}) collective-permute-start(bf16[256,1024]{1,0:T(8,128)(2,1)S(1)} %collective-permute-done.refs_2_), channel_id=1, source_target_pairs={{1,0},{0,1},{3,2},{2,3},{5,4},{4,5},{7,6},{6,7},{9,8},{8,9},{11,10... | collective-permute-start | bytes 1572872 | tf_op jit(solution)/shard_map/ppermute | solution.py:30

commit v3 on v2

--- a/solution.py
+++ b/solution.py
@@ -22,6 +22,8 @@
 PLUS = 384
 LANES = 512
 BINS = LOWBIN + np.concatenate([np.arange(0, F, 2), np.arange(1, F, 2)])
+PACK = 4
+TAIL = 128
 MIB = 1024 * 1024
 
 
@@ -46,46 +48,62 @@
     return np.ascontiguousarray(table).astype(np.float32).astype(jnp.bfloat16)
 
 
-def spectrum_kernel(capacity, id_ref, x0_ref, x1_ref, table_ref, out_ref, first, second):
+def spectrum_kernel(capacity, id_ref, x0_ref, x1_ref, table_ref, out_ref, even, odd):
     step = pl.program_id(0)
 
-    @pl.when(step == 0)
-    def _():
-        first[...] = jnp.dot(table_ref[...], x0_ref[...], preferred_element_type=jnp.float32)
-        second[...] = jnp.dot(table_ref[...], x1_ref[...], preferred_element_type=jnp.float32)
-
-    @pl.when(step > 0)
-    def _():
-        first[...] += jnp.dot(table_ref[...], x0_ref[...], preferred_element_type=jnp.float32)
-        second[...] += jnp.dot(table_ref[...], x1_ref[...], preferred_element_type=jnp.float32)
+    def add(start):
+        for part, total in enumerate((even, odd)):
+            table = table_ref[part * F : (part + 1) * F, :]
+            first = jnp.dot(table, x0_ref[...], preferred_element_type=jnp.float32)
+            second = jnp.dot(table, x1_ref[...], preferred_element_type=jnp.float32)
+            both = first + second if part == 0 else first - second
+            total[...] = both if start else total[...] + both
+
+    pl.when(step == 0)(functools.partial(add, True))
+    pl.when(step > 0)(functools.partial(add, False))
 
     @pl.when(step == STEPS - 1)
     def _():
         rec_count = id_ref.shape[1]
-        owner = id_ref[...] // rec_count
+        ids = id_ref[...]
+        owner = ids // rec_count
         row = jnp.broadcast_to(owner, (rec_count, rec_count))
         before = lax.broadcasted_iota(jnp.int32, row.shape, 0) < lax.broadcasted_iota(
             jnp.int32, row.shape, 1
         )
         rank = jnp.sum(jnp.where((row == row.T) & before, 1, 0), axis=0, keepdims=True)
         target = owner * capacity + rank
-        slot = lax.broadcasted_iota(jnp.int32, (out_ref.shape[0], rec_count), 0)
-        pick = jnp.where(slot == target, 1.0, 0.0).astype(jnp.bfloat16)
-        first[:F, :] += second[:F, :]
-        first[F:, :] -= second[F:, :]
-        power = jnp.sum(first[...] * first[...], axis=0, keepdims=True) / F
+        label = (ids % rec_count + 1).astype(jnp.float32)
+        power = jnp.sum(even[...] * even[...], axis=0, keepdims=True)
+        power = (power + jnp.sum(odd[...] * odd[...], axis=0, keepdims=True)) / F
         scale = lax.rsqrt(power + 1e-06)
         half = F // 2
-        for place, base in enumerate((0, F, half, F + half)):
-            white = (first[base : base + half, :] * scale).astype(jnp.bfloat16)
-            out_ref[:, place * half : (place + 1) * half] = lax.dot_general(
-                pick, white, (((1,), (1,)), ((), ())), preferred_element_type=jnp.float32
-            ).astype(jnp.bfloat16)
+        white = [
+            (part[base : base + half, :] * scale).astype(jnp.bfloat16)
+            for part, base in ((even, 0), (odd, 0), (even, half), (odd, half))
+        ]
+        rows = out_ref.shape[0]
+        slot = lax.broadcasted_iota(jnp.int32, (rows, rec_count), 0) * PACK
+        lane = lax.broadcasted_iota(jnp.int32, (rows, TAIL), 1)
+        labels = jnp.zeros((rows, TAIL), jnp.float32)
+        for q in range(PACK):
+            hit = slot + q == target
+            labels = jnp.where(
+                lane == q, jnp.sum(jnp.where(hit, label, 0.0), axis=1, keepdims=True), labels
+            )
+            pick = jnp.where(hit, 1.0, 0.0).astype(jnp.bfloat16)
+            for place, block in enumerate(white):
+                base = q * 2 * F + place * half
+                out_ref[:, base : base + half] = lax.dot_general(
+                    pick, block, (((1,), (1,)), ((), ())), preferred_element_type=jnp.float32
+                ).astype(jnp.bfloat16)
+        out_ref[:, PACK * 2 * F :] = labels.astype(jnp.bfloat16)
 
 
 def spectra(traces, record_id, capacity, slots):
     rec_count = traces.shape[0]
     lanes = traces.T
+    shape = (slots // PACK, PACK * 2 * F + TAIL)
     return pl.pallas_call(
         functools.partial(spectrum_kernel, capacity),
         grid=(STEPS,),
@@ -95,11 +113,11 @@
             pl.BlockSpec((CHUNK, rec_count), lambda i: (i + STEPS, 0)),
             pl.BlockSpec((None, 2 * F, CHUNK), lambda i: (i, 0, 0)),
         ],
-        out_specs=pl.BlockSpec((slots, 2 * F), lambda i: (0, 0)),
-        out_shape=jax.ShapeDtypeStruct((slots, 2 * F), jnp.bfloat16),
+        out_specs=pl.BlockSpec(shape, lambda i: (0, 0)),
+        out_shape=jax.ShapeDtypeStruct(shape, jnp.bfloat16),
         scratch_shapes=[
-            pltpu.VMEM((2 * F, rec_count), jnp.float32),
-            pltpu.VMEM((2 * F, rec_count), jnp.float32),
+            pltpu.VMEM((F, rec_count), jnp.float32),
+            pltpu.VMEM((F, rec_count), jnp.float32),
         ],
         compiler_params=pltpu.CompilerParams(vmem_limit_bytes=56 * MIB),
         cost_estimate=pl.CostEstimate(
@@ -109,57 +127,32 @@
     )(record_id.reshape(1, rec_count), lanes, lanes, jnp.asarray(forward_table()))
 
 
-def rows_kernel(capacity, me_ref, id_ref, row_ref):
-    ids = id_ref[...]
-    peers, rec_count = ids.shape
-    hit = ids // rec_count == me_ref[0]
-    before = lax.broadcasted_iota(jnp.int32, (rec_count, rec_count), 0) < lax.broadcasted_iota(
-        jnp.int32, (rec_count, rec_count), 1
-    )
-    rank = jnp.dot(
-        jnp.where(hit, 1.0, 0.0).astype(jnp.bfloat16),
-        jnp.where(before, 1.0, 0.0).astype(jnp.bfloat16),
-        preferred_element_type=jnp.float32,
-    ).astype(jnp.int32)
-    local = (ids % rec_count + 1).astype(jnp.float32)
-    slots = row_ref.shape[1]
-    slot = lax.broadcasted_iota(jnp.int32, (1, slots), 1)
-    peer = lax.broadcasted_iota(jnp.int32, (peers, slots), 0)
-    label = jnp.zeros((peers, slots), jnp.float32)
-    for j in range(capacity):
-        value = jnp.sum(jnp.where(hit & (rank == j), local, 0.0), axis=1, keepdims=True)
-        label = jnp.where(slot == peer * capacity + j, value, label)
-    label = jnp.sum(label, axis=0, keepdims=True).astype(jnp.int32) - 1
-    row = label % NWIN * (rec_count // NWIN) + label // NWIN
-    row_ref[...] = jnp.where(label >= 0, row, -1)
-
-
-def arrival_rows(all_ids, capacity):
-    peers = all_ids.shape[0]
-    me = lax.axis_index("blk").astype(jnp.int32).reshape(1)
-    return pl.pallas_call(
-        functools.partial(rows_kernel, capacity),
-        in_specs=[pl.BlockSpec(memory_space=pltpu.SMEM), pl.BlockSpec(memory_space=pltpu.VMEM)],
-        out_shape=jax.ShapeDtypeStruct((1, peers * capacity), jnp.int32),
-        name="rows",
-    )(me, all_ids)
-
-
-def place_kernel(row_ref, arrived_ref, out_ref):
-    want = lax.broadcasted_iota(jnp.int32, (out_ref.shape[0], row_ref.shape[1]), 0)
-    pick = jnp.where(want == row_ref[...], 1.0, 0.0).astype(jnp.bfloat16)
-    out_ref[...] = jnp.dot(pick, arrived_ref[...], preferred_element_type=jnp.float32).astype(
-        jnp.bfloat16
-    )
-
-
-def place(rows, arrived, rec_count):
+def place_kernel(arrived_ref, out_ref):
+    rec_count = out_ref.shape[0]
+    rows = arrived_ref.shape[0]
+    labels = arrived_ref[:, PACK * 2 * F :].astype(jnp.float32).T.astype(jnp.int32) - 1
+    want = lax.broadcasted_iota(jnp.int32, (rec_count, rows), 0)
+    total = None
+    for q in range(PACK):
+        label = labels[q : q + 1, :]
+        row = jnp.where(label >= 0, label % NWIN * (rec_count // NWIN) + label // NWIN, -1)
+        pick = jnp.where(want == row, 1.0, 0.0).astype(jnp.bfloat16)
+        part = jnp.dot(
+            pick,
+            arrived_ref[:, q * 2 * F : (q + 1) * 2 * F],
+            preferred_element_type=jnp.float32,
+        )
+        total = part if q == 0 else total + part
+    out_ref[...] = total.astype(jnp.bfloat16)
+
+
+def place(arrived, rec_count):
     return pl.pallas_call(
         place_kernel,
         out_shape=jax.ShapeDtypeStruct((rec_count, 2 * F), jnp.bfloat16),
         compiler_params=pltpu.CompilerParams(vmem_limit_bytes=8 * MIB),
         name="place",
-    )(rows, arrived)
+    )(arrived)
 
 
 def correlate_kernel(hop_index, group, *refs):
@@ -269,20 +262,13 @@
     peers = lax.axis_size("blk")
     capacity = 2 * rec_count // peers
     slots = peers * capacity
-    outgoing = spectra(traces, record_id, capacity, slots).reshape(peers, capacity, 2 * F)
-    outgoing, ids = lax.optimization_barrier((outgoing, record_id))
-    arrived = lax.all_to_all(outgoing, "blk", split_axis=0, concat_axis=0, tiled=True)
-    all_ids = lax.all_to_all(
-        jnp.broadcast_to(ids[None, None], (peers, 1, rec_count)),
-        "blk",
-        split_axis=0,
-        concat_axis=0,
-        tiled=True,
-    ).reshape(peers, rec_count)
-    arrived, rows, inverse = lax.optimization_barrier(
-        (arrived, arrival_rows(all_ids, capacity), inverse_table())
+    outgoing = spectra(traces, record_id, capacity, slots)
+    width = outgoing.shape[1]
+    arrived = lax.all_to_all(
+        outgoing.reshape(peers, capacity // PACK, width), "blk", split_axis=0, concat_axis=0, tiled=True
     )
-    own = place(rows, arrived.reshape(slots, 2 * F), rec_count)
+    arrived, inverse = lax.optimization_barrier((arrived, inverse_table()))
+    own = place(arrived.reshape(slots // PACK, width), rec_count)
 
     odd = lax.axis_index("blk") % 2
     near_hop, far_hop = 1 + 2 * odd, 3 - 2 * odd

time: 94.6 us -> 84.5 us (0.89)
  blocking collectives: 13.7 us -> 0 us
  starting transfers between devices: 9.15 us -> 13.1 us
  waiting for transfers between devices: 20 us -> 23 us
  Pallas kernels: 45.3 us -> 43.4 us
  local copies, waits for them, and re-layouts: 1.27 us -> 0.01 us
    all_to_all x1 -> x0, blocking collectives: 13.7 us -> none  [on_device(): lax.all_to_all(jnp.broadcast_to(ids[None, None], (peers, 1, rec_count)),...]
    all_to_all x1, starting transfers between devices: 3.66 us -> 7.39 us  [on_device(): lax.all_to_all(outgoing.reshape(peers, capacity // PACK, width), 'blk', s...]
    all_to_all x1, waiting for transfers between devices: 15.8 us -> 18.8 us  [on_device(): lax.all_to_all(outgoing.reshape(peers, capacity // PACK, width), 'blk', s...]
    pallas_call x1 -> x0, Pallas kernels: 1.71 us -> none  [arrival_rows(): pl.pallas_call(functools.partial(rows_kernel, capacity), in_specs=[pl.Blo...]
    unnamed x7 -> x2, local copies, waits for them, and re-layouts: 1.26 us -> 0.01 us
  transfers between devices with their start and end apart: 4 -> 4, of which waited for: 2 -> 2; matrix products, arithmetic and copies ran while one was open for 6% -> 6% of each run, Pallas kernels for 25% -> 26%
where the time goes in v3:
time: 84.5 us; the launch traced here: 84.2 us
  Pallas kernels  43.4 us (51%)
  waiting for transfers between devices  23 us (27%)
  starting transfers between devices  13.1 us (16%)
  other arithmetic  4.72 us (6%)
    pallas_call x4, Pallas kernels, correlate(): pl.pallas_call(functools.partial(correlate_kernel, hop if isinstance(hop,...  29.7 us
    all_to_all x1, waiting for transfers between devices, on_device(): lax.all_to_all(outgoing.reshape(peers, capacity // PACK, width), 'blk', s...  18.8 us
    pallas_call x1, Pallas kernels, spectra(): pl.pallas_call(functools.partial(spectrum_kernel, capacity), grid=(STEPS,...  13 us
    all_to_all x1, starting transfers between devices, on_device(): lax.all_to_all(outgoing.reshape(peers, capacity // PACK, width), 'blk', s...  7.39 us
    ppermute x3, starting transfers between devices, moved(): lax.ppermute(block, 'blk', [(source_of(i) % count, i) for i in range(coun...  5.69 us
    convert_element_type x1, other arithmetic, inverse_table(): (-jnp.sin(angles)).astype(jnp.bfloat16)  4.72 us
    ppermute x3, waiting for transfers between devices, moved(): lax.ppermute(block, 'blk', [(source_of(i) % count, i) for i in range(coun...  4.21 us
  transfers between devices with their start and end apart: 4, of which 2 were waited for; matrix products, arithmetic and copies ran while one was open for 6% of the time, Pallas kernels for 26%

profile of v3, /device:TPU:0, one launch (start us, length us, event | category | flops | bytes accessed | tf_op | source)
XLA Modules:
  0.0 84.2 jit_solution(2222856142759909513)
XLA Ops:
  0.0 0.0 copy-start
  0.0 13.0 %spectra.1 = bf16[128,4224]{1,0:T(8,128)(2,1)} custom-call(s32[1,256]{1,0:T(1,128)} %bitcast.10, bf16[12000,256]{1,0:T(8,128)(2,1)} %bitcast.7, bf16[12000,256]{1,0:T(8,128)(2,1)} %bitcast.8, bf16[5,1024,1200]{2,1,0:T(8,128)(2,1)} %constant.46.clone.table_ref), custom_call_target="tpu_custom_call" | custom-call | flops 6291456000 | bytes 18432000 | tf_op jit(solution)/shard_map/spectra/pallas_call | solution.py:107
  13.0 7.4 %all-to-all-start = ((bf16[16,8,4224]{2,1,0:T(8,128)(2,1)}), bf16[16,8,4224]{2,1,0:T(8,128)(2,1)S(1)}, u32[]{:S(2)}, u32[]{:S(2)}) async-start(bf16[16,8,4224]{2,1,0:T(8,128)(2,1)} %bitcast.9), calls=%async_computation | async-start | bytes 2162688 | tf_op jit(solution)/shard_map/all_to_all | solution.py:267
  20.4 0.0 copy-done
  20.4 4.7 %negate_convert_fusion = (bf16[512,512]{1,0:T(8,128)(2,1)S(1)}, bf16[512,512]{1,0:T(8,128)(2,1)S(1)}) fusion(s32[512]{0:T(512)S(1)} %iota_add_fusion, s32[512]{0:T(512)S(1)} %copy-done), kind=kLoop, calls=%fused_computation.3 | loop fusion | flops 3145728 | bytes 1052672 | tf_op jit(solution)/shard_map/convert_element_type | solution.py:40
  25.1 18.8 %all-to-all-done = bf16[16,8,4224]{2,1,0:T(8,128)(2,1)S(1)} async-done(((bf16[16,8,4224]{2,1,0:T(8,128)(2,1)}), bf16[16,8,4224]{2,1,0:T(8,128)(2,1)S(1)}, u32[]{:S(2)}, u32[]{:S(2)}) %all-to-all-start) | async-done | bytes 1081376 | tf_op jit(solution)/shard_map/all_to_all | solution.py:267
  43.9 0.8 place.1.refs_1_.refs_2_
  44.7 5.7 %collective-permute-start = (bf16[256,1024]{1,0:T(8,128)(2,1)S(1)}, bf16[256,1024]{1,0:T(8,128)(2,1)S(1)}, u32[]{:S(2)}, u32[]{:S(2)}) collective-permute-start(bf16[256,1024]{1,0:T(8,128)(2,1)S(1)} %place.1.refs_1_.refs_2_), channel_id=1, source_target_pairs={{2,0},{3,1},{4,2},{5,3},{6,4},{7,5},{8,6},{9,7},{10,8},{11,9},{12,... | collective-permute-start | bytes 1572872 | tf_op jit(solution)/shard_map/ppermute | solution.py:32
  50.4 0.0 collective-permute-start.2
  50.4 7.4 %correlate.4.refs_5_ = bf16[32,4,32,801]{3,2,1,0:T(8,128)(2,1)} custom-call(s32[1]{0:T(128)} %constant.44.clone.1.refs_0_, bf16[256,1024]{1,0:T(8,128)(2,1)S(1)} %place.1.refs_1_.refs_2_, bf16[256,1024]{1,0:T(8,128)(2,1)S(1)} %place.1.refs_1_.refs_2_, bf16[512,512]{1,0:T(8,128)(2,1)S(1)} %get-tuple-element.15.refs_3_, ...), custom_call_target="tpu_custom_call" | custom-call | flops 3359637504 | bytes 1640448 | tf_op jit(solution)/shard_map/correlate/pallas_call | solution.py:237
  57.8 4.2 %collective-permute-done.refs_2_ = bf16[256,1024]{1,0:T(8,128)(2,1)S(1)} collective-permute-done((bf16[256,1024]{1,0:T(8,128)(2,1)S(1)}, bf16[256,1024]{1,0:T(8,128)(2,1)S(1)}, u32[]{:S(2)}, u32[]{:S(2)}) %collective-permute-start) | collective-permute-done | bytes 524320 | tf_op jit(solution)/shard_map/ppermute | solution.py:32
  62.0 0.0 collective-permute-start.1
  62.0 7.4 %correlate.5.refs_5_ = bf16[32,4,32,801]{3,2,1,0:T(8,128)(2,1)} custom-call(s32[1]{0:T(128)} %constant.45.clone.1.refs_0_, bf16[256,1024]{1,0:T(8,128)(2,1)S(1)} %place.1.refs_1_.refs_2_, bf16[256,1024]{1,0:T(8,128)(2,1)S(1)} %collective-permute-done.refs_2_, bf16[512,512]{1,0:T(8,128)(2,1)S(1)} %get-tuple-element.15.refs_3_, ...), custom_call_target="tpu_custom_call", output_to_operand_aliasing={{}: (5, {})} | custom-call | flops 3359637504 | bytes 1640448 | tf_op jit(solution)/shard_map/correlate/pallas_call | solution.py:237
  69.4 0.0 collective-permute-done.2.refs_2_
  69.4 7.4 %correlate.6.refs_5_ = bf16[32,4,32,801]{3,2,1,0:T(8,128)(2,1)} custom-call(s32[1]{0:T(128)} %bitcast.5.refs_0_, bf16[256,1024]{1,0:T(8,128)(2,1)S(1)} %place.1.refs_1_.refs_2_, bf16[256,1024]{1,0:T(8,128)(2,1)S(1)} %collective-permute-done.2.refs_2_, bf16[512,512]{1,0:T(8,128)(2,1)S(1)} %get-tuple-element.15.refs_3_, ...), custom_call_target="tpu_custom_call", output_to_operand_aliasing={{}: (5, {})} | custom-call | flops 3359637504 | bytes 1640448 | tf_op jit(solution)/shard_map/correlate/pallas_call | solution.py:237
  76.8 0.0 collective-permute-done.1.refs_2_
  76.8 7.4 %correlate.7 = bf16[32,4,32,801]{3,2,1,0:T(8,128)(2,1)} custom-call(s32[1]{0:T(128)} %bitcast.refs_0_, bf16[256,1024]{1,0:T(8,128)(2,1)S(1)} %place.1.refs_1_.refs_2_, bf16[256,1024]{1,0:T(8,128)(2,1)S(1)} %collective-permute-done.1.refs_2_, bf16[512,512]{1,0:T(8,128)(2,1)S(1)} %get-tuple-element.15.refs_3_, ...), custom_call_target="tpu_custom_call", output_to_operand_aliasing={{}: (5, {})} | custom-call | flops 3359637504 | bytes 1640448 | tf_op jit(solution)/shard_map/correlate/pallas_call | solution.py:237
  (1 shorter events, 0.0 us)
Async XLA Ops:
  0.0 20.4 %copy-start = (s32[512]{0:T(512)S(1)}, s32[512]{0:T(512)}, u32[]{:S(2)}) copy-start(s32[512]{0:T(512)} %constant.47.clone) | copy-start | bytes 6148
  13.0 30.9 %all-to-all-start = ((bf16[16,8,4224]{2,1,0:T(8,128)(2,1)}), bf16[16,8,4224]{2,1,0:T(8,128)(2,1)S(1)}, u32[]{:S(2)}, u32[]{:S(2)}) async-start(bf16[16,8,4224]{2,1,0:T(8,128)(2,1)} %bitcast.9), calls=%async_computation | async-start | bytes 2162688 | tf_op jit(solution)/shard_map/all_to_all | solution.py:267
  44.7 17.3 %collective-permute-start = (bf16[256,1024]{1,0:T(8,128)(2,1)S(1)}, bf16[256,1024]{1,0:T(8,128)(2,1)S(1)}, u32[]{:S(2)}, u32[]{:S(2)}) collective-permute-start(bf16[256,1024]{1,0:T(8,128)(2,1)S(1)} %place.1.refs_1_.refs_2_), channel_id=1, source_target_pairs={{2,0},{3,1},{4,2},{5,3},{6,4},{7,5},{8,6},{9,7},{10,8},{11,9},{12,... | collective-permute-start | bytes 1572872 | tf_op jit(solution)/shard_map/ppermute | solution.py:32
  50.4 19.1 %collective-permute-start.2 = (bf16[256,1024]{1,0:T(8,128)(2,1)S(1)}, bf16[256,1024]{1,0:T(8,128)(2,1)S(1)}, u32[]{:S(2)}, u32[]{:S(2)}) collective-permute-start(bf16[256,1024]{1,0:T(8,128)(2,1)S(1)} %place.1.refs_1_.refs_2_), channel_id=1, source_target_pairs={{1,0},{4,1},{3,2},{6,3},{5,4},{8,5},{7,6},{10,7},{9,8},{12,9},{11,... | collective-permute-start | bytes 1572872 | tf_op jit(solution)/shard_map/ppermute | solution.py:32
  62.0 14.8 %collective-permute-start.1 = (bf16[256,1024]{1,0:T(8,128)(2,1)S(1)}, bf16[256,1024]{1,0:T(8,128)(2,1)S(1)}, u32[]{:S(2)}, u32[]{:S(2)}) collective-permute-start(bf16[256,1024]{1,0:T(8,128)(2,1)S(1)} %collective-permute-done.refs_2_), channel_id=1, source_target_pairs={{1,0},{0,1},{3,2},{2,3},{5,4},{4,5},{7,6},{6,7},{9,8},{8,9},{11,10... | collective-permute-start | bytes 1572872 | tf_op jit(solution)/shard_map/ppermute | solution.py:32

commit v4 on v3

v4 whole, which is shorter than its diff:
```python
import functools
import math

import jax
import jax.numpy as jnp
import numpy as np
from jax import lax
from jax.experimental import pallas as pl
from jax.experimental.pallas import tpu as pltpu
from jax.sharding import PartitionSpec as P

NWIN = 8
WS = 12000
F = 512
LOWBIN = 60
LAG = 400
HOPS = 3
NLAG = 2 * LAG + 1
QUARTER = WS // 4
ENDS = (512, 1536, QUARTER)
PADDED = -(-QUARTER // 128) * 128
PLUS = 384
LANES = 512
FOURTH = F // 4
BINS = np.concatenate([LOWBIN + np.arange((m - LOWBIN) % 4, F, 4) for m in (0, 2, 1, 3)])
PACK = 4
TAIL = 128
MIB = 1024 * 1024


def moved(block, source_of):
    count = lax.axis_size("blk")
    return lax.ppermute(block, "blk", [(source_of(i) % count, i) for i in range(count)])


def inverse_table():
    bin_index = jnp.asarray(BINS, jnp.int32)[:, None]
    lag_index = jnp.arange(LANES, dtype=jnp.int32)[None, :] - (LAG - PLUS) + WS
    residue = (bin_index * lag_index % WS).astype(jnp.float32)
    angles = 2.0 * math.pi / WS * residue
    return jnp.cos(angles).astype(jnp.bfloat16), (-jnp.sin(angles)).astype(jnp.bfloat16)


def forward_table():
    angles = 2.0 * np.pi / WS * (BINS[:, None] * np.arange(QUARTER)[None, :] % WS)
    even, odd = np.split(angles, 2)
    table = np.zeros((2 * F, PADDED), np.float32)
    table[:, :QUARTER] = np.concatenate([np.cos(even), -np.sin(even), np.cos(odd), -np.sin(odd)])
    return table.astype(jnp.bfloat16)


def spectrum_kernel(capacity, id_ref, x_ref, table_ref, out_ref, samples, table, even, odd, sems):
    begins = (0,) + ENDS[:-1]
    copies = []
    for c, (begin, end) in enumerate(zip(begins, ENDS)):
        lanes = slice(begin, end if end < QUARTER else PADDED)
        pairs = [(table_ref.at[:, lanes], table.at[:, lanes])]
        for j in range(4):
            source = x_ref.at[j * QUARTER + begin : j * QUARTER + end, :]
            pairs.append((source, samples.at[j, begin:end, :]))
        copies.append(
            [pltpu.make_async_copy(a, b, sems.at[c, i]) for i, (a, b) in enumerate(pairs)]
        )
    for group in copies:
        for copy in group:
            copy.start()
    for group, begin, end in zip(copies, begins, ENDS):
        for copy in group:
            copy.wait()
        for turn, total in enumerate((even, odd)):
            rows = slice(turn * F, (turn + 1) * F)
            parts = [
                jnp.dot(
                    table[rows, begin:end],
                    samples[j, begin:end, :],
                    preferred_element_type=jnp.float32,
                )
                for j in range(4)
            ]
            if turn == 0:
                straight, across = parts[0] + parts[2], parts[1] + parts[3]
                signs, order = (1, -1, 1, -1), (0, 1, 2, 3)
            else:
                straight, across = parts[0] - parts[2], parts[1] - parts[3]
                signs, order = (1, -1, -1, 1), (2, 3, 0, 1)
            for block in range(4):
                mine = slice(block * FOURTH, (block + 1) * FOURTH)
                theirs = slice(order[block] * FOURTH, (order[block] + 1) * FOURTH)
                both = straight[mine] + across[theirs] if signs[block] > 0 else straight[mine] - across[theirs]
                total[mine, :] = both if begin == 0 else total[mine, :] + both

    rec_count = id_ref.shape[1]
    ids = id_ref[...]
    owner = ids // rec_count
    row = jnp.broadcast_to(owner, (rec_count, rec_count))
    before = lax.broadcasted_iota(jnp.int32, row.shape, 0) < lax.broadcasted_iota(
        jnp.int32, row.shape, 1
    )
    rank = jnp.sum(jnp.where((row == row.T) & before, 1, 0), axis=0, keepdims=True)
    target = owner * capacity + rank
    label = (ids % rec_count + 1).astype(jnp.float32)
    power = jnp.sum(even[...] * even[...], axis=0, keepdims=True)
    power = (power + jnp.sum(odd[...] * odd[...], axis=0, keepdims=True)) / F
    scale = lax.rsqrt(power + 1e-06)
    half = F // 2
    rows = out_ref.shape[0]
    slot = lax.broadcasted_iota(jnp.int32, (rows, rec_count), 0) * PACK
    lane = lax.broadcasted_iota(jnp.int32, (rows, TAIL), 1)
    labels = jnp.zeros((rows, TAIL), jnp.float32)
    picks = []
    for q in range(PACK):
        hit = slot + q == target
        labels = jnp.where(
            lane == q, jnp.sum(jnp.where(hit, label, 0.0), axis=1, keepdims=True), labels
        )
        picks.append(jnp.where(hit, 1.0, 0.0).astype(jnp.bfloat16))
    pick = jnp.concatenate(picks)
    for place, (part, base) in enumerate(((even, 0), (odd, 0), (even, half), (odd, half))):
        white = (part[base : base + half, :] * scale).astype(jnp.bfloat16)
        moved = lax.dot_general(
            pick, white, (((1,), (1,)), ((), ())), preferred_element_type=jnp.float32
        ).astype(jnp.bfloat16)
        for q in range(PACK):
            lanes = slice(q * 2 * F + place * half, q * 2 * F + (place + 1) * half)
            out_ref[:, lanes] = moved[q * rows : (q + 1) * rows]
    out_ref[:, PACK * 2 * F :] = labels.astype(jnp.bfloat16)


def spectra(traces, record_id, capacity, slots):
    rec_count = traces.shape[0]
    shape = (slots // PACK, PACK * 2 * F + TAIL)
    return pl.pallas_call(
        functools.partial(spectrum_kernel, capacity),
        in_specs=[
            pl.BlockSpec(memory_space=pltpu.VMEM),
            pl.BlockSpec(memory_space=pl.ANY),
            pl.BlockSpec(memory_space=pl.ANY),
        ],
        out_specs=pl.BlockSpec(memory_space=pltpu.VMEM),
        out_shape=jax.ShapeDtypeStruct(shape, jnp.bfloat16),
        scratch_shapes=[
            pltpu.VMEM((4, QUARTER, rec_count), jnp.bfloat16),
            pltpu.VMEM((2 * F, PADDED), jnp.bfloat16),
            pltpu.VMEM((F, rec_count), jnp.float32),
            pltpu.VMEM((F, rec_count), jnp.float32),
            pltpu.SemaphoreType.DMA((len(ENDS), 5)),
        ],
        compiler_params=pltpu.CompilerParams(vmem_limit_bytes=56 * MIB),
        cost_estimate=pl.CostEstimate(
            flops=4 * rec_count * WS * F, bytes_accessed=2 * WS * (rec_count + F), transcendentals=0
        ),
        name="spectra",
    )(record_id.reshape(1, rec_count), traces.T, jnp.asarray(forward_table()))


def place_kernel(arrived_ref, out_ref):
    rec_count = out_ref.shape[0]
    rows = arrived_ref.shape[0]
    labels = arrived_ref[:, PACK * 2 * F :].astype(jnp.float32).T.astype(jnp.int32) - 1
    want = lax.broadcasted_iota(jnp.int32, (rec_count, rows), 0)
    total = None
    for q in range(PACK):
        label = labels[q : q + 1, :]
        row = jnp.where(label >= 0, label % NWIN * (rec_count // NWIN) + label // NWIN, -1)
        pick = jnp.where(want == row, 1.0, 0.0).astype(jnp.bfloat16)
        part = jnp.dot(
            pick,
            arrived_ref[:, q * 2 * F : (q + 1) * 2 * F],
            preferred_element_type=jnp.float32,
        )
        total = part if q == 0 else total + part
    out_ref[...] = total.astype(jnp.bfloat16)


def place(arrived, rec_count):
    return pl.pallas_call(
        place_kernel,
        out_shape=jax.ShapeDtypeStruct((rec_count, 2 * F), jnp.bfloat16),
        compiler_params=pltpu.CompilerParams(vmem_limit_bytes=8 * MIB),
        name="place",
    )(arrived)


def correlate_kernel(hop_index, group, batch, *refs):
    hop_ref, own_ref, other_ref, cos_ref, sin_ref = refs[:5]
    out_ref, mine, theirs, cross, done, sems = refs[-6:]
    width = own_ref.shape[0] // NWIN
    for w in range(NWIN):
        rows = slice(w * width, (w + 1) * width)
        real = own_ref[rows, :F].astype(jnp.float32)
        imag = own_ref[rows, F:].astype(jnp.float32)
        mine[0, rows, :] = real + imag
        mine[1, rows, :] = real
        mine[2, rows, :] = imag
        real = other_ref[rows, :F].astype(jnp.float32)
        imag = other_ref[rows, F:].astype(jnp.float32)
        theirs[0, rows, :] = real
        theirs[1, rows, :] = real + imag
        theirs[2, rows, :] = real - imag

    def channels_from(step, carry):
        blocks = [
            pl.ds(pl.multiple_of(w * width + step * group, group), group) for w in range(NWIN)
        ]
        for tile in range(F // 128):
            lanes = slice(tile * 128, (tile + 1) * 128)
            for first in range(0, group, 2):
                total = [[None] * 3 for _ in range(2)]
                for w in range(NWIN):
                    for j in range(3):
                        factor = theirs[j, w * width : (w + 1) * width, lanes]
                        rows = mine.at[j, blocks[w], lanes]
                        for c in range(2):
                            term = factor * rows[first + c : first + c + 1, :]
                            total[c][j] = term if w == 0 else total[c][j] + term
                for c in range(2):
                    rows = pl.ds(
                        pl.multiple_of((step * group + first + c) * width, width), width
                    )
                    cross[rows, tile * 128 : (tile + 1) * 128] = (
                        total[c][0] - total[c][2]
                    ).astype(jnp.bfloat16)
                    cross[rows, F + tile * 128 : F + (tile + 1) * 128] = (
                        total[c][0] - total[c][1]
                    ).astype(jnp.bfloat16)
        return carry

    lax.fori_loop(0, width // group, channels_from, 0)
    unit = 1.0 / math.sqrt(F * NWIN)
    copies = []
    for step in range(width // batch):
        mine_rows = slice(step * batch * width, (step + 1) * batch * width)
        even = jnp.dot(cross[mine_rows, :F], cos_ref[...], preferred_element_type=jnp.float32)
        uneven = jnp.dot(cross[mine_rows, F:], sin_ref[...], preferred_element_type=jnp.float32)
        later = (even + uneven) * unit
        earlier = (even - uneven) * unit
        lane = lax.broadcasted_iota(jnp.int32, (batch * width, 128), 1)
        last = (2 * LAG - PLUS) % 128
        mirror = (last - lane) & 127
        turned = [
            jnp.take_along_axis(earlier[:, q * 128 : (q + 1) * 128], mirror, axis=1)
            for q in range(LANES // 128)
        ]
        top = (2 * LAG - PLUS) // 128
        pieces = [
            jnp.where(lane <= last, turned[top - t], turned[top - 1 - t]) for t in range(PLUS // 128)
        ]
        lagged = jnp.concatenate(pieces + [later[:, : NLAG - PLUS]], axis=1)
        lagged = lagged.reshape(batch, width, NLAG)
        if hop_index == 0:
            channel = lax.broadcasted_iota(jnp.int32, lagged.shape, 0) + step * batch
            partner = lax.broadcasted_iota(jnp.int32, lagged.shape, 1)
            lagged = jnp.where(channel == partner, 0.0, lagged)
        channels = slice(step * batch, (step + 1) * batch)
        done[channels] = lagged.astype(jnp.bfloat16)
        copy = pltpu.make_async_copy(
            done.at[channels], out_ref.at[channels, hop_ref[0]], sems.at[step]
        )
        copy.start()
        copies.append(copy)
    for copy in copies:
        copy.wait()


def correlate(own, other, inverse, hop, result):
    rec_count = own.shape[0]
    width = rec_count // NWIN
    group, batch = 8, 8
    operands = [jnp.asarray(hop, jnp.int32).reshape(1), own, other, *inverse]
    in_specs = [pl.BlockSpec(memory_space=pltpu.SMEM)]
    in_specs += [pl.BlockSpec(memory_space=pltpu.VMEM)] * 4
    aliases = {}
    if result is not None:
        in_specs.append(pl.BlockSpec(memory_space=pl.ANY))
        operands.append(result)
        aliases = {5: 0}
    pairs = width * width
    return pl.pallas_call(
        functools.partial(correlate_kernel, hop if isinstance(hop, int) else None, group, batch),
        in_specs=in_specs,
        out_specs=pl.BlockSpec(memory_space=pl.ANY),
        out_shape=jax.ShapeDtypeStruct((width, HOPS + 1, width, NLAG), jnp.bfloat16),
        scratch_shapes=[
            pltpu.VMEM((3, rec_count, F), jnp.float32),
            pltpu.VMEM((3, rec_count, F), jnp.float32),
            pltpu.VMEM((width * width, 2 * F), jnp.bfloat16),
            pltpu.VMEM((width, width, NLAG), jnp.bfloat16),
            pltpu.SemaphoreType.DMA((width // batch,)),
        ],
        input_output_aliases=aliases,
        compiler_params=pltpu.CompilerParams(vmem_limit_bytes=24 * MIB),
        cost_estimate=pl.CostEstimate(
            flops=pairs * 2 * F * NLAG * 4, bytes_accessed=pairs * NLAG * 2, transcendentals=0
        ),
        name="correlate",
    )(*operands)


def on_device(traces, record_id):
    rec_count = traces.shape[0]
    peers = lax.axis_size("blk")
    capacity = 2 * rec_count // peers
    slots = peers * capacity
    outgoing = spectra(traces, record_id, capacity, slots)
    width = outgoing.shape[1]
    arrived = lax.all_to_all(
        outgoing.reshape(peers, capacity // PACK, width), "blk", split_axis=0, concat_axis=0, tiled=True
    )
    arrived, inverse = lax.optimization_barrier((arrived, inverse_table()))
    own = place(arrived.reshape(slots // PACK, width), rec_count)

    odd = lax.axis_index("blk") % 2
    near_hop, far_hop = 1 + 2 * odd, 3 - 2 * odd
    ahead = moved(own, lambda i: i + 2)
    result = correlate(own, own, inverse, 0, None)
    own_again, result = lax.optimization_barrier((own, result))
    near = moved(own_again, lambda i: i + 3 if i % 2 else i + 1)
    ahead, result = lax.optimization_barrier((ahead, result))
    far = moved(ahead, lambda i: i ^ 1)
    result = correlate(own, ahead, inverse, 2, result)
    near, result = lax.optimization_barrier((near, result))
    result = correlate(own, near, inverse, near_hop, result)
    far, result = lax.optimization_barrier((far, result))
    return correlate(own, far, inverse, far_hop, result)


def solution(mesh):
    return jax.shard_map(
        on_device,
        mesh=mesh,
        in_specs=(P(("groups", "blk"), None), P(("groups", "blk"))),
        out_specs=P(("groups", "blk"), None, None, None),
        check_vma=False,
    )
```

time: 84.5 us -> 80.2 us (0.949)
  Pallas kernels: 43.4 us -> 38.1 us
    pallas_call x4, Pallas kernels: 29.7 us -> 26.3 us  [correlate(): pl.pallas_call(functools.partial(correlate_kernel, hop if isinstance(hop,...]
    pallas_call x1, Pallas kernels: 13 us -> 11 us  [spectra(): pl.pallas_call(functools.partial(spectrum_kernel, capacity), in_specs=[pl...]
  transfers between devices with their start and end apart: 4 -> 4, of which waited for: 2 -> 2; matrix products, arithmetic and copies ran while one was open for 6% -> 6% of each run, Pallas kernels for 26% -> 25%
where the time goes in v4:
time: 80.2 us; the launch traced here: 79.9 us
  Pallas kernels  38.1 us (48%)
  waiting for transfers between devices  23.5 us (29%)
  starting transfers between devices  13.3 us (17%)
  other arithmetic  4.72 us (6%)
    pallas_call x4, Pallas kernels, correlate(): pl.pallas_call(functools.partial(correlate_kernel, hop if isinstance(hop,...  26.3 us
    all_to_all x1, waiting for transfers between devices, on_device(): lax.all_to_all(outgoing.reshape(peers, capacity // PACK, width), 'blk', s...  18.8 us
    pallas_call x1, Pallas kernels, spectra(): pl.pallas_call(functools.partial(spectrum_kernel, capacity), in_specs=[pl...  11 us
    all_to_all x1, starting transfers between devices, on_device(): lax.all_to_all(outgoing.reshape(peers, capacity // PACK, width), 'blk', s...  7.41 us
    ppermute x3, starting transfers between devices, moved(): lax.ppermute(block, 'blk', [(source_of(i) % count, i) for i in range(coun...  5.92 us
    ppermute x3, waiting for transfers between devices, moved(): lax.ppermute(block, 'blk', [(source_of(i) % count, i) for i in range(coun...  4.75 us
    convert_element_type x1, other arithmetic, inverse_table(): (-jnp.sin(angles)).astype(jnp.bfloat16)  4.72 us
  transfers between devices with their start and end apart: 4, of which 2 were waited for; matrix products, arithmetic and copies ran while one was open for 6% of the time, Pallas kernels for 25%

profile of v4, /device:TPU:0, one launch (start us, length us, event | category | flops | bytes accessed | tf_op | source)
XLA Modules:
  0.0 79.9 jit_solution(17447711539316154543)
XLA Ops:
  0.0 0.0 copy-start
  0.0 11.0 %spectra.1 = bf16[128,4224]{1,0:T(8,128)(2,1)} custom-call(s32[1,256]{1,0:T(1,128)} %bitcast.9, bf16[12000,256]{1,0:T(8,128)(2,1)} %bitcast.8, bf16[1024,3072]{1,0:T(8,128)(2,1)} %constant.46.clone.table_ref), custom_call_target="tpu_custom_call" | custom-call | flops 6291456000 | bytes 18432000 | tf_op jit(solution)/shard_map/spectra/pallas_call | solution.py:132
  11.0 7.4 %all-to-all-start = ((bf16[16,8,4224]{2,1,0:T(8,128)(2,1)}), bf16[16,8,4224]{2,1,0:T(8,128)(2,1)S(1)}, u32[]{:S(2)}, u32[]{:S(2)}) async-start(bf16[16,8,4224]{2,1,0:T(8,128)(2,1)} %bitcast.7), calls=%async_computation | async-start | bytes 2162688 | tf_op jit(solution)/shard_map/all_to_all | solution.py:306
  18.4 0.0 copy-done
  18.4 4.7 %negate_convert_fusion = (bf16[512,512]{1,0:T(8,128)(2,1)S(1)}, bf16[512,512]{1,0:T(8,128)(2,1)S(1)}) fusion(s32[512]{0:T(512)S(1)} %iota_add_fusion, s32[512]{0:T(512)S(1)} %copy-done), kind=kLoop, calls=%fused_computation.3 | loop fusion | flops 3145728 | bytes 1052672 | tf_op jit(solution)/shard_map/convert_element_type | solution.py:41
  23.1 18.8 %all-to-all-done = bf16[16,8,4224]{2,1,0:T(8,128)(2,1)S(1)} async-done(((bf16[16,8,4224]{2,1,0:T(8,128)(2,1)}), bf16[16,8,4224]{2,1,0:T(8,128)(2,1)S(1)}, u32[]{:S(2)}, u32[]{:S(2)}) %all-to-all-start) | async-done | bytes 1081376 | tf_op jit(solution)/shard_map/all_to_all | solution.py:306
  41.9 0.8 place.1.refs_1_.refs_2_
  42.7 5.7 %collective-permute-start = (bf16[256,1024]{1,0:T(8,128)(2,1)S(1)}, bf16[256,1024]{1,0:T(8,128)(2,1)S(1)}, u32[]{:S(2)}, u32[]{:S(2)}) collective-permute-start(bf16[256,1024]{1,0:T(8,128)(2,1)S(1)} %place.1.refs_1_.refs_2_), channel_id=1, source_target_pairs={{2,0},{3,1},{4,2},{5,3},{6,4},{7,5},{8,6},{9,7},{10,8},{11,9},{12,... | collective-permute-start | bytes 1572872 | tf_op jit(solution)/shard_map/ppermute | solution.py:33
  48.4 6.6 %correlate.4.refs_5_ = bf16[32,4,32,801]{3,2,1,0:T(8,128)(2,1)} custom-call(s32[1]{0:T(128)} %constant.44.clone.1.refs_0_, bf16[256,1024]{1,0:T(8,128)(2,1)S(1)} %place.1.refs_1_.refs_2_, bf16[256,1024]{1,0:T(8,128)(2,1)S(1)} %place.1.refs_1_.refs_2_, bf16[512,512]{1,0:T(8,128)(2,1)S(1)} %get-tuple-element.17.refs_3_, ...), custom_call_target="tpu_custom_call" | custom-call | flops 3359637504 | bytes 1640448 | tf_op jit(solution)/shard_map/correlate/pallas_call | solution.py:278
  55.0 0.2 collective-permute-start.2
  55.3 4.7 %collective-permute-done.refs_2_ = bf16[256,1024]{1,0:T(8,128)(2,1)S(1)} collective-permute-done((bf16[256,1024]{1,0:T(8,128)(2,1)S(1)}, bf16[256,1024]{1,0:T(8,128)(2,1)S(1)}, u32[]{:S(2)}, u32[]{:S(2)}) %collective-permute-start) | collective-permute-done | bytes 524320 | tf_op jit(solution)/shard_map/ppermute | solution.py:33
  60.0 0.0 collective-permute-start.1
  60.0 6.6 %correlate.5.refs_5_ = bf16[32,4,32,801]{3,2,1,0:T(8,128)(2,1)} custom-call(s32[1]{0:T(128)} %constant.45.clone.1.refs_0_, bf16[256,1024]{1,0:T(8,128)(2,1)S(1)} %place.1.refs_1_.refs_2_, bf16[256,1024]{1,0:T(8,128)(2,1)S(1)} %collective-permute-done.refs_2_, bf16[512,512]{1,0:T(8,128)(2,1)S(1)} %get-tuple-element.17.refs_3_, ...), custom_call_target="tpu_custom_call", output_to_operand_aliasing={{}: (5, {})} | custom-call | flops 3359637504 | bytes 1640448 | tf_op jit(solution)/shard_map/correlate/pallas_call | solution.py:278
  66.6 0.0 collective-permute-done.2.refs_2_
  66.6 6.6 %correlate.6.refs_5_ = bf16[32,4,32,801]{3,2,1,0:T(8,128)(2,1)} custom-call(s32[1]{0:T(128)} %bitcast.5.refs_0_, bf16[256,1024]{1,0:T(8,128)(2,1)S(1)} %place.1.refs_1_.refs_2_, bf16[256,1024]{1,0:T(8,128)(2,1)S(1)} %collective-permute-done.2.refs_2_, bf16[512,512]{1,0:T(8,128)(2,1)S(1)} %get-tuple-element.17.refs_3_, ...), custom_call_target="tpu_custom_call", output_to_operand_aliasing={{}: (5, {})} | custom-call | flops 3359637504 | bytes 1640448 | tf_op jit(solution)/shard_map/correlate/pallas_call | solution.py:278
  73.2 0.0 collective-permute-done.1.refs_2_
  73.2 6.6 %correlate.7 = bf16[32,4,32,801]{3,2,1,0:T(8,128)(2,1)} custom-call(s32[1]{0:T(128)} %bitcast.refs_0_, bf16[256,1024]{1,0:T(8,128)(2,1)S(1)} %place.1.refs_1_.refs_2_, bf16[256,1024]{1,0:T(8,128)(2,1)S(1)} %collective-permute-done.1.refs_2_, bf16[512,512]{1,0:T(8,128)(2,1)S(1)} %get-tuple-element.17.refs_3_, ...), custom_call_target="tpu_custom_call", output_to_operand_aliasing={{}: (5, {})} | custom-call | flops 3359637504 | bytes 1640448 | tf_op jit(solution)/shard_map/correlate/pallas_call | solution.py:278
  (1 shorter events, 0.0 us)
Async XLA Ops:
  0.0 18.4 %copy-start = (s32[512]{0:T(512)S(1)}, s32[512]{0:T(512)}, u32[]{:S(2)}) copy-start(s32[512]{0:T(512)} %constant.47.clone) | copy-start | bytes 6148
  11.0 30.9 %all-to-all-start = ((bf16[16,8,4224]{2,1,0:T(8,128)(2,1)}), bf16[16,8,4224]{2,1,0:T(8,128)(2,1)S(1)}, u32[]{:S(2)}, u32[]{:S(2)}) async-start(bf16[16,8,4224]{2,1,0:T(8,128)(2,1)} %bitcast.7), calls=%async_computation | async-start | bytes 2162688 | tf_op jit(solution)/shard_map/all_to_all | solution.py:306
  42.7 17.3 %collective-permute-start = (bf16[256,1024]{1,0:T(8,128)(2,1)S(1)}, bf16[256,1024]{1,0:T(8,128)(2,1)S(1)}, u32[]{:S(2)}, u32[]{:S(2)}) collective-permute-start(bf16[256,1024]{1,0:T(8,128)(2,1)S(1)} %place.1.refs_1_.refs_2_), channel_id=1, source_target_pairs={{2,0},{3,1},{4,2},{5,3},{6,4},{7,5},{8,6},{9,7},{10,8},{11,9},{12,... | collective-permute-start | bytes 1572872 | tf_op jit(solution)/shard_map/ppermute | solution.py:33
  55.0 11.6 %collective-permute-start.2 = (bf16[256,1024]{1,0:T(8,128)(2,1)S(1)}, bf16[256,1024]{1,0:T(8,128)(2,1)S(1)}, u32[]{:S(2)}, u32[]{:S(2)}) collective-permute-start(bf16[256,1024]{1,0:T(8,128)(2,1)S(1)} %place.1.refs_1_.refs_2_), channel_id=1, source_target_pairs={{1,0},{4,1},{3,2},{6,3},{5,4},{8,5},{7,6},{10,7},{9,8},{12,9},{11,... | collective-permute-start | bytes 1572872 | tf_op jit(solution)/shard_map/ppermute | solution.py:33
  60.0 13.2 %collective-permute-start.1 = (bf16[256,1024]{1,0:T(8,128)(2,1)S(1)}, bf16[256,1024]{1,0:T(8,128)(2,1)S(1)}, u32[]{:S(2)}, u32[]{:S(2)}) collective-permute-start(bf16[256,1024]{1,0:T(8,128)(2,1)S(1)} %collective-permute-done.refs_2_), channel_id=1, source_target_pairs={{1,0},{0,1},{3,2},{2,3},{5,4},{4,5},{7,6},{6,7},{9,8},{8,9},{11,10... | collective-permute-start | bytes 1572872 | tf_op jit(solution)/shard_map/ppermute | solution.py:33

commit v5 on v4

--- a/solution.py
+++ b/solution.py
@@ -153,67 +153,91 @@
     )(record_id.reshape(1, rec_count), traces.T, jnp.asarray(forward_table()))
 
 
-def place_kernel(arrived_ref, out_ref):
+def place_kernel(arrived_ref, out_ref, *half_refs):
     rec_count = out_ref.shape[0]
     rows = arrived_ref.shape[0]
+    side = rec_count // NWIN // 2
     labels = arrived_ref[:, PACK * 2 * F :].astype(jnp.float32).T.astype(jnp.int32) - 1
     want = lax.broadcasted_iota(jnp.int32, (rec_count, rows), 0)
     total = None
     for q in range(PACK):
         label = labels[q : q + 1, :]
-        row = jnp.where(label >= 0, label % NWIN * (rec_count // NWIN) + label // NWIN, -1)
-        pick = jnp.where(want == row, 1.0, 0.0).astype(jnp.bfloat16)
+        channel, window = label // NWIN, label % NWIN
+        row = (channel // side * NWIN + window) * side + channel % side
+        pick = jnp.where(want == jnp.where(label >= 0, row, -1), 1.0, 0.0).astype(jnp.bfloat16)
         part = jnp.dot(
             pick,
             arrived_ref[:, q * 2 * F : (q + 1) * 2 * F],
             preferred_element_type=jnp.float32,
         )
         total = part if q == 0 else total + part
-    out_ref[...] = total.astype(jnp.bfloat16)
+    panel = total.astype(jnp.bfloat16)
+    out_ref[...] = panel
+    for half, ref in enumerate(half_refs):
+        ref[...] = panel[half * rec_count // 2 : (half + 1) * rec_count // 2]
 
 
 def place(arrived, rec_count):
     return pl.pallas_call(
         place_kernel,
-        out_shape=jax.ShapeDtypeStruct((rec_count, 2 * F), jnp.bfloat16),
+        out_shape=[
+            jax.ShapeDtypeStruct((rows, 2 * F), jnp.bfloat16)
+            for rows in (rec_count, rec_count // 2, rec_count // 2)
+        ],
         compiler_params=pltpu.CompilerParams(vmem_limit_bytes=8 * MIB),
         name="place",
     )(arrived)
 
 
-def correlate_kernel(hop_index, group, batch, *refs):
-    hop_ref, own_ref, other_ref, cos_ref, sin_ref = refs[:5]
+def correlate_kernel(hop_index, begin, group, batch, count, *refs):
+    hop_ref, own_ref = refs[:2]
+    other_refs = refs[2 : 2 + count]
+    cos_ref, sin_ref = refs[2 + count : 4 + count]
     out_ref, mine, theirs, cross, done, sems = refs[-6:]
-    width = own_ref.shape[0] // NWIN
+    full = own_ref.shape[0] // NWIN
+    side = full // 2
+    width = theirs.shape[1] // NWIN
+    own_blocks = [(own_ref, half * NWIN * side, half * side) for half in range(2)]
+    if other_refs[0].shape[0] == own_ref.shape[0]:
+        blocks = [(other_refs[0], half * NWIN * side, half * side) for half in range(2)]
+    else:
+        blocks = [(ref, 0, half * side) for half, ref in enumerate(other_refs)]
     for w in range(NWIN):
-        rows = slice(w * width, (w + 1) * width)
-        real = own_ref[rows, :F].astype(jnp.float32)
-        imag = own_ref[rows, F:].astype(jnp.float32)
-        mine[0, rows, :] = real + imag
-        mine[1, rows, :] = real
-        mine[2, rows, :] = imag
-        real = other_ref[rows, :F].astype(jnp.float32)
-        imag = other_ref[rows, F:].astype(jnp.float32)
-        theirs[0, rows, :] = real
-        theirs[1, rows, :] = real + imag
-        theirs[2, rows, :] = real - imag
+        for ref, base, place in own_blocks:
+            source = slice(base + w * side, base + (w + 1) * side)
+            rows = slice(w * full + place, w * full + place + side)
+            real = ref[source, :F].astype(jnp.float32)
+            imag = ref[source, F:].astype(jnp.float32)
+            mine[0, rows, :] = real + imag
+            mine[1, rows, :] = real
+            mine[2, rows, :] = imag
+        for ref, base, place in blocks:
+            source = slice(base + w * side, base + (w + 1) * side)
+            rows = slice(w * width + place, w * width + place + side)
+            real = ref[source, :F].astype(jnp.float32)
+            imag = ref[source, F:].astype(jnp.float32)
+            theirs[0, rows, :] = real
+            theirs[1, rows, :] = real + imag
+            theirs[2, rows, :] = real - imag
+
+    shared = 64 // width
 
     def channels_from(step, carry):
         blocks = [
-            pl.ds(pl.multiple_of(w * width + step * group, group), group) for w in range(NWIN)
+            pl.ds(pl.multiple_of(w * full + step * group, group), group) for w in range(NWIN)
         ]
         for tile in range(F // 128):
             lanes = slice(tile * 128, (tile + 1) * 128)
-            for first in range(0, group, 2):
-                total = [[None] * 3 for _ in range(2)]
+            for first in range(0, group, shared):
+                total = [[None] * 3 for _ in range(shared)]
                 for w in range(NWIN):
                     for j in range(3):
                         factor = theirs[j, w * width : (w + 1) * width, lanes]
                         rows = mine.at[j, blocks[w], lanes]
-                        for c in range(2):
+                        for c in range(shared):
                             term = factor * rows[first + c : first + c + 1, :]
                             total[c][j] = term if w == 0 else total[c][j] + term
-                for c in range(2):
+                for c in range(shared):
                     rows = pl.ds(
                         pl.multiple_of((step * group + first + c) * width, width), width
                     )
@@ -225,10 +249,10 @@
                     ).astype(jnp.bfloat16)
         return carry
 
-    lax.fori_loop(0, width // group, channels_from, 0)
+    lax.fori_loop(0, full // group, channels_from, 0)
     unit = 1.0 / math.sqrt(F * NWIN)
     copies = []
-    for step in range(width // batch):
+    for step in range(full // batch):
         mine_rows = slice(step * batch * width, (step + 1) * batch * width)
         even = jnp.dot(cross[mine_rows, :F], cos_ref[...], preferred_element_type=jnp.float32)
         uneven = jnp.dot(cross[mine_rows, F:], sin_ref[...], preferred_element_type=jnp.float32)
@@ -254,7 +278,9 @@
         channels = slice(step * batch, (step + 1) * batch)
         done[channels] = lagged.astype(jnp.bfloat16)
         copy = pltpu.make_async_copy(
-            done.at[channels], out_ref.at[channels, hop_ref[0]], sems.at[step]
+            done.at[channels],
+            out_ref.at[channels, hop_ref[0], begin : begin + width],
+            sems.at[step],
         )
         copy.start()
         copies.append(copy)
@@ -262,30 +288,35 @@
         copy.wait()
 
 
-def correlate(own, other, inverse, hop, result):
+def correlate(own, others, inverse, hop, result, begin=0):
     rec_count = own.shape[0]
-    width = rec_count // NWIN
-    group, batch = 8, 8
-    operands = [jnp.asarray(hop, jnp.int32).reshape(1), own, other, *inverse]
+    full = rec_count // NWIN
+    rows = sum(other.shape[0] for other in others)
+    width = rows // NWIN
+    group = 8
+    batch = 256 // width
+    operands = [jnp.asarray(hop, jnp.int32).reshape(1), own, *others, *inverse]
     in_specs = [pl.BlockSpec(memory_space=pltpu.SMEM)]
-    in_specs += [pl.BlockSpec(memory_space=pltpu.VMEM)] * 4
+    in_specs += [pl.BlockSpec(memory_space=pltpu.VMEM)] * (len(operands) - 1)
     aliases = {}
     if result is not None:
         in_specs.append(pl.BlockSpec(memory_space=pl.ANY))
+        aliases = {len(operands): 0}
         operands.append(result)
-        aliases = {5: 0}
-    pairs = width * width
+    pairs = full * width
     return pl.pallas_call(
-        functools.partial(correlate_kernel, hop if isinstance(hop, int) else None, group, batch),
+        functools.partial(
+            correlate_kernel, hop if isinstance(hop, int) else None, begin, group, batch, len(others)
+        ),
         in_specs=in_specs,
         out_specs=pl.BlockSpec(memory_space=pl.ANY),
-        out_shape=jax.ShapeDtypeStruct((width, HOPS + 1, width, NLAG), jnp.bfloat16),
+        out_shape=jax.ShapeDtypeStruct((full, HOPS + 1, full, NLAG), jnp.bfloat16),
         scratch_shapes=[
             pltpu.VMEM((3, rec_count, F), jnp.float32),
-            pltpu.VMEM((3, rec_count, F), jnp.float32),
-            pltpu.VMEM((width * width, 2 * F), jnp.bfloat16),
-            pltpu.VMEM((width, width, NLAG), jnp.bfloat16),
-            pltpu.SemaphoreType.DMA((width // batch,)),
+            pltpu.VMEM((3, rows, F), jnp.float32),
+            pltpu.VMEM((pairs, 2 * F), jnp.bfloat16),
+            pltpu.VMEM((full, width, NLAG), jnp.bfloat16),
+            pltpu.SemaphoreType.DMA((full // batch,)),
         ],
         input_output_aliases=aliases,
         compiler_params=pltpu.CompilerParams(vmem_limit_bytes=24 * MIB),
@@ -307,21 +338,28 @@
         outgoing.reshape(peers, capacity // PACK, width), "blk", split_axis=0, concat_axis=0, tiled=True
     )
     arrived, inverse = lax.optimization_barrier((arrived, inverse_table()))
-    own = place(arrived.reshape(slots // PACK, width), rec_count)
+    own, low, high = place(arrived.reshape(slots // PACK, width), rec_count)
 
     odd = lax.axis_index("blk") % 2
     near_hop, far_hop = 1 + 2 * odd, 3 - 2 * odd
-    ahead = moved(own, lambda i: i + 2)
-    result = correlate(own, own, inverse, 0, None)
-    own_again, result = lax.optimization_barrier((own, result))
-    near = moved(own_again, lambda i: i + 3 if i % 2 else i + 1)
-    ahead, result = lax.optimization_barrier((ahead, result))
-    far = moved(ahead, lambda i: i ^ 1)
-    result = correlate(own, ahead, inverse, 2, result)
-    near, result = lax.optimization_barrier((near, result))
-    result = correlate(own, near, inverse, near_hop, result)
-    far, result = lax.optimization_barrier((far, result))
-    return correlate(own, far, inverse, far_hop, result)
+    barrier = lax.optimization_barrier
+    side = rec_count // NWIN // 2
+    low = moved(low, lambda i: i + 2)
+    high = moved(high, lambda i: i + 1 if i % 2 else i + 3)
+    result = correlate(own, [own], inverse, 0, None)
+    low, result = barrier((low, result))
+    far_low = moved(low, lambda i: i ^ 1)
+    result = correlate(own, [low], inverse, 2, result)
+    again, high, result = barrier((own, high, result))
+    near = moved(again, lambda i: i + 3 if i % 2 else i + 1)
+    far_high = moved(high, lambda i: i ^ 1)
+    result = correlate(own, [high], inverse, far_hop, result, side)
+    far_low, result = barrier((far_low, result))
+    result = correlate(own, [far_low], inverse, far_hop, result)
+    near, result = barrier((near, result))
+    result = correlate(own, [near], inverse, near_hop, result)
+    far_high, result = barrier((far_high, result))
+    return correlate(own, [far_high], inverse, 2, result, side)
 
 
 def solution(mesh):

time: 80.2 us -> 80.4 us (level); the launches traced: 79.9 us -> 78.8 us
  waiting for transfers between devices: 23.5 us -> 20.2 us
  starting transfers between devices: 13.3 us -> 14.6 us
  Pallas kernels: 38.1 us -> 39 us
    ppermute x3 -> x5, waiting for transfers between devices: 4.75 us -> 1.46 us  [moved(): lax.ppermute(block, 'blk', [(source_of(i) % count, i) for i in range(coun...]
    ppermute x3 -> x5, starting transfers between devices: 5.92 us -> 7.19 us  [moved(): lax.ppermute(block, 'blk', [(source_of(i) % count, i) for i in range(coun...]
    pallas_call x4 -> x6, Pallas kernels: 26.3 us -> 27.3 us  [correlate(): pl.pallas_call(functools.partial(correlate_kernel, hop if isinstance(hop,...]
  transfers between devices with their start and end apart: 4 -> 6, of which waited for: 2 -> 2; matrix products, arithmetic and copies ran while one was open for 6% -> 6% of each run, Pallas kernels for 25% -> 30%
where the time goes in v5:
time: 80.4 us; the launch traced here: 78.8 us
  Pallas kernels  39 us (49%)
  waiting for transfers between devices  20.2 us (25%)
  starting transfers between devices  14.6 us (18%)
  other arithmetic  4.72 us (6%)
    pallas_call x6, Pallas kernels, correlate(): pl.pallas_call(functools.partial(correlate_kernel, hop if isinstance(hop,...  27.3 us
    all_to_all x1, waiting for transfers between devices, on_device(): lax.all_to_all(outgoing.reshape(peers, capacity // PACK, width), 'blk', s...  18.8 us
    pallas_call x1, Pallas kernels, spectra(): pl.pallas_call(functools.partial(spectrum_kernel, capacity), in_specs=[pl...  11 us
    all_to_all x1, starting transfers between devices, on_device(): lax.all_to_all(outgoing.reshape(peers, capacity // PACK, width), 'blk', s...  7.41 us
    ppermute x5, starting transfers between devices, moved(): lax.ppermute(block, 'blk', [(source_of(i) % count, i) for i in range(coun...  7.19 us
    convert_element_type x1, other arithmetic, inverse_table(): (-jnp.sin(angles)).astype(jnp.bfloat16)  4.72 us
  transfers between devices with their start and end apart: 6, of which 2 were waited for; matrix products, arithmetic and copies ran while one was open for 6% of the time, Pallas kernels for 30%

profile of v5, /device:TPU:0, one launch (start us, length us, event | category | flops | bytes accessed | tf_op | source)
XLA Modules:
  0.0 78.8 jit_solution(13417378485720938439)
XLA Ops:
  0.0 0.0 copy-start
  0.0 11.0 %spectra.1 = bf16[128,4224]{1,0:T(8,128)(2,1)} custom-call(s32[1,256]{1,0:T(1,128)} %bitcast.9, bf16[12000,256]{1,0:T(8,128)(2,1)} %bitcast.8, bf16[1024,3072]{1,0:T(8,128)(2,1)} %constant.46.clone.table_ref), custom_call_target="tpu_custom_call" | custom-call | flops 6291456000 | bytes 18432000 | tf_op jit(solution)/shard_map/spectra/pallas_call | solution.py:132
  11.0 7.4 %all-to-all-start = ((bf16[16,8,4224]{2,1,0:T(8,128)(2,1)}), bf16[16,8,4224]{2,1,0:T(8,128)(2,1)S(1)}, u32[]{:S(2)}, u32[]{:S(2)}) async-start(bf16[16,8,4224]{2,1,0:T(8,128)(2,1)} %bitcast.7), calls=%async_computation | async-start | bytes 2162688 | tf_op jit(solution)/shard_map/all_to_all | solution.py:337
  18.4 0.0 copy-done
  18.4 4.7 %negate_convert_fusion = (bf16[512,512]{1,0:T(8,128)(2,1)S(1)}, bf16[512,512]{1,0:T(8,128)(2,1)S(1)}) fusion(s32[512]{0:T(512)S(1)} %iota_add_fusion, s32[512]{0:T(512)S(1)} %copy-done), kind=kLoop, calls=%fused_computation.3 | loop fusion | flops 3145728 | bytes 1052672 | tf_op jit(solution)/shard_map/convert_element_type | solution.py:41
  23.1 18.8 %all-to-all-done = bf16[16,8,4224]{2,1,0:T(8,128)(2,1)S(1)} async-done(((bf16[16,8,4224]{2,1,0:T(8,128)(2,1)}), bf16[16,8,4224]{2,1,0:T(8,128)(2,1)S(1)}, u32[]{:S(2)}, u32[]{:S(2)}) %all-to-all-start) | async-done | bytes 1081376 | tf_op jit(solution)/shard_map/all_to_all | solution.py:337
  41.9 0.8 %place.1 = (bf16[256,1024]{1,0:T(8,128)(2,1)S(1)}, bf16[128,1024]{1,0:T(8,128)(2,1)S(1)}, bf16[128,1024]{1,0:T(8,128)(2,1)S(1)}) custom-call(bf16[128,4224]{1,0:T(8,128)(2,1)S(1)} %bitcast.6), custom_call_target="tpu_custom_call" | custom-call | tf_op jit(solution)/shard_map/place/pallas_call | solution.py:181
  42.7 5.7 %collective-permute-start.1 = (bf16[128,1024]{1,0:T(8,128)(2,1)S(1)}, bf16[128,1024]{1,0:T(8,128)(2,1)S(1)}, u32[]{:S(2)}, u32[]{:S(2)}) collective-permute-start(bf16[128,1024]{1,0:T(8,128)(2,1)S(1)} %get-tuple-element.25), channel_id=1, source_target_pairs={{2,0},{3,1},{4,2},{5,3},{6,4},{7,5},{8,6},{9,7},{10,8},{11,9},{12,... | collective-permute-start | bytes 786440 | tf_op jit(solution)/shard_map/ppermute | solution.py:33
  48.4 0.0 collective-permute-start
  48.4 6.6 %correlate.6.refs_5_ = bf16[32,4,32,801]{3,2,1,0:T(8,128)(2,1)} custom-call(s32[1]{0:T(128)} %constant.41.clone.1.refs_0_, bf16[256,1024]{1,0:T(8,128)(2,1)S(1)} %get-tuple-element.31.refs_1_.refs_2_, bf16[256,1024]{1,0:T(8,128)(2,1)S(1)} %get-tuple-element.31.refs_1_.refs_2_, bf16[512,512]{1,0:T(8,128)(2,1)S(1)} %get-tuple-element.26.refs_3_, ...), custom_call_target="tpu_custom_call" | custom-call | flops 3359637504 | bytes 1640448 | tf_op jit(solution)/shard_map/correlate/pallas_call | solution.py:307
  55.1 0.0 collective-permute-done.1.refs_2_
  55.1 3.5 %correlate.7.refs_5_ = bf16[32,4,32,801]{3,2,1,0:T(8,128)(2,1)} custom-call(s32[1]{0:T(128)} %constant.36.clone.1.refs_0_, bf16[256,1024]{1,0:T(8,128)(2,1)S(1)} %get-tuple-element.31.refs_1_.refs_2_, bf16[128,1024]{1,0:T(8,128)(2,1)S(1)} %collective-permute-done.1.refs_2_, ...), custom_call_target="tpu_custom_call", output_to_operand_aliasing={{}: (5, {})} | custom-call | flops 1679818752 | bytes 820224 | tf_op jit(solution)/shard_map/correlate/pallas_call | solution.py:307
  58.6 1.4 %collective-permute-done.refs_2_ = bf16[128,1024]{1,0:T(8,128)(2,1)S(1)} collective-permute-done((bf16[128,1024]{1,0:T(8,128)(2,1)S(1)}, bf16[128,1024]{1,0:T(8,128)(2,1)S(1)}, u32[]{:S(2)}, u32[]{:S(2)}) %collective-permute-start) | collective-permute-done | bytes 262176 | tf_op jit(solution)/shard_map/ppermute | solution.py:33
  60.0 1.0 %collective-permute-start.3 = (bf16[256,1024]{1,0:T(8,128)(2,1)S(1)}, bf16[256,1024]{1,0:T(8,128)(2,1)S(1)}, u32[]{:S(2)}, u32[]{:S(2)}) collective-permute-start(bf16[256,1024]{1,0:T(8,128)(2,1)S(1)} %get-tuple-element.31.refs_1_.refs_2_), channel_id=1, source_target_pairs={{1,0},{4,1},{3,2},{6,3},{5,4},{8,5},{7,6},{10,7},{9,8},{12,9},{11,... | collective-permute-start | bytes 1572872 | tf_op jit(solution)/shard_map/ppermute | solution.py:33
  61.0 0.0 collective-permute-start.4
  61.0 0.5 collective-permute-start.2
  61.5 3.5 %correlate.8.refs_5_ = bf16[32,4,32,801]{3,2,1,0:T(8,128)(2,1)} custom-call(s32[1]{0:T(128)} %bitcast.5.refs_0_, bf16[256,1024]{1,0:T(8,128)(2,1)S(1)} %get-tuple-element.31.refs_1_.refs_2_, bf16[128,1024]{1,0:T(8,128)(2,1)S(1)} %collective-permute-done.refs_2_, bf16[512,512]{1,0:T(8,128)(2,1)S(1)} %get-tuple-element.26.refs_3_, ...), custom_call_target="tpu_custom_call", output_to_operand_aliasing={{}: (5, {})} | custom-call | flops 1679818752 | bytes 820224 | tf_op jit(solution)/shard_map/correlate/pallas_call | solution.py:307
  65.0 0.0 collective-permute-done.4.refs_2_
  65.0 3.5 %correlate.9.refs_5_ = bf16[32,4,32,801]{3,2,1,0:T(8,128)(2,1)} custom-call(s32[1]{0:T(128)} %bitcast.5.refs_0_, bf16[256,1024]{1,0:T(8,128)(2,1)S(1)} %get-tuple-element.31.refs_1_.refs_2_, bf16[128,1024]{1,0:T(8,128)(2,1)S(1)} %collective-permute-done.4.refs_2_, bf16[512,512]{1,0:T(8,128)(2,1)S(1)} %get-tuple-element.26.refs_3_, ...), custom_call_target="tpu_custom_call", output_to_operand_aliasing={{}: (5, {})} | custom-call | flops 1679818752 | bytes 820224 | tf_op jit(solution)/shard_map/correlate/pallas_call | solution.py:307
  68.6 0.0 collective-permute-done.3.refs_2_
  68.6 6.6 %correlate.10.refs_5_ = bf16[32,4,32,801]{3,2,1,0:T(8,128)(2,1)} custom-call(s32[1]{0:T(128)} %bitcast.4.refs_0_, bf16[256,1024]{1,0:T(8,128)(2,1)S(1)} %get-tuple-element.31.refs_1_.refs_2_, bf16[256,1024]{1,0:T(8,128)(2,1)S(1)} %collective-permute-done.3.refs_2_, bf16[512,512]{1,0:T(8,128)(2,1)S(1)} %get-tuple-element.26.refs_3_, ...), custom_call_target="tpu_custom_call", output_to_operand_aliasing={{}: (5, {})} | custom-call | flops 3359637504 | bytes 1640448 | tf_op jit(solution)/shard_map/correlate/pallas_call | solution.py:307
  75.1 0.0 collective-permute-done.2.refs_2_
  75.2 3.5 %correlate.11 = bf16[32,4,32,801]{3,2,1,0:T(8,128)(2,1)} custom-call(s32[1]{0:T(128)} %constant.36.clone.1.refs_0_, bf16[256,1024]{1,0:T(8,128)(2,1)S(1)} %get-tuple-element.31.refs_1_.refs_2_, bf16[128,1024]{1,0:T(8,128)(2,1)S(1)} %collective-permute-done.2.refs_2_, bf16[512,512]{1,0:T(8,128)(2,1)S(1)} %get-tuple-element.26.refs_3_, ...), custom_call_target="tpu_custom_call", output_to_operand_aliasing={{}: (5, {})} | custom-call | flops 1679818752 | bytes 820224 | tf_op jit(solution)/shard_map/correlate/pallas_call | solution.py:307
  (1 shorter events, 0.0 us)
Async XLA Ops:
  0.0 18.4 %copy-start = (s32[512]{0:T(512)S(1)}, s32[512]{0:T(512)}, u32[]{:S(2)}) copy-start(s32[512]{0:T(512)} %constant.47.clone) | copy-start | bytes 6148
  11.0 30.9 %all-to-all-start = ((bf16[16,8,4224]{2,1,0:T(8,128)(2,1)}), bf16[16,8,4224]{2,1,0:T(8,128)(2,1)S(1)}, u32[]{:S(2)}, u32[]{:S(2)}) async-start(bf16[16,8,4224]{2,1,0:T(8,128)(2,1)} %bitcast.7), calls=%async_computation | async-start | bytes 2162688 | tf_op jit(solution)/shard_map/all_to_all | solution.py:337
  42.7 12.4 %collective-permute-start.1 = (bf16[128,1024]{1,0:T(8,128)(2,1)S(1)}, bf16[128,1024]{1,0:T(8,128)(2,1)S(1)}, u32[]{:S(2)}, u32[]{:S(2)}) collective-permute-start(bf16[128,1024]{1,0:T(8,128)(2,1)S(1)} %get-tuple-element.25), channel_id=1, source_target_pairs={{2,0},{3,1},{4,2},{5,3},{6,4},{7,5},{8,6},{9,7},{10,8},{11,9},{12,... | collective-permute-start | bytes 786440 | tf_op jit(solution)/shard_map/ppermute | solution.py:33
  48.4 11.6 %collective-permute-start = (bf16[128,1024]{1,0:T(8,128)(2,1)S(1)}, bf16[128,1024]{1,0:T(8,128)(2,1)S(1)}, u32[]{:S(2)}, u32[]{:S(2)}) collective-permute-start(bf16[128,1024]{1,0:T(8,128)(2,1)S(1)} %get-tuple-element.24), channel_id=1, source_target_pairs={{3,0},{2,1},{5,2},{4,3},{7,4},{6,5},{9,6},{8,7},{11,8},{10,9},{13,... | collective-permute-start | bytes 786440 | tf_op jit(solution)/shard_map/ppermute | solution.py:33
  60.0 8.5 %collective-permute-start.3 = (bf16[256,1024]{1,0:T(8,128)(2,1)S(1)}, bf16[256,1024]{1,0:T(8,128)(2,1)S(1)}, u32[]{:S(2)}, u32[]{:S(2)}) collective-permute-start(bf16[256,1024]{1,0:T(8,128)(2,1)S(1)} %get-tuple-element.31.refs_1_.refs_2_), channel_id=1, source_target_pairs={{1,0},{4,1},{3,2},{6,3},{5,4},{8,5},{7,6},{10,7},{9,8},{12,9},{11,... | collective-permute-start | bytes 1572872 | tf_op jit(solution)/shard_map/ppermute | solution.py:33
  61.0 4.0 %collective-permute-start.4 = (bf16[128,1024]{1,0:T(8,128)(2,1)S(1)}, bf16[128,1024]{1,0:T(8,128)(2,1)S(1)}, u32[]{:S(2)}, u32[]{:S(2)}) collective-permute-start(bf16[128,1024]{1,0:T(8,128)(2,1)S(1)} %collective-permute-done.1.refs_2_), channel_id=1, source_target_pairs={{1,0},{0,1},{3,2},{2,3},{5,4},{4,5},{7,6},{6,7},{9,8},{8,9},{11,10... | collective-permute-start | bytes 786440 | tf_op jit(solution)/shard_map/ppermute | solution.py:33
  61.0 14.1 %collective-permute-start.2 = (bf16[128,1024]{1,0:T(8,128)(2,1)S(1)}, bf16[128,1024]{1,0:T(8,128)(2,1)S(1)}, u32[]{:S(2)}, u32[]{:S(2)}) collective-permute-start(bf16[128,1024]{1,0:T(8,128)(2,1)S(1)} %collective-permute-done.refs_2_), channel_id=1, source_target_pairs={{1,0},{0,1},{3,2},{2,3},{5,4},{4,5},{7,6},{6,7},{9,8},{8,9},{11,10... | collective-permute-start | bytes 786440 | tf_op jit(solution)/shard_map/ppermute | solution.py:33

commit v6 on v5

--- a/solution.py
+++ b/solution.py
@@ -64,6 +64,29 @@
     for group in copies:
         for copy in group:
             copy.start()
+    rec_count = id_ref.shape[1]
+    ids = id_ref[...]
+    owner = ids // rec_count
+    row = jnp.broadcast_to(owner, (rec_count, rec_count))
+    before = lax.broadcasted_iota(jnp.int32, row.shape, 0) < lax.broadcasted_iota(
+        jnp.int32, row.shape, 1
+    )
+    rank = jnp.sum(jnp.where((row == row.T) & before, 1, 0), axis=0, keepdims=True)
+    target = owner * capacity + rank
+    label = (ids % rec_count + 1).astype(jnp.float32)
+    out_rows = out_ref.shape[0]
+    slot = lax.broadcasted_iota(jnp.int32, (out_rows, rec_count), 0) * PACK
+    lane = lax.broadcasted_iota(jnp.int32, (out_rows, TAIL), 1)
+    labels = jnp.zeros((out_rows, TAIL), jnp.float32)
+    picks = []
+    for q in range(PACK):
+        hit = slot + q == target
+        labels = jnp.where(
+            lane == q, jnp.sum(jnp.where(hit, label, 0.0), axis=1, keepdims=True), labels
+        )
+        picks.append(jnp.where(hit, 1.0, 0.0).astype(jnp.bfloat16))
+    pick = jnp.concatenate(picks)
+    out_ref[:, PACK * 2 * F :] = labels.astype(jnp.bfloat16)
     for group, begin, end in zip(copies, begins, ENDS):
         for copy in group:
             copy.wait()
@@ -89,32 +112,10 @@
                 both = straight[mine] + across[theirs] if signs[block] > 0 else straight[mine] - across[theirs]
                 total[mine, :] = both if begin == 0 else total[mine, :] + both
 
-    rec_count = id_ref.shape[1]
-    ids = id_ref[...]
-    owner = ids // rec_count
-    row = jnp.broadcast_to(owner, (rec_count, rec_count))
-    before = lax.broadcasted_iota(jnp.int32, row.shape, 0) < lax.broadcasted_iota(
-        jnp.int32, row.shape, 1
-    )
-    rank = jnp.sum(jnp.where((row == row.T) & before, 1, 0), axis=0, keepdims=True)
-    target = owner * capacity + rank
-    label = (ids % rec_count + 1).astype(jnp.float32)
     power = jnp.sum(even[...] * even[...], axis=0, keepdims=True)
     power = (power + jnp.sum(odd[...] * odd[...], axis=0, keepdims=True)) / F
     scale = lax.rsqrt(power + 1e-06)
     half = F // 2
-    rows = out_ref.shape[0]
-    slot = lax.broadcasted_iota(jnp.int32, (rows, rec_count), 0) * PACK
-    lane = lax.broadcasted_iota(jnp.int32, (rows, TAIL), 1)
-    labels = jnp.zeros((rows, TAIL), jnp.float32)
-    picks = []
-    for q in range(PACK):
-        hit = slot + q == target
-        labels = jnp.where(
-            lane == q, jnp.sum(jnp.where(hit, label, 0.0), axis=1, keepdims=True), labels
-        )
-        picks.append(jnp.where(hit, 1.0, 0.0).astype(jnp.bfloat16))
-    pick = jnp.concatenate(picks)
     for place, (part, base) in enumerate(((even, 0), (odd, 0), (even, half), (odd, half))):
         white = (part[base : base + half, :] * scale).astype(jnp.bfloat16)
         moved = lax.dot_general(
@@ -122,8 +123,7 @@
         ).astype(jnp.bfloat16)
         for q in range(PACK):
             lanes = slice(q * 2 * F + place * half, q * 2 * F + (place + 1) * half)
-            out_ref[:, lanes] = moved[q * rows : (q + 1) * rows]
-    out_ref[:, PACK * 2 * F :] = labels.astype(jnp.bfloat16)
+            out_ref[:, lanes] = moved[q * out_rows : (q + 1) * out_rows]
 
 
 def spectra(traces, record_id, capacity, slots):
@@ -189,28 +189,23 @@
     )(arrived)
 
 
-def correlate_kernel(hop_index, begin, group, batch, count, *refs):
-    hop_ref, own_ref = refs[:2]
-    other_refs = refs[2 : 2 + count]
-    cos_ref, sin_ref = refs[2 + count : 4 + count]
-    out_ref, mine, theirs, cross, done, sems = refs[-6:]
-    full = own_ref.shape[0] // NWIN
+def correlate_kernel(own_pair, spans, group, batch, count, *refs):
+    hop_ref = refs[0]
+    other_refs = refs[1 : 1 + count]
+    cos_ref, sin_ref = refs[1 + count : 3 + count]
+    if own_pair:
+        out_ref, mine, theirs, cross, done, sems = refs[-6:]
+    else:
+        mine = refs[3 + count]
+        out_ref, theirs, cross, done, sems = refs[-5:]
+    full = mine.shape[1] // NWIN
     side = full // 2
     width = theirs.shape[1] // NWIN
-    own_blocks = [(own_ref, half * NWIN * side, half * side) for half in range(2)]
-    if other_refs[0].shape[0] == own_ref.shape[0]:
+    if len(other_refs) * side < width:
         blocks = [(other_refs[0], half * NWIN * side, half * side) for half in range(2)]
     else:
         blocks = [(ref, 0, half * side) for half, ref in enumerate(other_refs)]
     for w in range(NWIN):
-        for ref, base, place in own_blocks:
-            source = slice(base + w * side, base + (w + 1) * side)
-            rows = slice(w * full + place, w * full + place + side)
-            real = ref[source, :F].astype(jnp.float32)
-            imag = ref[source, F:].astype(jnp.float32)
-            mine[0, rows, :] = real + imag
-            mine[1, rows, :] = real
-            mine[2, rows, :] = imag
         for ref, base, place in blocks:
             source = slice(base + w * side, base + (w + 1) * side)
             rows = slice(w * width + place, w * width + place + side)
@@ -219,6 +214,10 @@
             theirs[0, rows, :] = real
             theirs[1, rows, :] = real + imag
             theirs[2, rows, :] = real - imag
+            if own_pair:
+                mine[0, rows, :] = real + imag
+                mine[1, rows, :] = real
+                mine[2, rows, :] = imag
 
     shared = 64 // width
 
@@ -271,52 +270,58 @@
         ]
         lagged = jnp.concatenate(pieces + [later[:, : NLAG - PLUS]], axis=1)
         lagged = lagged.reshape(batch, width, NLAG)
-        if hop_index == 0:
+        if own_pair:
             channel = lax.broadcasted_iota(jnp.int32, lagged.shape, 0) + step * batch
             partner = lax.broadcasted_iota(jnp.int32, lagged.shape, 1)
             lagged = jnp.where(channel == partner, 0.0, lagged)
         channels = slice(step * batch, (step + 1) * batch)
         done[channels] = lagged.astype(jnp.bfloat16)
-        copy = pltpu.make_async_copy(
-            done.at[channels],
-            out_ref.at[channels, hop_ref[0], begin : begin + width],
-            sems.at[step],
-        )
-        copy.start()
-        copies.append(copy)
+        for k, (hop, begin, start, length) in enumerate(spans):
+            copy = pltpu.make_async_copy(
+                done.at[channels, start : start + length],
+                out_ref.at[channels, hop_ref[0] if hop is None else hop, begin : begin + length],
+                sems.at[step, k],
+            )
+            copy.start()
+            copies.append(copy)
     for copy in copies:
         copy.wait()
 
 
-def correlate(own, others, inverse, hop, result, begin=0):
-    rec_count = own.shape[0]
-    full = rec_count // NWIN
+def correlate(mine, others, inverse, hop, spans, result):
+    own_pair = mine is None
     rows = sum(other.shape[0] for other in others)
     width = rows // NWIN
+    form = jax.ShapeDtypeStruct((3, rows, F), jnp.float32) if own_pair else mine
+    full = form.shape[1] // NWIN
     group = 8
     batch = 256 // width
-    operands = [jnp.asarray(hop, jnp.int32).reshape(1), own, *others, *inverse]
+    operands = [jnp.asarray(hop, jnp.int32).reshape(1), *others, *inverse]
+    if not own_pair:
+        operands.append(mine)
     in_specs = [pl.BlockSpec(memory_space=pltpu.SMEM)]
     in_specs += [pl.BlockSpec(memory_space=pltpu.VMEM)] * (len(operands) - 1)
+    out_specs = [pl.BlockSpec(memory_space=pl.ANY)]
+    out_shape = [jax.ShapeDtypeStruct((full, HOPS + 1, full, NLAG), jnp.bfloat16)]
     aliases = {}
-    if result is not None:
+    if own_pair:
+        out_specs.append(pl.BlockSpec(memory_space=pltpu.VMEM))
+        out_shape.append(form)
+    else:
         in_specs.append(pl.BlockSpec(memory_space=pl.ANY))
         aliases = {len(operands): 0}
         operands.append(result)
     pairs = full * width
     return pl.pallas_call(
-        functools.partial(
-            correlate_kernel, hop if isinstance(hop, int) else None, begin, group, batch, len(others)
-        ),
+        functools.partial(correlate_kernel, own_pair, spans, group, batch, len(others)),
         in_specs=in_specs,
-        out_specs=pl.BlockSpec(memory_space=pl.ANY),
-        out_shape=jax.ShapeDtypeStruct((full, HOPS + 1, full, NLAG), jnp.bfloat16),
+        out_specs=out_specs,
+        out_shape=out_shape,
         scratch_shapes=[
-            pltpu.VMEM((3, rec_count, F), jnp.float32),
             pltpu.VMEM((3, rows, F), jnp.float32),
             pltpu.VMEM((pairs, 2 * F), jnp.bfloat16),
             pltpu.VMEM((full, width, NLAG), jnp.bfloat16),
-            pltpu.SemaphoreType.DMA((full // batch,)),
+            pltpu.SemaphoreType.DMA((full // batch, len(spans))),
         ],
         input_output_aliases=aliases,
         compiler_params=pltpu.CompilerParams(vmem_limit_bytes=24 * MIB),
@@ -346,20 +351,23 @@
     side = rec_count // NWIN // 2
     low = moved(low, lambda i: i + 2)
     high = moved(high, lambda i: i + 1 if i % 2 else i + 3)
-    result = correlate(own, [own], inverse, 0, None)
+    whole, first = (None, 0, 0, 2 * side), (None, 0, 0, side)
+    result, mine = correlate(None, [own], inverse, 0, (whole,), None)
+
+    def add(others, hop, *spans):
+        return correlate(mine, others, inverse, hop, spans, result)[0]
+
     low, result = barrier((low, result))
     far_low = moved(low, lambda i: i ^ 1)
-    result = correlate(own, [low], inverse, 2, result)
+    result = add([low], 2, first)
     again, high, result = barrier((own, high, result))
     near = moved(again, lambda i: i + 3 if i % 2 else i + 1)
     far_high = moved(high, lambda i: i ^ 1)
-    result = correlate(own, [high], inverse, far_hop, result, side)
-    far_low, result = barrier((far_low, result))
-    result = correlate(own, [far_low], inverse, far_hop, result)
+    result = add([high], far_hop, (None, side, 0, side))
     near, result = barrier((near, result))
-    result = correlate(own, [near], inverse, near_hop, result)
-    far_high, result = barrier((far_high, result))
-    return correlate(own, [far_high], inverse, 2, result, side)
+    result = add([near], near_hop, whole)
+    far_low, far_high, result = barrier((far_low, far_high, result))
+    return add([far_low, far_high], far_hop, first, (2, side, side, side))
 
 
 def solution(mesh):

time: 80.4 us -> 84.1 us (1.046)
  Pallas kernels: 39 us -> 41.1 us
  waiting for transfers between devices: 20.2 us -> 21.3 us
  starting transfers between devices: 14.6 us -> 15.5 us
    pallas_call x6 -> x5, Pallas kernels: 27.3 us -> 28.5 us  [correlate(): pl.pallas_call(functools.partial(correlate_kernel, own_pair, spans, group...]
    ppermute x5, waiting for transfers between devices: 1.46 us -> 2.56 us  [moved(): lax.ppermute(block, 'blk', [(source_of(i) % count, i) for i in range(coun...]
    ppermute x5, starting transfers between devices: 7.19 us -> 8.1 us  [moved(): lax.ppermute(block, 'blk', [(source_of(i) % count, i) for i in range(coun...]
  transfers between devices with their start and end apart: 6 -> 6, of which waited for: 2 -> 3; matrix products, arithmetic and copies ran while one was open for 6% -> 6% of each run, Pallas kernels for 30% -> 27%
where the time goes in v6:
time: 84.1 us; the launch traced here: 82.9 us
  Pallas kernels  41.1 us (49%)
  waiting for transfers between devices  21.3 us (25%)
  starting transfers between devices  15.5 us (18%)
  other arithmetic  4.73 us (6%)
    pallas_call x5, Pallas kernels, correlate(): pl.pallas_call(functools.partial(correlate_kernel, own_pair, spans, group...  28.5 us
    all_to_all x1, waiting for transfers between devices, on_device(): lax.all_to_all(outgoing.reshape(peers, capacity // PACK, width), 'blk', s...  18.7 us
    pallas_call x1, Pallas kernels, spectra(): pl.pallas_call(functools.partial(spectrum_kernel, capacity), in_specs=[pl...  11 us
    ppermute x5, starting transfers between devices, moved(): lax.ppermute(block, 'blk', [(source_of(i) % count, i) for i in range(coun...  8.1 us
    all_to_all x1, starting transfers between devices, on_device(): lax.all_to_all(outgoing.reshape(peers, capacity // PACK, width), 'blk', s...  7.4 us
    convert_element_type x1, other arithmetic, inverse_table(): (-jnp.sin(angles)).astype(jnp.bfloat16)  4.73 us
    ppermute x5, waiting for transfers between devices, moved(): lax.ppermute(block, 'blk', [(source_of(i) % count, i) for i in range(coun...  2.56 us
  transfers between devices with their start and end apart: 6, of which 3 were waited for; matrix products, arithmetic and copies ran while one was open for 6% of the time, Pallas kernels for 27%

profile of v6, /device:TPU:0, one launch (start us, length us, event | category | flops | bytes accessed | tf_op | source)
XLA Modules:
  0.0 82.9 jit_solution(15318551048751118486)
XLA Ops:
  0.0 0.0 copy-start
  0.0 11.0 %spectra.1 = bf16[128,4224]{1,0:T(8,128)(2,1)} custom-call(s32[1,256]{1,0:T(1,128)} %bitcast.9, bf16[12000,256]{1,0:T(8,128)(2,1)} %bitcast.8, bf16[1024,3072]{1,0:T(8,128)(2,1)} %constant.46.clone.table_ref), custom_call_target="tpu_custom_call" | custom-call | flops 6291456000 | bytes 18432000 | tf_op jit(solution)/shard_map/spectra/pallas_call | solution.py:132
  11.0 7.4 %all-to-all-start = ((bf16[16,8,4224]{2,1,0:T(8,128)(2,1)}), bf16[16,8,4224]{2,1,0:T(8,128)(2,1)S(1)}, u32[]{:S(2)}, u32[]{:S(2)}) async-start(bf16[16,8,4224]{2,1,0:T(8,128)(2,1)} %bitcast.7), calls=%async_computation | async-start | bytes 2162688 | tf_op jit(solution)/shard_map/all_to_all | solution.py:342
  18.4 0.0 copy-done
  18.4 4.7 %negate_convert_fusion = (bf16[512,512]{1,0:T(8,128)(2,1)S(1)}, bf16[512,512]{1,0:T(8,128)(2,1)S(1)}) fusion(s32[512]{0:T(512)S(1)} %iota_add_fusion, s32[512]{0:T(512)S(1)} %copy-done), kind=kLoop, calls=%fused_computation.3 | loop fusion | flops 3145728 | bytes 1052672 | tf_op jit(solution)/shard_map/convert_element_type | solution.py:41
  23.2 18.7 %all-to-all-done = bf16[16,8,4224]{2,1,0:T(8,128)(2,1)S(1)} async-done(((bf16[16,8,4224]{2,1,0:T(8,128)(2,1)}), bf16[16,8,4224]{2,1,0:T(8,128)(2,1)S(1)}, u32[]{:S(2)}, u32[]{:S(2)}) %all-to-all-start) | async-done | bytes 1081376 | tf_op jit(solution)/shard_map/all_to_all | solution.py:342
  41.9 1.6 %place.1 = (bf16[256,1024]{1,0:T(8,128)(2,1)}, bf16[128,1024]{1,0:T(8,128)(2,1)S(1)}, bf16[128,1024]{1,0:T(8,128)(2,1)S(1)}) custom-call(bf16[128,4224]{1,0:T(8,128)(2,1)S(1)} %bitcast.6), custom_call_target="tpu_custom_call" | custom-call | tf_op jit(solution)/shard_map/place/pallas_call | solution.py:181
  43.5 5.6 %collective-permute-start = (bf16[128,1024]{1,0:T(8,128)(2,1)S(1)}, bf16[128,1024]{1,0:T(8,128)(2,1)S(1)}, u32[]{:S(2)}, u32[]{:S(2)}) collective-permute-start(bf16[128,1024]{1,0:T(8,128)(2,1)S(1)} %get-tuple-element.24), channel_id=1, source_target_pairs={{2,0},{3,1},{4,2},{5,3},{6,4},{7,5},{8,6},{9,7},{10,8},{11,9},{12,... | collective-permute-start | bytes 786440 | tf_op jit(solution)/shard_map/ppermute | solution.py:33
  49.1 0.0 collective-permute-start.2
  49.2 7.7 %correlate.5 = (bf16[32,4,32,801]{3,2,1,0:T(8,128)(2,1)}, f32[3,256,512]{2,1,0:T(8,128)S(1)}) custom-call(s32[1]{0:T(128)} %constant.44.clone.1.refs_0_, bf16[256,1024]{1,0:T(8,128)(2,1)} %get-tuple-element.34.refs_1_, bf16[512,512]{1,0:T(8,128)(2,1)S(1)} %get-tuple-element.26.refs_2_.refs_3_, bf16[512,512]{1,0:T(8,128)(2,1)S(1)} %get-tuple-element.27.refs_3_.refs_4_), custom_call_target="tpu_custom_call" | custom-call | flops 3359637504 | bytes 1640448 | tf_op jit(solution)/shard_map/correlate/pallas_call | solution.py:315
  56.8 0.0 collective-permute-done.refs_1_
  56.8 3.5 %correlate.6.refs_5_ = bf16[32,4,32,801]{3,2,1,0:T(8,128)(2,1)} custom-call(s32[1]{0:T(128)} %constant.45.clone.1.refs_0_, bf16[128,1024]{1,0:T(8,128)(2,1)S(1)} %collective-permute-done.refs_1_, bf16[512,512]{1,0:T(8,128)(2,1)S(1)} %get-tuple-element.26.refs_2_.refs_3_, ...), custom_call_target="tpu_custom_call", output_to_operand_aliasing={{}: (5, {})} | custom-call | flops 1679818752 | bytes 820224 | tf_op jit(solution)/shard_map/correlate/pallas_call | solution.py:315
  60.3 0.5 collective-permute-done.2.refs_1_
  60.8 2.0 %collective-permute-start.4 = (bf16[256,1024]{1,0:T(8,128)(2,1)}, bf16[256,1024]{1,0:T(8,128)(2,1)S(1)}, u32[]{:S(2)}, u32[]{:S(2)}) collective-permute-start(bf16[256,1024]{1,0:T(8,128)(2,1)} %get-tuple-element.34.refs_1_), channel_id=1, source_target_pairs={{1,0},{4,1},{3,2},{6,3},{5,4},{8,5},{7,6},{10,7},{9,8},{12,9},{11,... | collective-permute-start | bytes 1572872 | tf_op jit(solution)/shard_map/ppermute | solution.py:33
  62.8 0.0 collective-permute-start.1
  62.8 0.5 collective-permute-start.3
  63.3 4.4 %correlate.7.refs_5_ = bf16[32,4,32,801]{3,2,1,0:T(8,128)(2,1)} custom-call(s32[1]{0:T(128)} %bitcast.refs_0_, bf16[128,1024]{1,0:T(8,128)(2,1)} %collective-permute-done.2.refs_1_, bf16[512,512]{1,0:T(8,128)(2,1)S(1)} %get-tuple-element.26.refs_2_.refs_3_, bf16[512,512]{1,0:T(8,128)(2,1)S(1)} %get-tuple-element.27.refs_3_.refs_4_, ...), custom_call_target="tpu_custom_call", output_to_operand_aliasing={{}: (5, {})} | custom-call | flops 1679818752 | bytes 820224 | tf_op jit(solution)/shard_map/correlate/pallas_call | solution.py:315
  67.7 2.1 %collective-permute-done.4.refs_1_ = bf16[256,1024]{1,0:T(8,128)(2,1)S(1)} collective-permute-done((bf16[256,1024]{1,0:T(8,128)(2,1)}, bf16[256,1024]{1,0:T(8,128)(2,1)S(1)}, u32[]{:S(2)}, u32[]{:S(2)}) %collective-permute-start.4) | collective-permute-done | bytes 524320 | tf_op jit(solution)/shard_map/ppermute | solution.py:33
  69.8 6.4 %correlate.8.refs_6_ = bf16[32,4,32,801]{3,2,1,0:T(8,128)(2,1)} custom-call(s32[1]{0:T(128)} %bitcast.5.refs_0_, bf16[256,1024]{1,0:T(8,128)(2,1)S(1)} %collective-permute-done.4.refs_1_, bf16[512,512]{1,0:T(8,128)(2,1)S(1)} %get-tuple-element.26.refs_2_.refs_3_, ...), custom_call_target="tpu_custom_call", output_to_operand_aliasing={{}: (5, {})} | custom-call | flops 3359637504 | bytes 1640448 | tf_op jit(solution)/shard_map/correlate/pallas_call | solution.py:315
  76.2 0.0 collective-permute-done.3.refs_2_
  76.2 0.0 collective-permute-done.1.refs_1_
  76.2 6.5 %correlate.9 = bf16[32,4,32,801]{3,2,1,0:T(8,128)(2,1)} custom-call(s32[1]{0:T(128)} %bitcast.refs_0_, bf16[128,1024]{1,0:T(8,128)(2,1)S(1)} %collective-permute-done.1.refs_1_, bf16[128,1024]{1,0:T(8,128)(2,1)S(1)} %collective-permute-done.3.refs_2_, bf16[512,512]{1,0:T(8,128)(2,1)S(1)} %get-tuple-element.26.refs_2_.refs_3_, ...), custom_call_target="tpu_custom_call", output_to_operand_aliasing={{}: (6, {})} | custom-call | flops 3359637504 | bytes 1640448 | tf_op jit(solution)/shard_map/correlate/pallas_call | solution.py:315
  (1 shorter events, 0.0 us)
Async XLA Ops:
  0.0 18.4 %copy-start = (s32[512]{0:T(512)S(1)}, s32[512]{0:T(512)}, u32[]{:S(2)}) copy-start(s32[512]{0:T(512)} %constant.47.clone) | copy-start | bytes 6148
  11.0 30.9 %all-to-all-start = ((bf16[16,8,4224]{2,1,0:T(8,128)(2,1)}), bf16[16,8,4224]{2,1,0:T(8,128)(2,1)S(1)}, u32[]{:S(2)}, u32[]{:S(2)}) async-start(bf16[16,8,4224]{2,1,0:T(8,128)(2,1)} %bitcast.7), calls=%async_computation | async-start | bytes 2162688 | tf_op jit(solution)/shard_map/all_to_all | solution.py:342
  43.5 13.3 %collective-permute-start = (bf16[128,1024]{1,0:T(8,128)(2,1)S(1)}, bf16[128,1024]{1,0:T(8,128)(2,1)S(1)}, u32[]{:S(2)}, u32[]{:S(2)}) collective-permute-start(bf16[128,1024]{1,0:T(8,128)(2,1)S(1)} %get-tuple-element.24), channel_id=1, source_target_pairs={{2,0},{3,1},{4,2},{5,3},{6,4},{7,5},{8,6},{9,7},{10,8},{11,9},{12,... | collective-permute-start | bytes 786440 | tf_op jit(solution)/shard_map/ppermute | solution.py:33
  49.1 11.6 %collective-permute-start.2 = (bf16[128,1024]{1,0:T(8,128)(2,1)S(1)}, bf16[128,1024]{1,0:T(8,128)(2,1)}, u32[]{:S(2)}, u32[]{:S(2)}) collective-permute-start(bf16[128,1024]{1,0:T(8,128)(2,1)S(1)} %get-tuple-element.30), channel_id=1, source_target_pairs={{3,0},{2,1},{5,2},{4,3},{7,4},{6,5},{9,6},{8,7},{11,8},{10,9},{13,... | collective-permute-start | bytes 786440 | tf_op jit(solution)/shard_map/ppermute | solution.py:33
  60.8 9.0 %collective-permute-start.4 = (bf16[256,1024]{1,0:T(8,128)(2,1)}, bf16[256,1024]{1,0:T(8,128)(2,1)S(1)}, u32[]{:S(2)}, u32[]{:S(2)}) collective-permute-start(bf16[256,1024]{1,0:T(8,128)(2,1)} %get-tuple-element.34.refs_1_), channel_id=1, source_target_pairs={{1,0},{4,1},{3,2},{6,3},{5,4},{8,5},{7,6},{10,7},{9,8},{12,9},{11,... | collective-permute-start | bytes 1572872 | tf_op jit(solution)/shard_map/ppermute | solution.py:33
  62.8 13.5 %collective-permute-start.1 = (bf16[128,1024]{1,0:T(8,128)(2,1)S(1)}, bf16[128,1024]{1,0:T(8,128)(2,1)S(1)}, u32[]{:S(2)}, u32[]{:S(2)}) collective-permute-start(bf16[128,1024]{1,0:T(8,128)(2,1)S(1)} %collective-permute-done.refs_1_), channel_id=1, source_target_pairs={{1,0},{0,1},{3,2},{2,3},{5,4},{4,5},{7,6},{6,7},{9,8},{8,9},{11,10... | collective-permute-start | bytes 786440 | tf_op jit(solution)/shard_map/ppermute | solution.py:33
  62.8 13.5 %collective-permute-start.3 = (bf16[128,1024]{1,0:T(8,128)(2,1)}, bf16[128,1024]{1,0:T(8,128)(2,1)S(1)}, u32[]{:S(2)}, u32[]{:S(2)}) collective-permute-start(bf16[128,1024]{1,0:T(8,128)(2,1)} %collective-permute-done.2.refs_1_), channel_id=1, source_target_pairs={{1,0},{0,1},{3,2},{2,3},{5,4},{4,5},{7,6},{6,7},{9,8},{8,9},{11,10... | collective-permute-start | bytes 786440 | tf_op jit(solution)/shard_map/ppermute | solution.py:33

commit v7 on v6

--- a/solution.py
+++ b/solution.py
@@ -190,22 +190,27 @@
 
 
 def correlate_kernel(own_pair, spans, group, batch, count, *refs):
-    hop_ref = refs[0]
-    other_refs = refs[1 : 1 + count]
-    cos_ref, sin_ref = refs[1 + count : 3 + count]
-    if own_pair:
-        out_ref, mine, theirs, cross, done, sems = refs[-6:]
-    else:
-        mine = refs[3 + count]
-        out_ref, theirs, cross, done, sems = refs[-5:]
+    hop_ref, own_ref = refs[:2]
+    other_refs = refs[2 : 2 + count]
+    cos_ref, sin_ref = refs[2 + count : 4 + count]
+    out_ref, mine, theirs, cross, done, sems = refs[-6:]
     full = mine.shape[1] // NWIN
     side = full // 2
     width = theirs.shape[1] // NWIN
+    own_blocks = [(own_ref, half * NWIN * side, half * side) for half in range(2)]
     if len(other_refs) * side < width:
         blocks = [(other_refs[0], half * NWIN * side, half * side) for half in range(2)]
     else:
         blocks = [(ref, 0, half * side) for half, ref in enumerate(other_refs)]
     for w in range(NWIN):
+        for ref, base, place in own_blocks:
+            source = slice(base + w * side, base + (w + 1) * side)
+            rows = slice(w * full + place, w * full + place + side)
+            real = ref[source, :F].astype(jnp.float32)
+            imag = ref[source, F:].astype(jnp.float32)
+            mine[0, rows, :] = real + imag
+            mine[1, rows, :] = real
+            mine[2, rows, :] = imag
         for ref, base, place in blocks:
             source = slice(base + w * side, base + (w + 1) * side)
             rows = slice(w * width + place, w * width + place + side)
@@ -214,10 +219,6 @@
             theirs[0, rows, :] = real
             theirs[1, rows, :] = real + imag
             theirs[2, rows, :] = real - imag
-            if own_pair:
-                mine[0, rows, :] = real + imag
-                mine[1, rows, :] = real
-                mine[2, rows, :] = imag
 
     shared = 64 // width
 
@@ -272,7 +273,7 @@
         lagged = lagged.reshape(batch, width, NLAG)
         if own_pair:
             channel = lax.broadcasted_iota(jnp.int32, lagged.shape, 0) + step * batch
-            partner = lax.broadcasted_iota(jnp.int32, lagged.shape, 1)
+            partner = lax.broadcasted_iota(jnp.int32, lagged.shape, 1) + spans[0][1]
             lagged = jnp.where(channel == partner, 0.0, lagged)
         channels = slice(step * batch, (step + 1) * batch)
         done[channels] = lagged.astype(jnp.bfloat16)
@@ -288,26 +289,17 @@
         copy.wait()
 
 
-def correlate(mine, others, inverse, hop, spans, result):
-    own_pair = mine is None
+def correlate(own, others, inverse, hop, spans, result, own_pair=False):
     rows = sum(other.shape[0] for other in others)
     width = rows // NWIN
-    form = jax.ShapeDtypeStruct((3, rows, F), jnp.float32) if own_pair else mine
-    full = form.shape[1] // NWIN
+    full = own.shape[0] // NWIN
     group = 8
     batch = 256 // width
-    operands = [jnp.asarray(hop, jnp.int32).reshape(1), *others, *inverse]
-    if not own_pair:
-        operands.append(mine)
+    operands = [jnp.asarray(hop, jnp.int32).reshape(1), own, *others, *inverse]
     in_specs = [pl.BlockSpec(memory_space=pltpu.SMEM)]
     in_specs += [pl.BlockSpec(memory_space=pltpu.VMEM)] * (len(operands) - 1)
-    out_specs = [pl.BlockSpec(memory_space=pl.ANY)]
-    out_shape = [jax.ShapeDtypeStruct((full, HOPS + 1, full, NLAG), jnp.bfloat16)]
     aliases = {}
-    if own_pair:
-        out_specs.append(pl.BlockSpec(memory_space=pltpu.VMEM))
-        out_shape.append(form)
-    else:
+    if result is not None:
         in_specs.append(pl.BlockSpec(memory_space=pl.ANY))
         aliases = {len(operands): 0}
         operands.append(result)
@@ -315,9 +307,10 @@
     return pl.pallas_call(
         functools.partial(correlate_kernel, own_pair, spans, group, batch, len(others)),
         in_specs=in_specs,
-        out_specs=out_specs,
-        out_shape=out_shape,
+        out_specs=pl.BlockSpec(memory_space=pl.ANY),
+        out_shape=jax.ShapeDtypeStruct((full, HOPS + 1, full, NLAG), jnp.bfloat16),
         scratch_shapes=[
+            pltpu.VMEM((3, own.shape[0], F), jnp.float32),
             pltpu.VMEM((3, rows, F), jnp.float32),
             pltpu.VMEM((pairs, 2 * F), jnp.bfloat16),
             pltpu.VMEM((full, width, NLAG), jnp.bfloat16),
@@ -349,25 +342,26 @@
     near_hop, far_hop = 1 + 2 * odd, 3 - 2 * odd
     barrier = lax.optimization_barrier
     side = rec_count // NWIN // 2
+    whole, first, second = (None, 0, 0, 2 * side), (None, 0, 0, side), (None, side, 0, side)
+
+    def add(others, hop, *spans, own_pair=False):
+        return correlate(own, others, inverse, hop, spans, result, own_pair)
+
+    result = None
     low = moved(low, lambda i: i + 2)
     high = moved(high, lambda i: i + 1 if i % 2 else i + 3)
-    whole, first = (None, 0, 0, 2 * side), (None, 0, 0, side)
-    result, mine = correlate(None, [own], inverse, 0, (whole,), None)
-
-    def add(others, hop, *spans):
-        return correlate(mine, others, inverse, hop, spans, result)[0]
-
+    result = add([own], 0, whole, own_pair=True)
     low, result = barrier((low, result))
     far_low = moved(low, lambda i: i ^ 1)
     result = add([low], 2, first)
     again, high, result = barrier((own, high, result))
     near = moved(again, lambda i: i + 3 if i % 2 else i + 1)
     far_high = moved(high, lambda i: i ^ 1)
-    result = add([high], far_hop, (None, side, 0, side))
+    result = add([high], far_hop, second)
+    far_low, far_high, result = barrier((far_low, far_high, result))
+    result = add([far_low, far_high], far_hop, first, (2, side, side, side))
     near, result = barrier((near, result))
-    result = add([near], near_hop, whole)
-    far_low, far_high, result = barrier((far_low, far_high, result))
-    return add([far_low, far_high], far_hop, first, (2, side, side, side))
+    return add([near], near_hop, whole)
 
 
 def solution(mesh):

time: 84.1 us -> 79.8 us (0.949)
  the two profiles are of different devices: /device:TPU:0 before, /device:TPU:4 now
where the time goes in v7:
time: 79.8 us; the launch traced here: 79.6 us
  Pallas kernels  38.5 us (48%)
  waiting for transfers between devices  19 us (24%)
  starting transfers between devices  17.1 us (21%)
  other arithmetic  4.72 us (6%)
    pallas_call x5, Pallas kernels, correlate(): pl.pallas_call(functools.partial(correlate_kernel, own_pair, spans, group...  26.8 us
    all_to_all x1, waiting for transfers between devices, on_device(): lax.all_to_all(outgoing.reshape(peers, capacity // PACK, width), 'blk', s...  18.8 us
    pallas_call x1, Pallas kernels, spectra(): pl.pallas_call(functools.partial(spectrum_kernel, capacity), in_specs=[pl...  10.9 us
    ppermute x5, starting transfers between devices, moved(): lax.ppermute(block, 'blk', [(source_of(i) % count, i) for i in range(coun...  10.7 us
    all_to_all x1, starting transfers between devices, on_device(): lax.all_to_all(outgoing.reshape(peers, capacity // PACK, width), 'blk', s...  6.37 us
    convert_element_type x1, other arithmetic, inverse_table(): (-jnp.sin(angles)).astype(jnp.bfloat16)  4.72 us
  transfers between devices with their start and end apart: 6, of which 2 were waited for; matrix products, arithmetic and copies ran while one was open for 6% of the time, Pallas kernels for 25%

profile of v7, /device:TPU:4, one launch (start us, length us, event | category | flops | bytes accessed | tf_op | source)
XLA Modules:
  0.0 79.6 jit_solution(11806795649327635856)
XLA Ops:
  0.0 0.0 copy-start
  0.0 10.9 %spectra.1 = bf16[128,4224]{1,0:T(8,128)(2,1)} custom-call(s32[1,256]{1,0:T(1,128)} %bitcast.9, bf16[12000,256]{1,0:T(8,128)(2,1)} %bitcast.8, bf16[1024,3072]{1,0:T(8,128)(2,1)} %constant.46.clone.table_ref), custom_call_target="tpu_custom_call" | custom-call | flops 6291456000 | bytes 18432000 | tf_op jit(solution)/shard_map/spectra/pallas_call | solution.py:132
  10.9 6.4 %all-to-all-start = ((bf16[16,8,4224]{2,1,0:T(8,128)(2,1)}), bf16[16,8,4224]{2,1,0:T(8,128)(2,1)S(1)}, u32[]{:S(2)}, u32[]{:S(2)}) async-start(bf16[16,8,4224]{2,1,0:T(8,128)(2,1)} %bitcast.7), calls=%async_computation | async-start | bytes 2162688 | tf_op jit(solution)/shard_map/all_to_all | solution.py:335
  17.3 0.0 copy-done
  17.3 4.7 %negate_convert_fusion = (bf16[512,512]{1,0:T(8,128)(2,1)S(1)}, bf16[512,512]{1,0:T(8,128)(2,1)S(1)}) fusion(s32[512]{0:T(512)S(1)} %iota_add_fusion, s32[512]{0:T(512)S(1)} %copy-done), kind=kLoop, calls=%fused_computation.3 | loop fusion | flops 3145728 | bytes 1052672 | tf_op jit(solution)/shard_map/convert_element_type | solution.py:41
  22.0 18.8 %all-to-all-done = bf16[16,8,4224]{2,1,0:T(8,128)(2,1)S(1)} async-done(((bf16[16,8,4224]{2,1,0:T(8,128)(2,1)}), bf16[16,8,4224]{2,1,0:T(8,128)(2,1)S(1)}, u32[]{:S(2)}, u32[]{:S(2)}) %all-to-all-start) | async-done | bytes 1081376 | tf_op jit(solution)/shard_map/all_to_all | solution.py:335
  40.8 0.8 place.1
  41.6 0.1 collective-permute-start.1
  41.7 5.3 %collective-permute-start = (bf16[128,1024]{1,0:T(8,128)(2,1)S(1)}, bf16[128,1024]{1,0:T(8,128)(2,1)S(1)}, u32[]{:S(2)}, u32[]{:S(2)}) collective-permute-start(bf16[128,1024]{1,0:T(8,128)(2,1)S(1)} %get-tuple-element.23), channel_id=1, source_target_pairs={{3,0},{2,1},{5,2},{4,3},{7,4},{6,5},{9,6},{8,7},{11,8},{10,9},{13,... | collective-permute-start | bytes 786440 | tf_op jit(solution)/shard_map/ppermute | solution.py:33
  47.0 6.6 %correlate.5.refs_5_ = bf16[32,4,32,801]{3,2,1,0:T(8,128)(2,1)} custom-call(s32[1]{0:T(128)} %constant.44.clone.1.refs_0_, bf16[256,1024]{1,0:T(8,128)(2,1)S(1)} %get-tuple-element.29.refs_1_.refs_2_, bf16[256,1024]{1,0:T(8,128)(2,1)S(1)} %get-tuple-element.29.refs_1_.refs_2_, bf16[512,512]{1,0:T(8,128)(2,1)S(1)} %get-tuple-element.25.refs_3_.refs_4_, ...), custom_call_target="tpu_custom_call" | custom-call | flops 3359637504 | bytes 1640448 | tf_op jit(solution)/shard_map/correlate/pallas_call | solution.py:307
  53.6 0.0 collective-permute-done.1.refs_2_
  53.6 3.5 %correlate.6.refs_5_ = bf16[32,4,32,801]{3,2,1,0:T(8,128)(2,1)} custom-call(s32[1]{0:T(128)} %constant.43.clone.1.refs_0_, bf16[256,1024]{1,0:T(8,128)(2,1)S(1)} %get-tuple-element.29.refs_1_.refs_2_, bf16[128,1024]{1,0:T(8,128)(2,1)S(1)} %collective-permute-done.1.refs_2_, ...), custom_call_target="tpu_custom_call", output_to_operand_aliasing={{}: (5, {})} | custom-call | flops 1679818752 | bytes 820224 | tf_op jit(solution)/shard_map/correlate/pallas_call | solution.py:307
  57.2 0.2 collective-permute-done.refs_2_
  57.4 0.4 collective-permute-start.4
  57.7 0.1 collective-permute-start.3
  57.9 4.8 %collective-permute-start.2 = (bf16[256,1024]{1,0:T(8,128)(2,1)S(1)}, bf16[256,1024]{1,0:T(8,128)(2,1)S(1)}, u32[]{:S(2)}, u32[]{:S(2)}) collective-permute-start(bf16[256,1024]{1,0:T(8,128)(2,1)S(1)} %get-tuple-element.29.refs_1_.refs_2_), channel_id=1, source_target_pairs={{1,0},{4,1},{3,2},{6,3},{5,4},{8,5},{7,6},{10,7},{9,8},{12,9},{11,... | collective-permute-start | bytes 1572872 | tf_op jit(solution)/shard_map/ppermute | solution.py:33
  62.7 3.5 %correlate.7.refs_6_ = bf16[32,4,32,801]{3,2,1,0:T(8,128)(2,1)} custom-call(s32[1]{0:T(128)} %bitcast.5.refs_0_, bf16[256,1024]{1,0:T(8,128)(2,1)S(1)} %get-tuple-element.29.refs_1_.refs_2_, bf16[128,1024]{1,0:T(8,128)(2,1)S(1)} %collective-permute-done.refs_2_, ...), custom_call_target="tpu_custom_call", output_to_operand_aliasing={{}: (5, {})} | custom-call | flops 1679818752 | bytes 820224 | tf_op jit(solution)/shard_map/correlate/pallas_call | solution.py:307
  66.2 0.0 collective-permute-done.4.refs_3_
  66.2 0.0 collective-permute-done.3.refs_2_
  66.2 6.6 %correlate.8.refs_5_ = bf16[32,4,32,801]{3,2,1,0:T(8,128)(2,1)} custom-call(s32[1]{0:T(128)} %bitcast.5.refs_0_, bf16[256,1024]{1,0:T(8,128)(2,1)S(1)} %get-tuple-element.29.refs_1_.refs_2_, bf16[128,1024]{1,0:T(8,128)(2,1)S(1)} %collective-permute-done.3.refs_2_, ...), custom_call_target="tpu_custom_call", output_to_operand_aliasing={{}: (6, {})} | custom-call | flops 3359637504 | bytes 1640448 | tf_op jit(solution)/shard_map/correlate/pallas_call | solution.py:307
  72.8 0.0 collective-permute-done.2.refs_2_
  72.8 6.6 %correlate.9 = bf16[32,4,32,801]{3,2,1,0:T(8,128)(2,1)} custom-call(s32[1]{0:T(128)} %bitcast.refs_0_, bf16[256,1024]{1,0:T(8,128)(2,1)S(1)} %get-tuple-element.29.refs_1_.refs_2_, bf16[256,1024]{1,0:T(8,128)(2,1)S(1)} %collective-permute-done.2.refs_2_, bf16[512,512]{1,0:T(8,128)(2,1)S(1)} %get-tuple-element.25.refs_3_.refs_4_, ...), custom_call_target="tpu_custom_call", output_to_operand_aliasing={{}: (5, {})} | custom-call | flops 3359637504 | bytes 1640448 | tf_op jit(solution)/shard_map/correlate/pallas_call | solution.py:307
  (1 shorter events, 0.0 us)
Async XLA Ops:
  0.0 17.3 %copy-start = (s32[512]{0:T(512)S(1)}, s32[512]{0:T(512)}, u32[]{:S(2)}) copy-start(s32[512]{0:T(512)} %constant.47.clone) | copy-start | bytes 6148
  10.9 29.9 %all-to-all-start = ((bf16[16,8,4224]{2,1,0:T(8,128)(2,1)}), bf16[16,8,4224]{2,1,0:T(8,128)(2,1)S(1)}, u32[]{:S(2)}, u32[]{:S(2)}) async-start(bf16[16,8,4224]{2,1,0:T(8,128)(2,1)} %bitcast.7), calls=%async_computation | async-start | bytes 2162688 | tf_op jit(solution)/shard_map/all_to_all | solution.py:335
  41.6 12.0 %collective-permute-start.1 = (bf16[128,1024]{1,0:T(8,128)(2,1)S(1)}, bf16[128,1024]{1,0:T(8,128)(2,1)S(1)}, u32[]{:S(2)}, u32[]{:S(2)}) collective-permute-start(bf16[128,1024]{1,0:T(8,128)(2,1)S(1)} %get-tuple-element.24), channel_id=1, source_target_pairs={{2,0},{3,1},{4,2},{5,3},{6,4},{7,5},{8,6},{9,7},{10,8},{11,9},{12,... | collective-permute-start | bytes 786440 | tf_op jit(solution)/shard_map/ppermute | solution.py:33
  41.7 15.6 %collective-permute-start = (bf16[128,1024]{1,0:T(8,128)(2,1)S(1)}, bf16[128,1024]{1,0:T(8,128)(2,1)S(1)}, u32[]{:S(2)}, u32[]{:S(2)}) collective-permute-start(bf16[128,1024]{1,0:T(8,128)(2,1)S(1)} %get-tuple-element.23), channel_id=1, source_target_pairs={{3,0},{2,1},{5,2},{4,3},{7,4},{6,5},{9,6},{8,7},{11,8},{10,9},{13,... | collective-permute-start | bytes 786440 | tf_op jit(solution)/shard_map/ppermute | solution.py:33
  57.4 8.8 %collective-permute-start.4 = (bf16[128,1024]{1,0:T(8,128)(2,1)S(1)}, bf16[128,1024]{1,0:T(8,128)(2,1)S(1)}, u32[]{:S(2)}, u32[]{:S(2)}) collective-permute-start(bf16[128,1024]{1,0:T(8,128)(2,1)S(1)} %collective-permute-done.refs_2_), channel_id=1, source_target_pairs={{1,0},{0,1},{3,2},{2,3},{5,4},{4,5},{7,6},{6,7},{9,8},{8,9},{11,10... | collective-permute-start | bytes 786440 | tf_op jit(solution)/shard_map/ppermute | solution.py:33
  57.7 8.5 %collective-permute-start.3 = (bf16[128,1024]{1,0:T(8,128)(2,1)S(1)}, bf16[128,1024]{1,0:T(8,128)(2,1)S(1)}, u32[]{:S(2)}, u32[]{:S(2)}) collective-permute-start(bf16[128,1024]{1,0:T(8,128)(2,1)S(1)} %collective-permute-done.1.refs_2_), channel_id=1, source_target_pairs={{1,0},{0,1},{3,2},{2,3},{5,4},{4,5},{7,6},{6,7},{9,8},{8,9},{11,10... | collective-permute-start | bytes 786440 | tf_op jit(solution)/shard_map/ppermute | solution.py:33
  57.9 15.0 %collective-permute-start.2 = (bf16[256,1024]{1,0:T(8,128)(2,1)S(1)}, bf16[256,1024]{1,0:T(8,128)(2,1)S(1)}, u32[]{:S(2)}, u32[]{:S(2)}) collective-permute-start(bf16[256,1024]{1,0:T(8,128)(2,1)S(1)} %get-tuple-element.29.refs_1_.refs_2_), channel_id=1, source_target_pairs={{1,0},{4,1},{3,2},{6,3},{5,4},{8,5},{7,6},{10,7},{9,8},{12,9},{11,... | collective-permute-start | bytes 1572872 | tf_op jit(solution)/shard_map/ppermute | solution.py:33

commit v8 on v7

--- a/solution.py
+++ b/solution.py
@@ -220,7 +220,7 @@
             theirs[1, rows, :] = real + imag
             theirs[2, rows, :] = real - imag
 
-    shared = 64 // width
+    shared = 4
 
     def channels_from(step, carry):
         blocks = [
@@ -294,7 +294,7 @@
     width = rows // NWIN
     full = own.shape[0] // NWIN
     group = 8
-    batch = 256 // width
+    batch = 128 // width
     operands = [jnp.asarray(hop, jnp.int32).reshape(1), own, *others, *inverse]
     in_specs = [pl.BlockSpec(memory_space=pltpu.SMEM)]
     in_specs += [pl.BlockSpec(memory_space=pltpu.VMEM)] * (len(operands) - 1)

time: 79.8 us -> 78.4 us (0.982)
  Pallas kernels: 38.5 us -> 36.4 us
  waiting for transfers between devices: 19 us -> 19.8 us
    pallas_call x5, Pallas kernels: 26.8 us -> 24.7 us  [correlate(): pl.pallas_call(functools.partial(correlate_kernel, own_pair, spans, group...]
  transfers between devices with their start and end apart: 6 -> 6, of which waited for: 2 -> 2; matrix products, arithmetic and copies ran while one was open for 6% -> 6% of each run, Pallas kernels for 25% -> 24%
where the time goes in v8:
time: 78.4 us; the launch traced here: 78.2 us
  Pallas kernels  36.4 us (46%)
  waiting for transfers between devices  19.8 us (25%)
  starting transfers between devices  17.1 us (22%)
  other arithmetic  4.72 us (6%)
    pallas_call x5, Pallas kernels, correlate(): pl.pallas_call(functools.partial(correlate_kernel, own_pair, spans, group...  24.7 us
    all_to_all x1, waiting for transfers between devices, on_device(): lax.all_to_all(outgoing.reshape(peers, capacity // PACK, width), 'blk', s...  18.8 us
    pallas_call x1, Pallas kernels, spectra(): pl.pallas_call(functools.partial(spectrum_kernel, capacity), in_specs=[pl...  10.9 us
    ppermute x5, starting transfers between devices, moved(): lax.ppermute(block, 'blk', [(source_of(i) % count, i) for i in range(coun...  10.7 us
    all_to_all x1, starting transfers between devices, on_device(): lax.all_to_all(outgoing.reshape(peers, capacity // PACK, width), 'blk', s...  6.37 us
    convert_element_type x1, other arithmetic, inverse_table(): (-jnp.sin(angles)).astype(jnp.bfloat16)  4.72 us
  transfers between devices with their start and end apart: 6, of which 2 were waited for; matrix products, arithmetic and copies ran while one was open for 6% of the time, Pallas kernels for 24%

profile of v8, /device:TPU:4, one launch (start us, length us, event | category | flops | bytes accessed | tf_op | source)
XLA Modules:
  0.0 78.2 jit_solution(4242617454904175304)
XLA Ops:
  0.0 0.0 copy-start
  0.0 10.9 %spectra.1 = bf16[128,4224]{1,0:T(8,128)(2,1)} custom-call(s32[1,256]{1,0:T(1,128)} %bitcast.9, bf16[12000,256]{1,0:T(8,128)(2,1)} %bitcast.8, bf16[1024,3072]{1,0:T(8,128)(2,1)} %constant.46.clone.table_ref), custom_call_target="tpu_custom_call" | custom-call | flops 6291456000 | bytes 18432000 | tf_op jit(solution)/shard_map/spectra/pallas_call | solution.py:132
  10.9 6.4 %all-to-all-start = ((bf16[16,8,4224]{2,1,0:T(8,128)(2,1)}), bf16[16,8,4224]{2,1,0:T(8,128)(2,1)S(1)}, u32[]{:S(2)}, u32[]{:S(2)}) async-start(bf16[16,8,4224]{2,1,0:T(8,128)(2,1)} %bitcast.7), calls=%async_computation | async-start | bytes 2162688 | tf_op jit(solution)/shard_map/all_to_all | solution.py:335
  17.3 0.0 copy-done
  17.3 4.7 %negate_convert_fusion = (bf16[512,512]{1,0:T(8,128)(2,1)S(1)}, bf16[512,512]{1,0:T(8,128)(2,1)S(1)}) fusion(s32[512]{0:T(512)S(1)} %iota_add_fusion, s32[512]{0:T(512)S(1)} %copy-done), kind=kLoop, calls=%fused_computation.3 | loop fusion | flops 3145728 | bytes 1052672 | tf_op jit(solution)/shard_map/convert_element_type | solution.py:41
  22.0 18.8 %all-to-all-done = bf16[16,8,4224]{2,1,0:T(8,128)(2,1)S(1)} async-done(((bf16[16,8,4224]{2,1,0:T(8,128)(2,1)}), bf16[16,8,4224]{2,1,0:T(8,128)(2,1)S(1)}, u32[]{:S(2)}, u32[]{:S(2)}) %all-to-all-start) | async-done | bytes 1081376 | tf_op jit(solution)/shard_map/all_to_all | solution.py:335
  40.8 0.8 %place.1 = (bf16[256,1024]{1,0:T(8,128)(2,1)S(1)}, bf16[128,1024]{1,0:T(8,128)(2,1)S(1)}, bf16[128,1024]{1,0:T(8,128)(2,1)S(1)}) custom-call(bf16[128,4224]{1,0:T(8,128)(2,1)S(1)} %bitcast.6), custom_call_target="tpu_custom_call" | custom-call | tf_op jit(solution)/shard_map/place/pallas_call | solution.py:181
  41.6 0.1 collective-permute-start.1
  41.7 5.3 %collective-permute-start = (bf16[128,1024]{1,0:T(8,128)(2,1)S(1)}, bf16[128,1024]{1,0:T(8,128)(2,1)S(1)}, u32[]{:S(2)}, u32[]{:S(2)}) collective-permute-start(bf16[128,1024]{1,0:T(8,128)(2,1)S(1)} %get-tuple-element.23), channel_id=1, source_target_pairs={{3,0},{2,1},{5,2},{4,3},{7,4},{6,5},{9,6},{8,7},{11,8},{10,9},{13,... | collective-permute-start | bytes 786440 | tf_op jit(solution)/shard_map/ppermute | solution.py:33
  47.0 5.9 %correlate.5.refs_5_ = bf16[32,4,32,801]{3,2,1,0:T(8,128)(2,1)} custom-call(s32[1]{0:T(128)} %constant.44.clone.1.refs_0_, bf16[256,1024]{1,0:T(8,128)(2,1)S(1)} %get-tuple-element.29.refs_1_.refs_2_, bf16[256,1024]{1,0:T(8,128)(2,1)S(1)} %get-tuple-element.29.refs_1_.refs_2_, bf16[512,512]{1,0:T(8,128)(2,1)S(1)} %get-tuple-element.25.refs_3_.refs_4_, ...), custom_call_target="tpu_custom_call" | custom-call | flops 3359637504 | bytes 1640448 | tf_op jit(solution)/shard_map/correlate/pallas_call | solution.py:307
  52.9 0.0 collective-permute-done.1.refs_2_
  53.0 3.4 %correlate.6.refs_5_ = bf16[32,4,32,801]{3,2,1,0:T(8,128)(2,1)} custom-call(s32[1]{0:T(128)} %constant.43.clone.1.refs_0_, bf16[256,1024]{1,0:T(8,128)(2,1)S(1)} %get-tuple-element.29.refs_1_.refs_2_, bf16[128,1024]{1,0:T(8,128)(2,1)S(1)} %collective-permute-done.1.refs_2_, ...), custom_call_target="tpu_custom_call", output_to_operand_aliasing={{}: (5, {})} | custom-call | flops 1679818752 | bytes 820224 | tf_op jit(solution)/shard_map/correlate/pallas_call | solution.py:307
  56.4 1.0 %collective-permute-done.refs_2_ = bf16[128,1024]{1,0:T(8,128)(2,1)S(1)} collective-permute-done((bf16[128,1024]{1,0:T(8,128)(2,1)S(1)}, bf16[128,1024]{1,0:T(8,128)(2,1)S(1)}, u32[]{:S(2)}, u32[]{:S(2)}) %collective-permute-start) | collective-permute-done | bytes 262176 | tf_op jit(solution)/shard_map/ppermute | solution.py:33
  57.4 0.0 collective-permute-start.4
  57.4 0.5 collective-permute-start.3
  57.9 4.8 %collective-permute-start.2 = (bf16[256,1024]{1,0:T(8,128)(2,1)S(1)}, bf16[256,1024]{1,0:T(8,128)(2,1)S(1)}, u32[]{:S(2)}, u32[]{:S(2)}) collective-permute-start(bf16[256,1024]{1,0:T(8,128)(2,1)S(1)} %get-tuple-element.29.refs_1_.refs_2_), channel_id=1, source_target_pairs={{1,0},{4,1},{3,2},{6,3},{5,4},{8,5},{7,6},{10,7},{9,8},{12,9},{11,... | collective-permute-start | bytes 1572872 | tf_op jit(solution)/shard_map/ppermute | solution.py:33
  62.7 3.4 %correlate.7.refs_6_ = bf16[32,4,32,801]{3,2,1,0:T(8,128)(2,1)} custom-call(s32[1]{0:T(128)} %bitcast.5.refs_0_, bf16[256,1024]{1,0:T(8,128)(2,1)S(1)} %get-tuple-element.29.refs_1_.refs_2_, bf16[128,1024]{1,0:T(8,128)(2,1)S(1)} %collective-permute-done.refs_2_, ...), custom_call_target="tpu_custom_call", output_to_operand_aliasing={{}: (5, {})} | custom-call | flops 1679818752 | bytes 820224 | tf_op jit(solution)/shard_map/correlate/pallas_call | solution.py:307
  66.1 0.0 collective-permute-done.4.refs_3_
  66.1 0.0 collective-permute-done.3.refs_2_
  66.1 6.0 %correlate.8.refs_5_ = bf16[32,4,32,801]{3,2,1,0:T(8,128)(2,1)} custom-call(s32[1]{0:T(128)} %bitcast.5.refs_0_, bf16[256,1024]{1,0:T(8,128)(2,1)S(1)} %get-tuple-element.29.refs_1_.refs_2_, bf16[128,1024]{1,0:T(8,128)(2,1)S(1)} %collective-permute-done.3.refs_2_, ...), custom_call_target="tpu_custom_call", output_to_operand_aliasing={{}: (6, {})} | custom-call | flops 3359637504 | bytes 1640448 | tf_op jit(solution)/shard_map/correlate/pallas_call | solution.py:307
  72.1 0.0 collective-permute-done.2.refs_2_
  72.1 5.9 %correlate.9 = bf16[32,4,32,801]{3,2,1,0:T(8,128)(2,1)} custom-call(s32[1]{0:T(128)} %bitcast.refs_0_, bf16[256,1024]{1,0:T(8,128)(2,1)S(1)} %get-tuple-element.29.refs_1_.refs_2_, bf16[256,1024]{1,0:T(8,128)(2,1)S(1)} %collective-permute-done.2.refs_2_, bf16[512,512]{1,0:T(8,128)(2,1)S(1)} %get-tuple-element.25.refs_3_.refs_4_, ...), custom_call_target="tpu_custom_call", output_to_operand_aliasing={{}: (5, {})} | custom-call | flops 3359637504 | bytes 1640448 | tf_op jit(solution)/shard_map/correlate/pallas_call | solution.py:307
  (1 shorter events, 0.0 us)
Async XLA Ops:
  0.0 17.3 %copy-start = (s32[512]{0:T(512)S(1)}, s32[512]{0:T(512)}, u32[]{:S(2)}) copy-start(s32[512]{0:T(512)} %constant.47.clone) | copy-start | bytes 6148
  10.9 29.9 %all-to-all-start = ((bf16[16,8,4224]{2,1,0:T(8,128)(2,1)}), bf16[16,8,4224]{2,1,0:T(8,128)(2,1)S(1)}, u32[]{:S(2)}, u32[]{:S(2)}) async-start(bf16[16,8,4224]{2,1,0:T(8,128)(2,1)} %bitcast.7), calls=%async_computation | async-start | bytes 2162688 | tf_op jit(solution)/shard_map/all_to_all | solution.py:335
  41.6 11.3 %collective-permute-start.1 = (bf16[128,1024]{1,0:T(8,128)(2,1)S(1)}, bf16[128,1024]{1,0:T(8,128)(2,1)S(1)}, u32[]{:S(2)}, u32[]{:S(2)}) collective-permute-start(bf16[128,1024]{1,0:T(8,128)(2,1)S(1)} %get-tuple-element.24), channel_id=1, source_target_pairs={{2,0},{3,1},{4,2},{5,3},{6,4},{7,5},{8,6},{9,7},{10,8},{11,9},{12,... | collective-permute-start | bytes 786440 | tf_op jit(solution)/shard_map/ppermute | solution.py:33
  41.7 15.6 %collective-permute-start = (bf16[128,1024]{1,0:T(8,128)(2,1)S(1)}, bf16[128,1024]{1,0:T(8,128)(2,1)S(1)}, u32[]{:S(2)}, u32[]{:S(2)}) collective-permute-start(bf16[128,1024]{1,0:T(8,128)(2,1)S(1)} %get-tuple-element.23), channel_id=1, source_target_pairs={{3,0},{2,1},{5,2},{4,3},{7,4},{6,5},{9,6},{8,7},{11,8},{10,9},{13,... | collective-permute-start | bytes 786440 | tf_op jit(solution)/shard_map/ppermute | solution.py:33
  57.4 8.7 %collective-permute-start.4 = (bf16[128,1024]{1,0:T(8,128)(2,1)S(1)}, bf16[128,1024]{1,0:T(8,128)(2,1)S(1)}, u32[]{:S(2)}, u32[]{:S(2)}) collective-permute-start(bf16[128,1024]{1,0:T(8,128)(2,1)S(1)} %collective-permute-done.refs_2_), channel_id=1, source_target_pairs={{1,0},{0,1},{3,2},{2,3},{5,4},{4,5},{7,6},{6,7},{9,8},{8,9},{11,10... | collective-permute-start | bytes 786440 | tf_op jit(solution)/shard_map/ppermute | solution.py:33
  57.4 8.7 %collective-permute-start.3 = (bf16[128,1024]{1,0:T(8,128)(2,1)S(1)}, bf16[128,1024]{1,0:T(8,128)(2,1)S(1)}, u32[]{:S(2)}, u32[]{:S(2)}) collective-permute-start(bf16[128,1024]{1,0:T(8,128)(2,1)S(1)} %collective-permute-done.1.refs_2_), channel_id=1, source_target_pairs={{1,0},{0,1},{3,2},{2,3},{5,4},{4,5},{7,6},{6,7},{9,8},{8,9},{11,10... | collective-permute-start | bytes 786440 | tf_op jit(solution)/shard_map/ppermute | solution.py:33
  57.9 14.3 %collective-permute-start.2 = (bf16[256,1024]{1,0:T(8,128)(2,1)S(1)}, bf16[256,1024]{1,0:T(8,128)(2,1)S(1)}, u32[]{:S(2)}, u32[]{:S(2)}) collective-permute-start(bf16[256,1024]{1,0:T(8,128)(2,1)S(1)} %get-tuple-element.29.refs_1_.refs_2_), channel_id=1, source_target_pairs={{1,0},{4,1},{3,2},{6,3},{5,4},{8,5},{7,6},{10,7},{9,8},{12,9},{11,... | collective-permute-start | bytes 1572872 | tf_op jit(solution)/shard_map/ppermute | solution.py:33

commit v9 on v8

--- a/solution.py
+++ b/solution.py
@@ -182,7 +182,7 @@
         place_kernel,
         out_shape=[
             jax.ShapeDtypeStruct((rows, 2 * F), jnp.bfloat16)
-            for rows in (rec_count, rec_count // 2, rec_count // 2)
+            for rows in (rec_count,)
         ],
         compiler_params=pltpu.CompilerParams(vmem_limit_bytes=8 * MIB),
         name="place",
@@ -336,7 +336,7 @@
         outgoing.reshape(peers, capacity // PACK, width), "blk", split_axis=0, concat_axis=0, tiled=True
     )
     arrived, inverse = lax.optimization_barrier((arrived, inverse_table()))
-    own, low, high = place(arrived.reshape(slots // PACK, width), rec_count)
+    (own,) = place(arrived.reshape(slots // PACK, width), rec_count)
 
     odd = lax.axis_index("blk") % 2
     near_hop, far_hop = 1 + 2 * odd, 3 - 2 * odd
@@ -348,20 +348,22 @@
         return correlate(own, others, inverse, hop, spans, result, own_pair)
 
     result = None
-    low = moved(low, lambda i: i + 2)
-    high = moved(high, lambda i: i + 1 if i % 2 else i + 3)
-    result = add([own], 0, whole, own_pair=True)
-    low, result = barrier((low, result))
-    far_low = moved(low, lambda i: i ^ 1)
-    result = add([low], 2, first)
-    again, high, result = barrier((own, high, result))
+    whole = (None, 0, 0, 2 * side)
+
+    def add(others, hop, own_pair=False):
+        return correlate(own, others, inverse, hop, (whole,), result, own_pair)
+
+    result = None
+    ahead = moved(own, lambda i: i + 2)
+    result = add([own], 0, own_pair=True)
+    again, ahead, result = barrier((own, ahead, result))
+    far = moved(ahead, lambda i: i ^ 1)
     near = moved(again, lambda i: i + 3 if i % 2 else i + 1)
-    far_high = moved(high, lambda i: i ^ 1)
-    result = add([high], far_hop, second)
-    far_low, far_high, result = barrier((far_low, far_high, result))
-    result = add([far_low, far_high], far_hop, first, (2, side, side, side))
+    result = add([ahead], 2)
+    far, result = barrier((far, result))
+    result = add([far], far_hop)
     near, result = barrier((near, result))
-    return add([near], near_hop, whole)
+    return add([near], near_hop)
 
 
 def solution(mesh):

time: 78.4 us -> 81.1 us (1.034)
  waiting for transfers between devices: 19.8 us -> 28.4 us
  starting transfers between devices: 17.1 us -> 12.1 us
  Pallas kernels: 36.4 us -> 35.4 us
    ppermute x5 -> x3, waiting for transfers between devices: 0.99 us -> 9.6 us  [moved(): lax.ppermute(block, 'blk', [(source_of(i) % count, i) for i in range(coun...]
    ppermute x5 -> x3, starting transfers between devices: 10.7 us -> 5.72 us  [moved(): lax.ppermute(block, 'blk', [(source_of(i) % count, i) for i in range(coun...]
    pallas_call x5 -> x4, Pallas kernels: 24.7 us -> 23.7 us  [correlate(): pl.pallas_call(functools.partial(correlate_kernel, own_pair, spans, group...]
  transfers between devices with their start and end apart: 6 -> 4, of which waited for: 2 -> 2; matrix products, arithmetic and copies ran while one was open for 6% -> 6% of each run, Pallas kernels for 24% -> 22%
where the time goes in v9:
time: 81.1 us; the launch traced here: 80.9 us
  Pallas kernels  35.4 us (44%)
  waiting for transfers between devices  28.4 us (35%)
  starting transfers between devices  12.1 us (15%)
  other arithmetic  4.72 us (6%)
    pallas_call x4, Pallas kernels, correlate(): pl.pallas_call(functools.partial(correlate_kernel, own_pair, spans, group...  23.7 us
    all_to_all x1, waiting for transfers between devices, on_device(): lax.all_to_all(outgoing.reshape(peers, capacity // PACK, width), 'blk', s...  18.8 us
    pallas_call x1, Pallas kernels, spectra(): pl.pallas_call(functools.partial(spectrum_kernel, capacity), in_specs=[pl...  10.9 us
    ppermute x3, waiting for transfers between devices, moved(): lax.ppermute(block, 'blk', [(source_of(i) % count, i) for i in range(coun...  9.6 us
    all_to_all x1, starting transfers between devices, on_device(): lax.all_to_all(outgoing.reshape(peers, capacity // PACK, width), 'blk', s...  6.37 us
    ppermute x3, starting transfers between devices, moved(): lax.ppermute(block, 'blk', [(source_of(i) % count, i) for i in range(coun...  5.72 us
    convert_element_type x1, other arithmetic, inverse_table(): (-jnp.sin(angles)).astype(jnp.bfloat16)  4.72 us
  transfers between devices with their start and end apart: 4, of which 2 were waited for; matrix products, arithmetic and copies ran while one was open for 6% of the time, Pallas kernels for 22%

profile of v9, /device:TPU:4, one launch (start us, length us, event | category | flops | bytes accessed | tf_op | source)
XLA Modules:
  0.0 80.9 jit_solution(18104848494657786757)
XLA Ops:
  0.0 0.0 copy-start
  0.0 10.9 %spectra.1 = bf16[128,4224]{1,0:T(8,128)(2,1)} custom-call(s32[1,256]{1,0:T(1,128)} %bitcast.9, bf16[12000,256]{1,0:T(8,128)(2,1)} %bitcast.8, bf16[1024,3072]{1,0:T(8,128)(2,1)} %constant.46.clone.table_ref), custom_call_target="tpu_custom_call" | custom-call | flops 6291456000 | bytes 18432000 | tf_op jit(solution)/shard_map/spectra/pallas_call | solution.py:132
  10.9 6.4 %all-to-all-start = ((bf16[16,8,4224]{2,1,0:T(8,128)(2,1)}), bf16[16,8,4224]{2,1,0:T(8,128)(2,1)S(1)}, u32[]{:S(2)}, u32[]{:S(2)}) async-start(bf16[16,8,4224]{2,1,0:T(8,128)(2,1)} %bitcast.7), calls=%async_computation | async-start | bytes 2162688 | tf_op jit(solution)/shard_map/all_to_all | solution.py:335
  17.3 0.0 copy-done
  17.3 4.7 %negate_convert_fusion = (bf16[512,512]{1,0:T(8,128)(2,1)S(1)}, bf16[512,512]{1,0:T(8,128)(2,1)S(1)}) fusion(s32[512]{0:T(512)S(1)} %iota_add_fusion, s32[512]{0:T(512)S(1)} %copy-done), kind=kLoop, calls=%fused_computation.3 | loop fusion | flops 3145728 | bytes 1052672 | tf_op jit(solution)/shard_map/convert_element_type | solution.py:41
  22.0 18.8 %all-to-all-done = bf16[16,8,4224]{2,1,0:T(8,128)(2,1)S(1)} async-done(((bf16[16,8,4224]{2,1,0:T(8,128)(2,1)}), bf16[16,8,4224]{2,1,0:T(8,128)(2,1)S(1)}, u32[]{:S(2)}, u32[]{:S(2)}) %all-to-all-start) | async-done | bytes 1081376 | tf_op jit(solution)/shard_map/all_to_all | solution.py:335
  40.8 0.8 place.1.refs_1_.refs_2_
  41.6 0.1 collective-permute-start
  41.7 5.9 %correlate.4.refs_5_ = bf16[32,4,32,801]{3,2,1,0:T(8,128)(2,1)} custom-call(s32[1]{0:T(128)} %constant.43.clone.1.refs_0_, bf16[256,1024]{1,0:T(8,128)(2,1)S(1)} %place.1.refs_1_.refs_2_, bf16[256,1024]{1,0:T(8,128)(2,1)S(1)} %place.1.refs_1_.refs_2_, bf16[512,512]{1,0:T(8,128)(2,1)S(1)} %get-tuple-element.16.refs_3_, ...), custom_call_target="tpu_custom_call" | custom-call | flops 3359637504 | bytes 1640448 | tf_op jit(solution)/shard_map/correlate/pallas_call | solution.py:307
  47.7 9.6 %collective-permute-done.refs_2_ = bf16[256,1024]{1,0:T(8,128)(2,1)S(1)} collective-permute-done((bf16[256,1024]{1,0:T(8,128)(2,1)S(1)}, bf16[256,1024]{1,0:T(8,128)(2,1)S(1)}, u32[]{:S(2)}, u32[]{:S(2)}) %collective-permute-start) | collective-permute-done | bytes 524320 | tf_op jit(solution)/shard_map/ppermute | solution.py:33
  57.3 0.1 collective-permute-start.2
  57.4 5.5 %collective-permute-start.1 = (bf16[256,1024]{1,0:T(8,128)(2,1)S(1)}, bf16[256,1024]{1,0:T(8,128)(2,1)S(1)}, u32[]{:S(2)}, u32[]{:S(2)}) collective-permute-start(bf16[256,1024]{1,0:T(8,128)(2,1)S(1)} %place.1.refs_1_.refs_2_), channel_id=1, source_target_pairs={{1,0},{4,1},{3,2},{6,3},{5,4},{8,5},{7,6},{10,7},{9,8},{12,9},{11,... | collective-permute-start | bytes 1572872 | tf_op jit(solution)/shard_map/ppermute | solution.py:33
  62.9 5.9 %correlate.5.refs_5_ = bf16[32,4,32,801]{3,2,1,0:T(8,128)(2,1)} custom-call(s32[1]{0:T(128)} %constant.45.clone.1.refs_0_, bf16[256,1024]{1,0:T(8,128)(2,1)S(1)} %place.1.refs_1_.refs_2_, bf16[256,1024]{1,0:T(8,128)(2,1)S(1)} %collective-permute-done.refs_2_, bf16[512,512]{1,0:T(8,128)(2,1)S(1)} %get-tuple-element.16.refs_3_, ...), custom_call_target="tpu_custom_call", output_to_operand_aliasing={{}: (5, {})} | custom-call | flops 3359637504 | bytes 1640448 | tf_op jit(solution)/shard_map/correlate/pallas_call | solution.py:307
  68.8 0.0 collective-permute-done.2.refs_2_
  68.8 5.9 %correlate.6.refs_5_ = bf16[32,4,32,801]{3,2,1,0:T(8,128)(2,1)} custom-call(s32[1]{0:T(128)} %bitcast.5.refs_0_, bf16[256,1024]{1,0:T(8,128)(2,1)S(1)} %place.1.refs_1_.refs_2_, bf16[256,1024]{1,0:T(8,128)(2,1)S(1)} %collective-permute-done.2.refs_2_, bf16[512,512]{1,0:T(8,128)(2,1)S(1)} %get-tuple-element.16.refs_3_, ...), custom_call_target="tpu_custom_call", output_to_operand_aliasing={{}: (5, {})} | custom-call | flops 3359637504 | bytes 1640448 | tf_op jit(solution)/shard_map/correlate/pallas_call | solution.py:307
  74.7 0.0 collective-permute-done.1.refs_2_
  74.8 5.9 %correlate.7 = bf16[32,4,32,801]{3,2,1,0:T(8,128)(2,1)} custom-call(s32[1]{0:T(128)} %bitcast.refs_0_, bf16[256,1024]{1,0:T(8,128)(2,1)S(1)} %place.1.refs_1_.refs_2_, bf16[256,1024]{1,0:T(8,128)(2,1)S(1)} %collective-permute-done.1.refs_2_, bf16[512,512]{1,0:T(8,128)(2,1)S(1)} %get-tuple-element.16.refs_3_, ...), custom_call_target="tpu_custom_call", output_to_operand_aliasing={{}: (5, {})} | custom-call | flops 3359637504 | bytes 1640448 | tf_op jit(solution)/shard_map/correlate/pallas_call | solution.py:307
  (1 shorter events, 0.0 us)
Async XLA Ops:
  0.0 17.3 %copy-start = (s32[512]{0:T(512)S(1)}, s32[512]{0:T(512)}, u32[]{:S(2)}) copy-start(s32[512]{0:T(512)} %constant.47.clone) | copy-start | bytes 6148
  10.9 29.9 %all-to-all-start = ((bf16[16,8,4224]{2,1,0:T(8,128)(2,1)}), bf16[16,8,4224]{2,1,0:T(8,128)(2,1)S(1)}, u32[]{:S(2)}, u32[]{:S(2)}) async-start(bf16[16,8,4224]{2,1,0:T(8,128)(2,1)} %bitcast.7), calls=%async_computation | async-start | bytes 2162688 | tf_op jit(solution)/shard_map/all_to_all | solution.py:335
  41.6 15.7 %collective-permute-start = (bf16[256,1024]{1,0:T(8,128)(2,1)S(1)}, bf16[256,1024]{1,0:T(8,128)(2,1)S(1)}, u32[]{:S(2)}, u32[]{:S(2)}) collective-permute-start(bf16[256,1024]{1,0:T(8,128)(2,1)S(1)} %place.1.refs_1_.refs_2_), channel_id=1, source_target_pairs={{2,0},{3,1},{4,2},{5,3},{6,4},{7,5},{8,6},{9,7},{10,8},{11,9},{12,... | collective-permute-start | bytes 1572872 | tf_op jit(solution)/shard_map/ppermute | solution.py:33
  57.3 11.5 %collective-permute-start.2 = (bf16[256,1024]{1,0:T(8,128)(2,1)S(1)}, bf16[256,1024]{1,0:T(8,128)(2,1)S(1)}, u32[]{:S(2)}, u32[]{:S(2)}) collective-permute-start(bf16[256,1024]{1,0:T(8,128)(2,1)S(1)} %collective-permute-done.refs_2_), channel_id=1, source_target_pairs={{1,0},{0,1},{3,2},{2,3},{5,4},{4,5},{7,6},{6,7},{9,8},{8,9},{11,10... | collective-permute-start | bytes 1572872 | tf_op jit(solution)/shard_map/ppermute | solution.py:33
  57.4 17.4 %collective-permute-start.1 = (bf16[256,1024]{1,0:T(8,128)(2,1)S(1)}, bf16[256,1024]{1,0:T(8,128)(2,1)S(1)}, u32[]{:S(2)}, u32[]{:S(2)}) collective-permute-start(bf16[256,1024]{1,0:T(8,128)(2,1)S(1)} %place.1.refs_1_.refs_2_), channel_id=1, source_target_pairs={{1,0},{4,1},{3,2},{6,3},{5,4},{8,5},{7,6},{10,7},{9,8},{12,9},{11,... | collective-permute-start | bytes 1572872 | tf_op jit(solution)/shard_map/ppermute | solution.py:33
